TPU v7x, 256 devices: a whole 4x4x8 slice. The times are simulated.
256 devices in a mesh: dp: 4 (over z_hi), expert: 64 (over x, y, z_lo, core).
Axes of the slice: x: 4, y: 4, z: 8 (z_hi: 4, z_lo: 2; z = z_hi * 2 + z_lo), core: 2. Of those that a mesh axis runs over, the one named last changes fastest.
Arguments:
- tokens: bfloat16 [32768, 1536], P(('dp', 'expert')), may hold values from -6 to 6
- routes: int32 [32768, 2], P(('dp', 'expert')), may hold values from 0 to 63, all different within a row; in each aligned block of 128 rows (0 to 127, 128 to 255, ...) at most 5 rows name the same one
- combine: float32 [32768, 2], P(('dp', 'expert')), may hold values from 0.1 to 1
- w_gate: bfloat16 [64, 1536, 1536], P('expert', None, 'dp'), may hold values from -0.15625 to 0.15625
- w_up: bfloat16 [64, 1536, 1536], P('expert', None, 'dp'), may hold values from -0.15625 to 0.15625
- w_down: bfloat16 [64, 1536, 1536], P('expert', 'dp'), may hold values from -0.15625 to 0.15625
- cotangent: bfloat16 [32768, 1536], P(('dp', 'expert')), may hold values from -2 to 2
Outputs:
- out: bfloat16 [32768, 1536], P(('dp', 'expert'))
- d_tokens: bfloat16 [32768, 1536], P(('dp', 'expert'))
- d_combine: float32 [32768, 2], P(('dp', 'expert'))
- grad_gate: bfloat16 [64, 1536, 1536], P('expert', None, 'dp')
- grad_up: bfloat16 [64, 1536, 1536], P('expert', None, 'dp')
- grad_down: bfloat16 [64, 1536, 1536], P('expert', 'dp')
Inputs may be any that keep to these rules, and one draw needn't show every extreme that they name: `routes`: the two experts of a token differ. Among the 128 tokens of one source block no expert is named more than 5 times, and in every draw some expert is named exactly 5 times by some source block.
All inputs are finite; a program needn't handle non-finite values.
Results may differ from a plain program's by a relative error of at most 0.013.
Values may be sent and summed in bfloat16 or wider, within the bound.
No kernel may reach another device: no remote copies, remote signals or barrier semaphores. Data moves between devices by JAX's collectives and lax.ppermute only.
A program may use at most 128 MiB of HBM per device.

v0:
```python
import jax
import jax.numpy as jnp
from jax import lax
from jax.sharding import PartitionSpec as P


def dot_plain(left, right):
    return jnp.dot(left, right, preferred_element_type=jnp.float32)


def dot_last(left, right):
    return lax.dot_general(
        left, right, (((1,), (1,)), ((), ())), preferred_element_type=jnp.float32
    )


def dot_first(left, right):
    return lax.dot_general(
        left, right, (((0,), (0,)), ((), ())), preferred_element_type=jnp.float32
    )


def gate_grads(d_hidden, gate_pre, up_pre, sigmoid_gate):
    d_gate = (d_hidden * up_pre * sigmoid_gate * (1.0 + gate_pre * (1.0 - sigmoid_gate))).astype(
        jnp.bfloat16
    )
    d_up = (d_hidden * gate_pre * sigmoid_gate).astype(jnp.bfloat16)
    return (d_gate, d_up)


def on_device(tokens, routes, combine, w_gate, w_up, w_down, cotangent):
    experts = lax.axis_size("expert")
    count = tokens.shape[0]
    width = tokens.shape[1]
    capacity = 10 * count // (4 * experts)
    slot_total = experts * capacity
    flat = routes.reshape(-1)
    onehot = (flat[:, None] == jnp.arange(experts, dtype=jnp.int32)[None, :]).astype(jnp.int32)
    before = jnp.cumsum(onehot, axis=0) - onehot
    target_row = (flat * capacity + jnp.sum(before * onehot, axis=1)).reshape(count, 2)
    positions = jnp.arange(slot_total, dtype=jnp.int32)[:, None]
    pick_first = (positions == target_row[None, :, 0]).astype(jnp.bfloat16)
    pick_second = (positions == target_row[None, :, 1]).astype(jnp.bfloat16)
    pick_both = pick_first + pick_second
    send_rows = dot_plain(pick_both, tokens).astype(jnp.bfloat16).reshape(experts, capacity, width)
    token_rows = lax.all_to_all(
        send_rows, "expert", split_axis=0, concat_axis=0, tiled=True
    ).reshape(slot_total, width)
    full_gate, full_up, full_down = (
        lax.all_gather(w_gate, "dp", axis=2, tiled=True),
        lax.all_gather(w_up, "dp", axis=2, tiled=True),
        lax.all_gather(w_down, "dp", axis=1, tiled=True),
    )
    full_gate = full_gate[0]
    full_up = full_up[0]
    full_down = full_down[0]
    gate_pre = dot_plain(token_rows, full_gate)
    up_pre = dot_plain(token_rows, full_up)
    sigmoid_gate = jax.nn.sigmoid(gate_pre)
    hidden = (gate_pre * sigmoid_gate * up_pre).astype(jnp.bfloat16)
    expert_out = dot_plain(hidden, full_down).astype(jnp.bfloat16)
    returned = lax.all_to_all(
        expert_out.reshape(experts, capacity, width),
        "expert",
        split_axis=0,
        concat_axis=0,
        tiled=True,
    ).reshape(slot_total, width)
    first_out = dot_first(pick_first, returned)
    second_out = dot_first(pick_second, returned)
    out = (combine[:, 0:1] * first_out + combine[:, 1:2] * second_out).astype(jnp.bfloat16)
    cot = cotangent.astype(jnp.float32)
    d_combine = jnp.stack(
        [jnp.sum(cot * first_out, axis=1), jnp.sum(cot * second_out, axis=1)], axis=1
    )
    first_cot = (combine[:, 0:1] * cot).astype(jnp.bfloat16)
    second_cot = (combine[:, 1:2] * cot).astype(jnp.bfloat16)
    send_cot = (dot_plain(pick_first, first_cot) + dot_plain(pick_second, second_cot)).astype(
        jnp.bfloat16
    )
    cot_rows = lax.all_to_all(
        send_cot.reshape(experts, capacity, width),
        "expert",
        split_axis=0,
        concat_axis=0,
        tiled=True,
    ).reshape(slot_total, width)
    d_hidden = dot_last(cot_rows, full_down)
    d_gate, d_up = gate_grads(d_hidden, gate_pre, up_pre, sigmoid_gate)
    back_rows = (dot_last(d_gate, full_gate) + dot_last(d_up, full_up)).astype(jnp.bfloat16)
    grad_gate, grad_up = (
        lax.psum_scatter(
            dot_first(token_rows, d_gate).astype(jnp.bfloat16),
            "dp",
            scatter_dimension=1,
            tiled=True,
        ).astype(jnp.float32),
        lax.psum_scatter(
            dot_first(token_rows, d_up).astype(jnp.bfloat16), "dp", scatter_dimension=1, tiled=True
        ).astype(jnp.float32),
    )
    grad_down = lax.psum_scatter(
        dot_first(hidden, cot_rows).astype(jnp.bfloat16), "dp", scatter_dimension=0, tiled=True
    ).astype(jnp.float32)
    grad_gate = grad_gate.astype(jnp.bfloat16)
    grad_up = grad_up.astype(jnp.bfloat16)
    grad_down = grad_down.astype(jnp.bfloat16)
    arrived = lax.all_to_all(
        back_rows.reshape(experts, capacity, width),
        "expert",
        split_axis=0,
        concat_axis=0,
        tiled=True,
    ).reshape(slot_total, width)
    d_tokens = dot_first(pick_both, arrived).astype(jnp.bfloat16)
    return (out, d_tokens, d_combine, grad_gate[None], grad_up[None], grad_down[None])


def solution(mesh):
    placed = (
        P(("dp", "expert"), None),
        P(("dp", "expert"), None),
        P(("dp", "expert"), None),
        P("expert", None, "dp"),
        P("expert", None, "dp"),
        P("expert", "dp", None),
        P(("dp", "expert"), None),
    )
    return jax.shard_map(
        on_device,
        mesh=mesh,
        in_specs=placed,
        out_specs=(
            P(("dp", "expert"), None),
            P(("dp", "expert"), None),
            P(("dp", "expert"), None),
            P("expert", None, "dp"),
            P("expert", None, "dp"),
            P("expert", "dp", None),
        ),
        check_vma=False,
    )
```

profile of v0, /device:TPU:1, one launch (start us, length us, event | category | flops | bytes accessed | tf_op | source)
XLA Modules:
  0.0 657.9 jit_solution(5116882305012822754)
XLA Ops:
  11.4 1.3 reshape.59
  12.8 10.5 %all-to-all-start = ((bf16[64,5,1536]{2,1,0:T(8,128)(2,1)}), bf16[64,5,1536]{2,1,0:T(8,128)(2,1)S(1)}, u32[]{:S(2)}, u32[]{:S(2)}) async-start(bf16[64,5,1536]{2,1,0:T(8,128)(2,1)} %reshape.59), calls=%async_computation | async-start | bytes 3145728 | tf_op jit(solution)/shard_map/all_to_all | solution.py:46
  24.3 1.4 reshape.63
  25.7 52.6 %all-to-all-done = bf16[64,5,1536]{2,1,0:T(8,128)(2,1)S(1)} async-done(((bf16[64,5,1536]{2,1,0:T(8,128)(2,1)}), bf16[64,5,1536]{2,1,0:T(8,128)(2,1)S(1)}, u32[]{:S(2)}, u32[]{:S(2)}) %all-to-all-start) | async-done | bytes 983072 | tf_op jit(solution)/shard_map/all_to_all | solution.py:46
  78.3 14.9 %all-to-all-start.2 = ((bf16[64,5,1536]{2,1,0:T(8,128)(2,1)}), bf16[64,5,1536]{2,1,0:T(8,128)(2,1)S(1)}, u32[]{:S(2)}, u32[]{:S(2)}) async-start(bf16[64,5,1536]{2,1,0:T(8,128)(2,1)} %reshape.63), calls=%async_computation.2 | async-start | bytes 3145728 | tf_op jit(solution)/shard_map/all_to_all | solution.py:81
  93.3 1.2 reshape.60
  94.5 45.2 %all-to-all-done.2 = bf16[64,5,1536]{2,1,0:T(8,128)(2,1)S(1)} async-done(((bf16[64,5,1536]{2,1,0:T(8,128)(2,1)}), bf16[64,5,1536]{2,1,0:T(8,128)(2,1)S(1)}, u32[]{:S(2)}, u32[]{:S(2)}) %all-to-all-start.2) | async-done | bytes 983072 | tf_op jit(solution)/shard_map/all_to_all | solution.py:81
  140.2 5.6 fusion.6
  145.8 74.8 %all-gather.8.cloned.1.call-done = bf16[1,1536,1536]{2,1,0:T(8,128)(2,1)} async-done(((bf16[1,384,1536]{2,1,0:T(8,128)(2,1)}), bf16[1,1536,1536]{2,1,0:T(8,128)(2,1)}) %all-gather.8.cloned.1.call-update) | async-done | bytes 4718608 | tf_op jit(solution)/shard_map/all_gather | solution.py:52
  220.6 5.3 fusion
  225.9 90.4 %all-gather.4.cloned.1.call-done = bf16[1,1536,1536]{2,1,0:T(8,128)(2,1)} async-done(((bf16[1,1536,384]{2,1,0:T(8,128)(2,1)}), bf16[1,1536,1536]{2,1,0:T(8,128)(2,1)}) %all-gather.4.cloned.1.call-update) | async-done | bytes 4718608 | tf_op jit(solution)/shard_map/all_gather | solution.py:50
  316.3 6.9 %multiply_convert_fusion.1 = (bf16[320,1536]{1,0:T(8,128)(2,1)S(1)}, bf16[320,1536]{1,0:T(8,128)(2,1)S(1)}, bf16[320,1536]{1,0:T(8,128)(2,1)}) fusion(f32[320,1536]{1,0:T(8,128)} %fusion, f32[320,1536]{1,0:T(8,128)} %fusion.6, bf16[320,1536]{1,0:T(8,128)(2,1)S(1)} %copy-done.4, bf16[1,1536,1536]{2,1,0:T(8,128)(2,1)} %all-gather.4.cloned.1.call-done), kind=kOutput, calls=%fused_computation.23 | convolution fusion | flops 1517813760 | bytes 12582912 | tf_op jit(solution)/shard_map/dot_general | solution.py:8
  324.1 4.4 convolution_convert_fusion.2
  328.5 6.7 %copy.32 = bf16[1536,1536]{0,1:T(8,128)(2,1)} copy(bf16[1536,1536]{1,0:T(8,128)(2,1)} %convolution_convert_fusion.2) | data formatting | bytes 9437184
  335.4 5.5 convolution_convert_fusion.1
  340.9 6.6 %copy.34 = bf16[1536,1536]{0,1:T(8,128)(2,1)} copy(bf16[1536,1536]{1,0:T(8,128)(2,1)} %convolution_convert_fusion.1) | data formatting | bytes 9437184
  347.6 4.4 convolution_convert_fusion
  353.2 4.1 fusion.4
  357.3 4.4 fusion.15
  361.8 1.4 reshape.65
  363.2 21.2 %all-to-all-start.3 = ((bf16[64,5,1536]{2,1,0:T(8,128)(2,1)}), bf16[64,5,1536]{2,1,0:T(8,128)(2,1)S(1)}, u32[]{:S(2)}, u32[]{:S(2)}) async-start(bf16[64,5,1536]{2,1,0:T(8,128)(2,1)} %reshape.65), calls=%async_computation.3 | async-start | bytes 3145728 | tf_op jit(solution)/shard_map/all_to_all | solution.py:108
  384.4 4.4 fusion.19
  388.9 1.4 reshape.61
  390.2 62.2 %all-to-all-done.3 = bf16[64,5,1536]{2,1,0:T(8,128)(2,1)S(1)} async-done(((bf16[64,5,1536]{2,1,0:T(8,128)(2,1)}), bf16[64,5,1536]{2,1,0:T(8,128)(2,1)S(1)}, u32[]{:S(2)}, u32[]{:S(2)}) %all-to-all-start.3) | async-done | bytes 983072 | tf_op jit(solution)/shard_map/all_to_all | solution.py:108
  452.4 5.8 all-to-all-start.1
  458.3 1.2 reshape.66
  459.5 47.4 %all-to-all-done.1 = bf16[64,5,1536]{2,1,0:T(8,128)(2,1)S(1)} async-done(((bf16[64,5,1536]{2,1,0:T(8,128)(2,1)}), bf16[64,5,1536]{2,1,0:T(8,128)(2,1)S(1)}, u32[]{:S(2)}, u32[]{:S(2)}) %all-to-all-start.1) | async-done | bytes 983072 | tf_op jit(solution)/shard_map/all_to_all | solution.py:62
  507.7 1.3 fusion.24
  510.8 2.4 copy.33
  513.2 42.8 %reduce-scatter.12.cloned.1.call-done = bf16[384,1536]{1,0:T(8,128)(2,1)} async-done(((bf16[1536,1536]{1,0:T(8,128)(2,1)}), bf16[384,1536]{1,0:T(8,128)(2,1)}) %reduce-scatter.12.cloned.1.call-update) | async-done | bytes 1179664
  556.0 2.4 copy.35
  558.4 92.6 %reduce-scatter.8.cloned.1.call-done = bf16[384,1536]{1,0:T(8,128)(2,1)} async-done(((bf16[1536,1536]{1,0:T(8,128)(2,1)}), bf16[384,1536]{1,0:T(8,128)(2,1)}) %reduce-scatter.8.cloned.1.call-update) | async-done | bytes 1179664 | tf_op jit(solution)/shard_map/reduce_scatter | solution.py:102
  (58 shorter events, 10.7 us)
Async XLA Ops:
  7.2 3.9 copy-start
  7.2 2.2 copy-start.5
  7.2 133.0 %all-gather.6.cloned.1.call-start = ((), (), s32[]{:S(2)}) async-start(), calls=%async_computation.8 | async-start | bytes 5898240 | tf_op jit(solution)/shard_map/all_gather | solution.py:51
  7.9 212.6 %all-gather.8.cloned.1.call-start = ((), (), s32[]{:S(2)}) async-start(), calls=%async_computation.9 | async-start | bytes 5898240 | tf_op jit(solution)/shard_map/all_gather | solution.py:52
  8.7 307.6 %all-gather.4.cloned.1.call-start = ((), (), s32[]{:S(2)}) async-start(), calls=%async_computation.7 | async-start | bytes 5898240 | tf_op jit(solution)/shard_map/all_gather | solution.py:50
  12.8 10.5 %copy-start.6 = (f32[128,2]{0,1:T(2,128)S(1)}, f32[128,2]{0,1:T(2,128)}, u32[]{:S(2)}) copy-start(f32[128,2]{0,1:T(2,128)} %param.9) | copy-start | bytes 3076
  12.8 10.5 %copy-start.3 = (bf16[128,1536]{1,0:T(8,128)(2,1)S(1)}, bf16[128,1536]{1,0:T(8,128)(2,1)}, u32[]{:S(2)}) copy-start(bf16[128,1536]{1,0:T(8,128)(2,1)} %param.13) | copy-start | bytes 1179652
  12.8 65.5 %all-to-all-start = ((bf16[64,5,1536]{2,1,0:T(8,128)(2,1)}), bf16[64,5,1536]{2,1,0:T(8,128)(2,1)S(1)}, u32[]{:S(2)}, u32[]{:S(2)}) async-start(bf16[64,5,1536]{2,1,0:T(8,128)(2,1)} %reshape.59), calls=%async_computation | async-start | bytes 3145728 | tf_op jit(solution)/shard_map/all_to_all | solution.py:46
  78.3 61.4 %all-to-all-start.2 = ((bf16[64,5,1536]{2,1,0:T(8,128)(2,1)}), bf16[64,5,1536]{2,1,0:T(8,128)(2,1)S(1)}, u32[]{:S(2)}, u32[]{:S(2)}) async-start(bf16[64,5,1536]{2,1,0:T(8,128)(2,1)} %reshape.63), calls=%async_computation.2 | async-start | bytes 3145728 | tf_op jit(solution)/shard_map/all_to_all | solution.py:81
  93.2 417.6 %reduce-scatter.10.cloned.1.call-start = ((), (), s32[]{:S(2)}) async-start(), calls=%async_computation.11 | async-start | bytes 5898240
  145.8 170.5 %copy-start.4 = (bf16[320,1536]{1,0:T(8,128)(2,1)S(1)}, bf16[320,1536]{1,0:T(8,128)(2,1)}, u32[]{:S(2)}) copy-start(bf16[320,1536]{1,0:T(8,128)(2,1)} %reshape.60) | copy-start | bytes 2949124
  323.2 1.0 copy-start.8
  323.2 24.4 %copy-start.7 = (bf16[320,1536]{1,0:T(8,128)(2,1)}, bf16[320,1536]{1,0:T(8,128)(2,1)S(1)}, u32[]{:S(2)}) copy-start(bf16[320,1536]{1,0:T(8,128)(2,1)S(1)} %get-tuple-element.9) | copy-start | bytes 2949124
  335.2 220.8 %reduce-scatter.12.cloned.1.call-start = ((), (), s32[]{:S(2)}) async-start(), calls=%async_computation.12 | async-start | bytes 5898240
  347.5 303.5 %reduce-scatter.8.cloned.1.call-start = ((), (), s32[]{:S(2)}) async-start(), calls=%async_computation.10 | async-start | bytes 5898240 | tf_op jit(solution)/shard_map/reduce_scatter | solution.py:102
  352.0 1.2 copy-start.10
  353.2 4.1 copy-start.9
  363.2 89.3 %all-to-all-start.3 = ((bf16[64,5,1536]{2,1,0:T(8,128)(2,1)}), bf16[64,5,1536]{2,1,0:T(8,128)(2,1)S(1)}, u32[]{:S(2)}, u32[]{:S(2)}) async-start(bf16[64,5,1536]{2,1,0:T(8,128)(2,1)} %reshape.65), calls=%async_computation.3 | async-start | bytes 3145728 | tf_op jit(solution)/shard_map/all_to_all | solution.py:108
  452.4 54.4 %all-to-all-start.1 = ((bf16[64,5,1536]{2,1,0:T(8,128)(2,1)}), bf16[64,5,1536]{2,1,0:T(8,128)(2,1)S(1)}, u32[]{:S(2)}, u32[]{:S(2)}) async-start(bf16[64,5,1536]{2,1,0:T(8,128)(2,1)} %reshape.61), calls=%async_computation.1 | async-start | bytes 3145728 | tf_op jit(solution)/shard_map/all_to_all | solution.py:62
  507.3 2.4 copy-start.2
  510.8 140.2 %copy-start.1 = (bf16[128,1536]{1,0:T(8,128)(2,1)S(1)}, bf16[128,1536]{1,0:T(8,128)(2,1)}, u32[]{:S(2)}) copy-start(bf16[128,1536]{1,0:T(8,128)(2,1)} %param.7) | copy-start | bytes 1179652
Sparse Core Ops, SparseCore 0:
  9.9 129.3 all-gather.5
  141.1 79.3 all-gather.7
  222.4 93.8 all-gather.3
  335.3 120.2 reduce-scatter.9
  458.1 97.9 reduce-scatter.11
  559.0 91.9 reduce-scatter.7
where the time goes:
time: 659 us; the launch traced here: 658 us
  waiting for transfers between devices  510 us (77%)
  starting transfers between devices  52.9 us (8%)
  matrix products  49.4 us (7%)
  local copies, waits for them, and re-layouts  29.8 us (5%)
  between operations  14.3 us (2%)
    reduce_scatter x1, waiting for transfers between devices, on_device(): lax.psum_scatter(dot_first(hidden, cot_rows).astype(jnp.bfloat16), 'dp',...  92.6 us
    all_gather x1, waiting for transfers between devices, on_device(): lax.all_gather(w_gate, 'dp', axis=2, tiled=True)  90.4 us
    all_gather x1, waiting for transfers between devices, on_device(): lax.all_gather(w_down, 'dp', axis=1, tiled=True)  74.8 us
    all_to_all x1, waiting for transfers between devices, on_device(): lax.all_to_all(back_rows.reshape(experts, capacity, width), 'expert', spl...  62.2 us
    all_to_all x1, waiting for transfers between devices, on_device(): lax.all_to_all(send_rows, 'expert', split_axis=0, concat_axis=0, tiled=True)  52.6 us
    all_to_all x1, waiting for transfers between devices, on_device(): lax.all_to_all(expert_out.reshape(experts, capacity, width), 'expert', sp...  47.4 us
    all_to_all x1, waiting for transfers between devices, on_device(): lax.all_to_all(send_cot.reshape(experts, capacity, width), 'expert', spli...  45.2 us
    unnamed x8, waiting for transfers between devices  44.9 us
  transfers between devices with their start and end apart: 10, of which 8 were waited for; matrix products, arithmetic and copies ran while one was open for 9% of the time, Pallas kernels for 0%

commit v1 on v0

v1 whole, which is shorter than its diff:
```python
import jax
import jax.numpy as jnp
from jax import lax
from jax.sharding import PartitionSpec as P


def dot_plain(left, right):
    return jnp.dot(left, right, preferred_element_type=jnp.float32)


def dot_last(left, right):
    return lax.dot_general(
        left, right, (((1,), (1,)), ((), ())), preferred_element_type=jnp.float32
    )


def dot_first(left, right):
    return lax.dot_general(
        left, right, (((0,), (0,)), ((), ())), preferred_element_type=jnp.float32
    )


def gate_grads(d_hidden, gate_pre, up_pre, sigmoid_gate):
    d_gate = (d_hidden * up_pre * sigmoid_gate * (1.0 + gate_pre * (1.0 - sigmoid_gate))).astype(
        jnp.bfloat16
    )
    d_up = (d_hidden * gate_pre * sigmoid_gate).astype(jnp.bfloat16)
    return (d_gate, d_up)


def column_of(expert):
    return expert // 4 * 2 + expert % 2


def pair_of(expert):
    return expert // 2 % 2


def on_device(tokens, routes, combine, w_gate, w_up, w_down, cotangent):
    experts = lax.axis_size("expert")
    groups = lax.axis_size("dp")
    count = tokens.shape[0]
    width = tokens.shape[1]
    capacity = 10 * count // (4 * experts)
    slot_total = experts * capacity
    row_total = groups * slot_total
    columns = experts // 2
    planes = 2 * groups
    column_groups = [
        [e for e in range(experts) if pair_of(e) == pair] for pair in range(2)
    ]
    ring_groups = [
        [g * experts + column // 2 * 4 + pair * 2 + column % 2 for g in range(groups) for pair in range(2)]
        for column in range(columns)
    ]
    everyone = ("dp", "expert")

    flat = routes.reshape(-1)
    onehot = (flat[:, None] == jnp.arange(experts, dtype=jnp.int32)[None, :]).astype(jnp.int32)
    before = jnp.cumsum(onehot, axis=0) - onehot
    slots = jnp.sum(before * onehot, axis=1).reshape(count, 2)
    target_row = routes * capacity + slots
    positions = jnp.arange(slot_total, dtype=jnp.int32)[:, None]
    pick_first = (positions == target_row[None, :, 0]).astype(jnp.bfloat16)
    pick_second = (positions == target_row[None, :, 1]).astype(jnp.bfloat16)

    info = jnp.concatenate([routes.T, slots.T], axis=0).astype(jnp.bfloat16)
    info = jnp.pad(info, ((0, 4), (0, width - count)))
    ring = lax.all_gather(
        jnp.concatenate([tokens, info], axis=0), everyone, axis_index_groups=ring_groups, axis=0, tiled=True
    )

    cot = cotangent.astype(jnp.float32)
    first_cot = (combine[:, 0:1] * cot).astype(jnp.bfloat16)
    second_cot = (combine[:, 1:2] * cot).astype(jnp.bfloat16)
    send_cot = (dot_plain(pick_first, first_cot) + dot_plain(pick_second, second_cot)).astype(
        jnp.bfloat16
    )
    got_cot = lax.all_to_all(
        send_cot.reshape(experts, capacity, width), "expert", split_axis=0, concat_axis=0, tiled=True
    ).reshape(slot_total, width)
    cot_rows = lax.all_gather(got_cot, "dp", axis=0, tiled=True)

    rows_held = count + 8
    held = ring.reshape(planes, rows_held, width)[:, count : count + 4, :count].astype(jnp.int32)
    block = jnp.arange(planes, dtype=jnp.int32)[:, None, None]
    ring_expert, ring_slot = held[:, 0:2], held[:, 2:4]
    ring_row = column_of(ring_expert) * (planes * capacity) + block * capacity + ring_slot
    here = pair_of(ring_expert) == pair_of(lax.axis_index("expert"))
    ring_row = jnp.where(here, ring_row, -1)
    held_row = jnp.pad(ring_row, ((0, 0), (0, 0), (0, 8)), constant_values=-1)
    row_ids = jnp.arange(row_total, dtype=jnp.int32)[:, None]
    held_row = held_row.transpose(1, 0, 2).reshape(2, 1, planes * rows_held)
    select = ((row_ids == held_row[0]) | (row_ids == held_row[1])).astype(jnp.bfloat16)
    send_tokens = dot_plain(select, ring).astype(jnp.bfloat16)
    token_rows = lax.all_to_all(
        send_tokens.reshape(columns, planes * capacity, width),
        "expert",
        split_axis=0,
        concat_axis=0,
        tiled=True,
        axis_index_groups=column_groups,
    ).reshape(row_total, width)

    ids = jnp.arange(row_total, dtype=jnp.int32)
    column, plane, slot = ids // (planes * capacity), ids // capacity % planes, ids % capacity
    source = column // 2 * 4 + plane % 2 * 2 + column % 2
    cot_place = (plane // 2 * experts + source) * capacity + slot
    to_token_order = (cot_place[:, None] == ids[None, :]).astype(jnp.bfloat16)

    gate_w, up_w, down_w = w_gate[0], w_up[0], w_down[0]
    gate_pre = dot_plain(token_rows, gate_w)
    up_pre = dot_plain(token_rows, up_w)
    sigmoid_gate = jax.nn.sigmoid(gate_pre)
    hidden = (gate_pre * sigmoid_gate * up_pre).astype(jnp.bfloat16)
    hidden_cot = dot_first(to_token_order, hidden).astype(jnp.bfloat16)
    part_out = dot_plain(hidden_cot, down_w).astype(jnp.bfloat16)
    expert_out = lax.psum_scatter(part_out, "dp", scatter_dimension=0, tiled=True)

    d_hidden = dot_last(cot_rows, down_w).astype(jnp.bfloat16)
    d_hidden = dot_plain(to_token_order, d_hidden)
    d_gate, d_up = gate_grads(d_hidden, gate_pre, up_pre, sigmoid_gate)
    back_rows = (dot_last(d_gate, gate_w) + dot_last(d_up, up_w)).astype(jnp.bfloat16)
    arrived = lax.all_to_all(
        back_rows.reshape(columns, planes * capacity, width),
        "expert",
        split_axis=0,
        concat_axis=0,
        tiled=True,
        axis_index_groups=column_groups,
    ).reshape(row_total, width)
    token_row = ring_row.transpose(1, 0, 2).reshape(2, planes * count, 1)
    add_up = ((token_row[0] == ids[None, :]) | (token_row[1] == ids[None, :])).astype(jnp.bfloat16)
    d_ring = dot_plain(add_up, arrived).astype(jnp.bfloat16)
    d_tokens = lax.psum_scatter(
        d_ring, everyone, axis_index_groups=ring_groups, scatter_dimension=0, tiled=True
    )

    returned = lax.all_to_all(
        expert_out.reshape(experts, capacity, width), "expert", split_axis=0, concat_axis=0, tiled=True
    ).reshape(slot_total, width)
    first_out = dot_first(pick_first, returned)
    second_out = dot_first(pick_second, returned)
    out = (combine[:, 0:1] * first_out + combine[:, 1:2] * second_out).astype(jnp.bfloat16)
    d_combine = jnp.stack(
        [jnp.sum(cot * first_out, axis=1), jnp.sum(cot * second_out, axis=1)], axis=1
    )

    grad_gate = dot_first(token_rows, d_gate).astype(jnp.bfloat16)
    grad_up = dot_first(token_rows, d_up).astype(jnp.bfloat16)
    grad_down = dot_first(hidden_cot, cot_rows).astype(jnp.bfloat16)
    return (out, d_tokens, d_combine, grad_gate[None], grad_up[None], grad_down[None])


def solution(mesh):
    placed = (
        P(("dp", "expert"), None),
        P(("dp", "expert"), None),
        P(("dp", "expert"), None),
        P("expert", None, "dp"),
        P("expert", None, "dp"),
        P("expert", "dp", None),
        P(("dp", "expert"), None),
    )
    return jax.shard_map(
        on_device,
        mesh=mesh,
        in_specs=placed,
        out_specs=(
            P(("dp", "expert"), None),
            P(("dp", "expert"), None),
            P(("dp", "expert"), None),
            P("expert", None, "dp"),
            P("expert", None, "dp"),
            P("expert", "dp", None),
        ),
        check_vma=False,
    )
```

time: 659 us -> 312 us (0.47)
  waiting for transfers between devices: 510 us -> 181 us
  local copies, waits for them, and re-layouts: 29.8 us -> 9.66 us
  starting transfers between devices: 52.9 us -> 34.3 us
  matrix products: 49.4 us -> 66.9 us
    all_gather x3 -> x2, waiting for transfers between devices: 165 us -> 12.9 us  [the longest x1 12.8 us: on_device(): lax.all_gather(jnp.concatenate([tokens, info], axis=0), everyone, axis_in...]
    reduce_scatter x1 -> x2, waiting for transfers between devices: 92.6 us -> 7.51 us  [the longest x1 6.39 us: on_device(): lax.psum_scatter(d_ring, everyone, axis_index_groups=ring_groups, scatter...]
    unnamed x8 -> x4, waiting for transfers between devices: 44.9 us -> 0.07 us
    all_to_all x1, waiting for transfers between devices: 47.4 us -> 23.6 us  [on_device(): lax.all_to_all(expert_out.reshape(experts, capacity, width), 'expert', sp...]
    dot_general x6 -> x8, matrix products: 18.3 us -> 39.3 us  [dot_plain(): return jnp.dot(left, right, preferred_element_type=jnp.float32)]
    unnamed x27 -> x45, local copies, waits for them, and re-layouts: 20.3 us -> 1.93 us
    all_to_all x2, waiting for transfers between devices: 115 us -> 97.8 us  [the longest x1 49 us: on_device(): lax.all_to_all(back_rows.reshape(columns, planes * capacity, width), 'exp...]
    all_to_all x2, starting transfers between devices: 31.7 us -> 15.3 us  [the longest x1 8.17 us: on_device(): lax.all_to_all(send_tokens.reshape(columns, planes * capacity, width), 'e...]
  transfers between devices with their start and end apart: 10 -> 8, of which waited for: 8 -> 7; matrix products, arithmetic and copies ran while one was open for 9% -> 24% of each run, Pallas kernels for 0% -> 0%
where the time goes in v1:
time: 312 us; the launch traced here: 311 us
  waiting for transfers between devices  181 us (58%)
  matrix products  66.9 us (21%)
  starting transfers between devices  34.3 us (11%)
  between operations  14.2 us (5%)
  local copies, waits for them, and re-layouts  9.66 us (3%)
  other arithmetic  4.85 us (2%)
    all_to_all x1, waiting for transfers between devices, on_device(): lax.all_to_all(back_rows.reshape(columns, planes * capacity, width), 'exp...  49 us
    all_to_all x1, waiting for transfers between devices, on_device(): lax.all_to_all(send_tokens.reshape(columns, planes * capacity, width), 'e...  48.9 us
    dot_general x8, matrix products, dot_plain(): return jnp.dot(left, right, preferred_element_type=jnp.float32)  39.3 us
    all_to_all x1, waiting for transfers between devices, on_device(): lax.all_to_all(send_cot.reshape(experts, capacity, width), 'expert', spli...  39 us
    all_to_all x1, waiting for transfers between devices, on_device(): lax.all_to_all(expert_out.reshape(experts, capacity, width), 'expert', sp...  23.6 us
    dot_general x6, matrix products, dot_first(): lax.dot_general(left, right, (((0,), (0,)), ((), ())), preferred_element_...  19.6 us
    all_gather x1, waiting for transfers between devices, on_device(): lax.all_gather(jnp.concatenate([tokens, info], axis=0), everyone, axis_in...  12.8 us
    all_to_all x1, starting transfers between devices, on_device(): lax.all_to_all(send_cot.reshape(experts, capacity, width), 'expert', spli...  10.3 us
  transfers between devices with their start and end apart: 8, of which 7 were waited for; matrix products, arithmetic and copies ran while one was open for 24% of the time, Pallas kernels for 0%

profile of v1, /device:TPU:1, one launch (start us, length us, event | category | flops | bytes accessed | tf_op | source)
XLA Modules:
  0.0 310.7 jit_solution(6558378729620191308)
XLA Ops:
  7.2 0.9 copy.33
  9.7 0.8 multiply_add_fusion
  10.5 1.8 pad_maximum_fusion
  13.4 1.4 reshape.183
  14.8 10.3 %all-to-all-start.2 = ((bf16[64,5,1536]{2,1,0:T(8,128)(2,1)}), bf16[64,5,1536]{2,1,0:T(8,128)(2,1)S(1)}, u32[]{:S(2)}, u32[]{:S(2)}) async-start(bf16[64,5,1536]{2,1,0:T(8,128)(2,1)} %reshape.183), calls=%async_computation.3 | async-start | bytes 3145728 | tf_op jit(solution)/shard_map/all_to_all | solution.py:79
  25.3 39.0 %all-to-all-done.2 = bf16[64,5,1536]{2,1,0:T(8,128)(2,1)S(1)} async-done(((bf16[64,5,1536]{2,1,0:T(8,128)(2,1)}), bf16[64,5,1536]{2,1,0:T(8,128)(2,1)S(1)}, u32[]{:S(2)}, u32[]{:S(2)}) %all-to-all-start.2) | async-done | bytes 983072 | tf_op jit(solution)/shard_map/all_to_all | solution.py:79
  64.3 1.2 reshape.184
  65.5 12.8 %all-gather.3.cloned.1.call-done = bf16[1088,1536]{1,0:T(8,128)(2,1)} async-done(((bf16[136,1536]{1,0:T(8,128)(2,1)}), bf16[1088,1536]{1,0:T(8,128)(2,1)}) %all-gather.3.cloned.1.call-update) | async-done | bytes 3342352 | tf_op jit(solution)/shard_map/all_gather | solution.py:69
  79.4 8.6 %convolution_convert_fusion = bf16[1280,1536]{1,0:T(8,128)(2,1)} fusion(bf16[1088,1536]{1,0:T(8,128)(2,1)} %all-gather.3.cloned.1.call-done, s32[1088]{0:T(1024)S(1)} %eq.172, s32[1088]{0:T(1024)S(1)} %eq.168), kind=kOutput, calls=%fused_computation.1 | convolution fusion | flops 4284334080 | bytes 7283200 | tf_op jit(solution)/shard_map/dot_general | solution.py:8
  88.0 8.2 %all-to-all-start = ((bf16[32,40,1536]{2,1,0:T(8,128)(2,1)}), bf16[32,40,1536]{2,1,0:T(8,128)(2,1)}, u32[]{:S(2)}, u32[]{:S(2)}) async-start(bf16[32,40,1536]{2,1,0:T(8,128)(2,1)} %bitcast.86), calls=%async_computation | async-start | bytes 7864320 | tf_op jit(solution)/shard_map/all_to_all | solution.py:96
  96.5 48.9 %all-to-all-done = bf16[32,40,1536]{2,1,0:T(8,128)(2,1)} async-done(((bf16[32,40,1536]{2,1,0:T(8,128)(2,1)}), bf16[32,40,1536]{2,1,0:T(8,128)(2,1)}, u32[]{:S(2)}, u32[]{:S(2)}) %all-to-all-start) | async-done | bytes 3932192 | tf_op jit(solution)/shard_map/all_to_all | solution.py:96
  145.3 4.4 %fusion.25 = f32[1280,384]{1,0:T(8,128)S(1)} fusion(bf16[1280,1536]{1,0:T(8,128)(2,1)} %bitcast.8, bf16[1,1536,384]{2,1,0:T(8,128)(2,1)S(1)} %copy-done.4), kind=kOutput, calls=%fused_computation.42 | convolution fusion | flops 1509949440 | bytes 7077888 | tf_op jit(solution)/shard_map/dot_general | solution.py:8
  149.8 5.0 %fusion.29 = f32[1280,384]{1,0:T(8,128)S(1)} fusion(bf16[1280,1536]{1,0:T(8,128)(2,1)} %bitcast.8, bf16[1,1536,384]{2,1,0:T(8,128)(2,1)S(1)} %copy-done.3), kind=kOutput, calls=%fused_computation.46 | convolution fusion | flops 1509949440 | bytes 7077888 | tf_op jit(solution)/shard_map/dot_general | solution.py:8
  154.8 2.2 fusion.15
  157.1 0.9 copy-done.20
  158.1 4.2 %convolution_convert_fusion.1 = bf16[1280,1536]{1,0:T(8,128)(2,1)} fusion(bf16[1280,384]{1,0:T(8,128)(2,1)S(1)} %fusion.15, bf16[1,384,1536]{2,1,0:T(8,128)(2,1)S(1)} %copy-done), kind=kOutput, calls=%fused_computation.3 | convolution fusion | flops 1511915520 | bytes 6094848 | tf_op jit(solution)/shard_map/dot_general | solution.py:8
  162.3 7.8 %multiply_convert_fusion = (bf16[1280,384]{1,0:T(8,128)(2,1)S(1)}, bf16[1280,384]{1,0:T(8,128)(2,1)S(1)}) fusion(f32[1280,384]{1,0:T(8,128)} %copy-done.19, f32[1280,384]{1,0:T(8,128)} %copy-done.18, bf16[1280,1536]{1,0:T(8,128)(2,1)} %all-gather.5.cloned.1.call-done, bf16[1,384,1536]{2,1,0:T(8,128)(2,1)S(1)} %copy-done, s32[1280]{0:T(1024)} %copy-done.6), kind=kOutput, calls=%fused_computation.31 | convolution fusion | flops 2776760320 | bytes 11015168 | tf_op jit(solution)/shard_map/dot_general | solution.py:8
  170.1 3.6 %fusion.27 = f32[1280,1536]{1,0:T(8,128)S(1)} fusion(bf16[1280,384]{1,0:T(8,128)(2,1)S(1)} %get-tuple-element.11, bf16[1,1536,384]{2,1,0:T(8,128)(2,1)} %param.10), kind=kOutput, calls=%fused_computation.44 | convolution fusion | flops 1509949440 | bytes 10027008 | tf_op jit(solution)/shard_map/dot_general | solution.py:12
  173.7 4.4 %fusion = bf16[1280,1536]{1,0:T(8,128)(2,1)} fusion(f32[1280,1536]{1,0:T(8,128)S(1)} %fusion.27, bf16[1280,384]{1,0:T(8,128)(2,1)S(1)} %get-tuple-element.10, bf16[1,1536,384]{2,1,0:T(8,128)(2,1)S(1)} %copy-done.5), kind=kOutput, calls=%fused_computation.2 | convolution fusion | flops 1513881600 | bytes 13959168 | tf_op jit(solution)/shard_map/dot_general | solution.py:12
  178.1 7.1 %all-to-all-start.3 = ((bf16[32,40,1536]{2,1,0:T(8,128)(2,1)}), bf16[32,40,1536]{2,1,0:T(8,128)(2,1)}, u32[]{:S(2)}, u32[]{:S(2)}) async-start(bf16[32,40,1536]{2,1,0:T(8,128)(2,1)} %bitcast.85), calls=%async_computation.4 | async-start | bytes 7864320 | tf_op jit(solution)/shard_map/all_to_all | solution.py:124
  185.4 49.0 %all-to-all-done.3 = bf16[32,40,1536]{2,1,0:T(8,128)(2,1)} async-done(((bf16[32,40,1536]{2,1,0:T(8,128)(2,1)}), bf16[32,40,1536]{2,1,0:T(8,128)(2,1)}, u32[]{:S(2)}, u32[]{:S(2)}) %all-to-all-start.3) | async-done | bytes 3932192 | tf_op jit(solution)/shard_map/all_to_all | solution.py:124
  234.4 8.2 %fusion.8 = bf16[1024,1536]{1,0:T(8,128)(2,1)} fusion(bf16[1280,1536]{1,0:T(8,128)(2,1)} %bitcast.18, s32[1024]{0:T(1024)S(1)} %bitcast.88, s32[1024]{0:T(1024)S(1)} %bitcast.87), kind=kOutput, calls=%fused_computation.14 | convolution fusion | flops 4032036864 | bytes 7086080 | tf_op jit(solution)/shard_map/dot_general | solution.py:8
  242.7 1.1 reduce-scatter.3.cloned.1.call-done
  243.8 2.5 reshape.181
  246.3 8.3 %all-to-all-start.1 = ((bf16[64,5,1536]{2,1,0:T(8,128)(2,1)}), bf16[64,5,1536]{2,1,0:T(8,128)(2,1)}, u32[]{:S(2)}, u32[]{:S(2)}) async-start(bf16[64,5,1536]{2,1,0:T(8,128)(2,1)} %reshape.181), calls=%async_computation.2 | async-start | bytes 3145728 | tf_op jit(solution)/shard_map/all_to_all | solution.py:139
  254.5 4.8 %fusion.21 = bf16[1,384,1536]{2,1,0:T(8,128)(2,1)} fusion(bf16[1280,384]{1,0:T(8,128)(2,1)S(1)} %copy-done.21, bf16[1280,1536]{1,0:T(8,128)(2,1)} %all-gather.5.cloned.1.call-done), kind=kOutput, calls=%fused_computation.30 | convolution fusion | flops 1510539264 | bytes 6094848 | tf_op jit(solution)/shard_map/dot_general | solution.py:18
  259.4 5.4 %fusion.20 = bf16[1,1536,384]{2,1,0:T(8,128)(2,1)} fusion(bf16[1280,1536]{1,0:T(8,128)(2,1)} %bitcast.8, bf16[1280,384]{1,0:T(8,128)(2,1)S(1)} %get-tuple-element.10), kind=kOutput, calls=%fused_computation.29 | convolution fusion | flops 1510539264 | bytes 6094848 | tf_op jit(solution)/shard_map/dot_general | solution.py:18
  264.8 5.4 %fusion.19 = bf16[1,1536,384]{2,1,0:T(8,128)(2,1)} fusion(bf16[1280,1536]{1,0:T(8,128)(2,1)} %bitcast.8, bf16[1280,384]{1,0:T(8,128)(2,1)S(1)} %get-tuple-element.11), kind=kOutput, calls=%fused_computation.28 | convolution fusion | flops 1510539264 | bytes 6094848 | tf_op jit(solution)/shard_map/dot_general | solution.py:18
  270.2 23.6 %all-to-all-done.1 = bf16[64,5,1536]{2,1,0:T(8,128)(2,1)} async-done(((bf16[64,5,1536]{2,1,0:T(8,128)(2,1)}), bf16[64,5,1536]{2,1,0:T(8,128)(2,1)}, u32[]{:S(2)}, u32[]{:S(2)}) %all-to-all-start.1) | async-done | bytes 983072 | tf_op jit(solution)/shard_map/all_to_all | solution.py:139
  293.7 1.7 reshape.182
  295.9 1.3 fusion.33
  297.8 6.4 %reduce-scatter.5.cloned.1.call-done = bf16[128,1536]{1,0:T(8,128)(2,1)} async-done(((bf16[1024,1536]{1,0:T(8,128)(2,1)}), bf16[128,1536]{1,0:T(8,128)(2,1)}) %reduce-scatter.5.cloned.1.call-update) | async-done | bytes 393232 | tf_op jit(solution)/shard_map/reduce_scatter | solution.py:135
  (81 shorter events, 5.2 us)
Async XLA Ops:
  7.2 150.9 %copy-start = (bf16[1,384,1536]{2,1,0:T(8,128)(2,1)S(1)}, bf16[1,384,1536]{2,1,0:T(8,128)(2,1)}, u32[]{:S(2)}) copy-start(bf16[1,384,1536]{2,1,0:T(8,128)(2,1)} %param.12) | copy-start | bytes 3538948
  7.2 5.1 %copy-start.17 = (f32[128,2]{0,1:T(2,128)S(1)}, f32[128,2]{0,1:T(2,128)}, u32[]{:S(2)}) copy-start(f32[128,2]{0,1:T(2,128)} %param.9) | copy-start | bytes 3076
  7.2 5.2 %copy-start.2 = (bf16[128,1536]{1,0:T(8,128)(2,1)S(1)}, bf16[128,1536]{1,0:T(8,128)(2,1)}, u32[]{:S(2)}) copy-start(bf16[128,1536]{1,0:T(8,128)(2,1)} %param.13) | copy-start | bytes 1179652
  7.2 71.1 %all-gather.3.cloned.1.call-start = ((), (), s32[]{:S(2)}) async-start(), calls=%async_computation.6 | async-start | bytes 3760128 | tf_op jit(solution)/shard_map/all_gather | solution.py:69
  12.3 0.6 copy-start.9
  12.3 0.6 copy-start.7
  12.4 0.5 copy-start.11
  12.4 0.6 copy-start.13
  14.8 49.4 %all-to-all-start.2 = ((bf16[64,5,1536]{2,1,0:T(8,128)(2,1)}), bf16[64,5,1536]{2,1,0:T(8,128)(2,1)S(1)}, u32[]{:S(2)}, u32[]{:S(2)}) async-start(bf16[64,5,1536]{2,1,0:T(8,128)(2,1)} %reshape.183), calls=%async_computation.3 | async-start | bytes 3145728 | tf_op jit(solution)/shard_map/all_to_all | solution.py:79
  25.2 137.1 %all-gather.5.cloned.1.call-start = ((), (), s32[]{:S(2)}) async-start(), calls=%async_computation.8 | async-start | bytes 4915200 | tf_op jit(solution)/shard_map/all_gather | solution.py:82
  25.3 62.7 %copy-start.15 = (s32[8]{0:T(128)}, s32[8]{0:T(128)S(1)}, u32[]{:S(2)}) copy-start(s32[8]{0:T(128)S(1)} %iota_multiply_fusion) | copy-start | bytes 100
  88.0 57.3 %copy-start.4 = (bf16[1,1536,384]{2,1,0:T(8,128)(2,1)S(1)}, bf16[1,1536,384]{2,1,0:T(8,128)(2,1)}, u32[]{:S(2)}) copy-start(bf16[1,1536,384]{2,1,0:T(8,128)(2,1)} %param.11) | copy-start | bytes 3538948
  88.0 57.3 %all-to-all-start = ((bf16[32,40,1536]{2,1,0:T(8,128)(2,1)}), bf16[32,40,1536]{2,1,0:T(8,128)(2,1)}, u32[]{:S(2)}, u32[]{:S(2)}) async-start(bf16[32,40,1536]{2,1,0:T(8,128)(2,1)} %bitcast.86), calls=%async_computation | async-start | bytes 7864320 | tf_op jit(solution)/shard_map/all_to_all | solution.py:96
  96.2 147.6 %reduce-scatter.3.cloned.1.call-start = ((), (), s32[]{:S(2)}) async-start(), calls=%async_computation.7 | async-start | bytes 4915200 | tf_op jit(solution)/shard_map/reduce_scatter | solution.py:118
  96.5 58.4 %copy-start.6 = (s32[1280]{0:T(1024)}, s32[1280]{0:T(1024)S(1)}, u32[]{:S(2)}) copy-start(s32[1280]{0:T(1024)S(1)} %fusion.68) | copy-start | bytes 15364
  145.3 4.4 %copy-start.3 = (bf16[1,1536,384]{2,1,0:T(8,128)(2,1)S(1)}, bf16[1,1536,384]{2,1,0:T(8,128)(2,1)}, u32[]{:S(2)}) copy-start(bf16[1,1536,384]{2,1,0:T(8,128)(2,1)} %param.10) | copy-start | bytes 3538948
  149.8 5.1 %copy-start.18 = (f32[1280,384]{1,0:T(8,128)}, f32[1280,384]{1,0:T(8,128)S(1)}, u32[]{:S(2)}) copy-start(f32[1280,384]{1,0:T(8,128)S(1)} %fusion.25) | copy-start | bytes 5898244
  154.8 2.3 copy-start.19
  157.1 0.9 copy-start.20
  170.1 3.6 %copy-start.5 = (bf16[1,1536,384]{2,1,0:T(8,128)(2,1)S(1)}, bf16[1,1536,384]{2,1,0:T(8,128)(2,1)}, u32[]{:S(2)}) copy-start(bf16[1,1536,384]{2,1,0:T(8,128)(2,1)} %param.11) | copy-start | bytes 3538948
  178.1 7.2 %copy-start.16 = (s32[8]{0:T(128)S(1)}, s32[8]{0:T(128)}, u32[]{:S(2)}) copy-start(s32[8]{0:T(128)} %copy-done.15) | copy-start | bytes 100
  178.1 56.3 %all-to-all-start.3 = ((bf16[32,40,1536]{2,1,0:T(8,128)(2,1)}), bf16[32,40,1536]{2,1,0:T(8,128)(2,1)}, u32[]{:S(2)}, u32[]{:S(2)}) async-start(bf16[32,40,1536]{2,1,0:T(8,128)(2,1)} %bitcast.85), calls=%async_computation.4 | async-start | bytes 7864320 | tf_op jit(solution)/shard_map/all_to_all | solution.py:124
  185.3 118.9 %reduce-scatter.5.cloned.1.call-start = ((), (), s32[]{:S(2)}) async-start(), calls=%async_computation.9 | async-start | bytes 3538944 | tf_op jit(solution)/shard_map/reduce_scatter | solution.py:135
  246.3 8.3 %copy-start.21 = (bf16[1280,384]{1,0:T(8,128)(2,1)S(1)}, bf16[1280,384]{1,0:T(8,128)(2,1)}, u32[]{:S(2)}) copy-start(bf16[1280,384]{1,0:T(8,128)(2,1)} %copy-done.20) | copy-start | bytes 2949124
  246.3 47.5 %all-to-all-start.1 = ((bf16[64,5,1536]{2,1,0:T(8,128)(2,1)}), bf16[64,5,1536]{2,1,0:T(8,128)(2,1)}, u32[]{:S(2)}, u32[]{:S(2)}) async-start(bf16[64,5,1536]{2,1,0:T(8,128)(2,1)} %reshape.181), calls=%async_computation.2 | async-start | bytes 3145728 | tf_op jit(solution)/shard_map/all_to_all | solution.py:139
  270.2 25.3 %copy-start.14 = (s32[128]{0:T(128)S(1)}, s32[128]{0:T(128)}, u32[]{:S(2)}) copy-start(s32[128]{0:T(128)} %copy-done.13) | copy-start | bytes 1540
  270.2 25.7 %copy-start.8 = (f32[128]{0:T(128)S(1)}, f32[128]{0:T(128)}, u32[]{:S(2)}) copy-start(f32[128]{0:T(128)} %copy-done.7) | copy-start | bytes 1540
  270.2 25.7 %copy-start.10 = (f32[128]{0:T(128)S(1)}, f32[128]{0:T(128)}, u32[]{:S(2)}) copy-start(f32[128]{0:T(128)} %copy-done.9) | copy-start | bytes 1540
  270.2 25.7 %copy-start.12 = (s32[128]{0:T(128)S(1)}, s32[128]{0:T(128)}, u32[]{:S(2)}) copy-start(s32[128]{0:T(128)} %copy-done.11) | copy-start | bytes 1540
  293.7 10.5 %copy-start.1 = (bf16[1,384,1536]{2,1,0:T(8,128)(2,1)S(1)}, bf16[1,384,1536]{2,1,0:T(8,128)(2,1)}, u32[]{:S(2)}) copy-start(bf16[1,384,1536]{2,1,0:T(8,128)(2,1)} %param.12) | copy-start | bytes 3538948
Sparse Core Ops, SparseCore 0:
  12.4 65.8 all-gather.2
  80.7 74.3 all-gather.4
  162.3 81.3 reduce-scatter.2
  246.8 57.3 reduce-scatter.4

commit v2 on v1

v2 whole, which is shorter than its diff:
```python
import jax
import jax.numpy as jnp
from jax import lax
from jax.experimental import pallas as pl
from jax.experimental.pallas import tpu as pltpu
from jax.sharding import PartitionSpec as P


def dot_plain(left, right):
    return jnp.dot(left, right, preferred_element_type=jnp.float32)


def dot_last(left, right):
    return lax.dot_general(
        left, right, (((1,), (1,)), ((), ())), preferred_element_type=jnp.float32
    )


def dot_first(left, right):
    return lax.dot_general(
        left, right, (((0,), (0,)), ((), ())), preferred_element_type=jnp.float32
    )


ROWS = 256


def forward_kernel(x_ref, w_ref, pre_ref, hidden_ref):
    pre = dot_plain(x_ref[...], w_ref[...])
    pre_ref[...] = pre
    half = pre.shape[1] // 2
    gate_pre, up_pre = pre[:, :half], pre[:, half:]
    hidden_ref[...] = (gate_pre * jax.nn.sigmoid(gate_pre) * up_pre).astype(jnp.bfloat16)


def forward(rows, weights):
    total, width = rows.shape
    both = weights.shape[1]
    return pl.pallas_call(
        forward_kernel,
        grid=(total // ROWS,),
        in_specs=[
            pl.BlockSpec((ROWS, width), lambda i: (i, 0)),
            pl.BlockSpec((width, both), lambda i: (0, 0), pipeline_mode=pl.Buffered(1)),
        ],
        out_specs=[
            pl.BlockSpec((ROWS, both), lambda i: (i, 0)),
            pl.BlockSpec((ROWS, both // 2), lambda i: (i, 0)),
        ],
        out_shape=[
            jax.ShapeDtypeStruct((total, both), jnp.float32),
            jax.ShapeDtypeStruct((total, both // 2), jnp.bfloat16),
        ],
        compiler_params=pltpu.CompilerParams(vmem_limit_bytes=24 << 20),
        name="forward_rows",
    )(rows, weights)


def backward_kernel(place_ref, d_ref, pre_ref, w_ref, grads_ref, back_ref):
    total = d_ref.shape[0]
    places = jnp.broadcast_to(place_ref[...], (ROWS, total))
    select = jnp.where(places == lax.broadcasted_iota(jnp.int32, (ROWS, total), 1), 1.0, 0.0)
    d_hidden = dot_plain(select.astype(jnp.bfloat16), d_ref[...])
    half = d_hidden.shape[1]
    gate_pre, up_pre = pre_ref[:, :half], pre_ref[:, half:]
    sigmoid_gate = jax.nn.sigmoid(gate_pre)
    d_gate = d_hidden * up_pre * sigmoid_gate * (1.0 + gate_pre * (1.0 - sigmoid_gate))
    d_up = d_hidden * gate_pre * sigmoid_gate
    grads_ref[:, :half] = d_gate.astype(jnp.bfloat16)
    grads_ref[:, half:] = d_up.astype(jnp.bfloat16)
    back_ref[...] = dot_plain(grads_ref[...], w_ref[...]).astype(jnp.bfloat16)


def backward(places, d_hidden, pre, weights):
    total, both = pre.shape
    width = weights.shape[1]
    return pl.pallas_call(
        backward_kernel,
        grid=(total // ROWS,),
        in_specs=[
            pl.BlockSpec((ROWS, 1), lambda i: (i, 0)),
            pl.BlockSpec((total, both // 2), lambda i: (0, 0), pipeline_mode=pl.Buffered(1)),
            pl.BlockSpec((ROWS, both), lambda i: (i, 0)),
            pl.BlockSpec((both, width), lambda i: (0, 0), pipeline_mode=pl.Buffered(1)),
        ],
        out_specs=[
            pl.BlockSpec((ROWS, both), lambda i: (i, 0)),
            pl.BlockSpec((ROWS, width), lambda i: (i, 0)),
        ],
        out_shape=[
            jax.ShapeDtypeStruct((total, both), jnp.bfloat16),
            jax.ShapeDtypeStruct((total, width), jnp.bfloat16),
        ],
        compiler_params=pltpu.CompilerParams(vmem_limit_bytes=24 << 20),
        name="backward_rows",
    )(places, d_hidden, pre, weights)


PADDED = 8


def prepare_kernel(tokens_ref, routes_ref, combine_ref, cot_ref, own_ref, send_ref, chosen_ref):
    count = tokens_ref.shape[0]
    square = (count, count)
    row, col = lax.broadcasted_iota(jnp.int32, square, 0), lax.broadcasted_iota(jnp.int32, square, 1)
    chosen = routes_ref[...].astype(jnp.float32)
    down = [jnp.broadcast_to(chosen[:, k : k + 1], square) for k in range(2)]
    across = [expert.T for expert in down]
    slots = [
        jnp.sum(
            jnp.where((row < col) & ((down[0] == expert) | (down[1] == expert)), 1.0, 0.0),
            axis=0,
            keepdims=True,
        )
        for expert in across
    ]
    own_ref[:count, :] = tokens_ref[...]
    own_ref[count:, :] = jnp.zeros((own_ref.shape[0] - count, own_ref.shape[1]), jnp.bfloat16)
    lines = [across[0][:1], across[1][:1], slots[0], slots[1], jnp.zeros((12, count), jnp.float32)]
    own_ref[count:, :count] = jnp.concatenate(lines, axis=0).astype(jnp.bfloat16)
    cot = cot_ref[...].astype(jnp.float32)
    total = None
    for k in range(2):
        expert, slot = across[k][:1].astype(jnp.int32), slots[k].astype(jnp.int32)
        chosen_ref[k : k + 1, :] = expert
        chosen_ref[k + 2 : k + 3, :] = slot
        quarter, last = lax.shift_right_logical(expert, 2), lax.bitwise_and(expert, 1)
        pair = lax.bitwise_and(lax.shift_right_logical(expert, 1), 1)
        places = ((quarter * 2 + last) * 2 + pair) * PADDED + slot
        places = jnp.broadcast_to(places, (send_ref.shape[0], count))
        pick = jnp.where(lax.broadcasted_iota(jnp.int32, places.shape, 0) == places, 1.0, 0.0)
        weighted = (combine_ref[:, k : k + 1] * cot).astype(jnp.bfloat16)
        part = dot_plain(pick.astype(jnp.bfloat16), weighted)
        total = part if total is None else total + part
    send_ref[...] = total.astype(jnp.bfloat16)


def prepare(tokens, routes, combine, cotangent, experts):
    count, width = tokens.shape
    return pl.pallas_call(
        prepare_kernel,
        out_shape=[
            jax.ShapeDtypeStruct((count + 16, width), jnp.bfloat16),
            jax.ShapeDtypeStruct((experts * PADDED, width), jnp.bfloat16),
            jax.ShapeDtypeStruct((4, count), jnp.int32),
        ],
        compiler_params=pltpu.CompilerParams(vmem_limit_bytes=24 << 20),
        name="prepare_rows",
    )(tokens, routes, combine, cotangent)


def column_of(expert):
    return expert // 4 * 2 + expert % 2


def pair_of(expert):
    return expert // 2 % 2


def ring_shift(x, step):
    groups, experts = lax.axis_size("dp"), lax.axis_size("expert")
    pairs = []
    for group in range(groups):
        for expert in range(experts):
            z = (group * 2 + pair_of(expert) + step) % (2 * groups)
            target = z // 2 * experts + expert // 4 * 4 + z % 2 * 2 + expert % 2
            pairs.append((group * experts + expert, target))
    return lax.ppermute(x, ("dp", "expert"), pairs)


def group_shift(x, step):
    groups = lax.axis_size("dp")
    return lax.ppermute(x, "dp", [(g, (g + step) % groups) for g in range(groups)])


def pair_swap(x):
    experts = lax.axis_size("expert")
    return lax.ppermute(x, "expert", [(e, e + 2 - pair_of(e) * 4) for e in range(experts)])


def sum_of(*parts):
    total = parts[0].astype(jnp.float32)
    for part in parts[1:]:
        total = total + part.astype(jnp.float32)
    return total.astype(jnp.bfloat16)


def join(size, blocks):
    whole = jnp.zeros((size, blocks[0][1].shape[1]), blocks[0][1].dtype)
    for start, block in blocks:
        whole = lax.dynamic_update_slice_in_dim(whole, block, start, 0)
    return whole


def on_device(tokens, routes, combine, w_gate, w_up, w_down, cotangent):
    experts = lax.axis_size("expert")
    groups = lax.axis_size("dp")
    count = tokens.shape[0]
    width = tokens.shape[1]
    capacity = 10 * count // (4 * experts)
    slot_total = experts * capacity
    row_total = groups * slot_total
    columns = experts // 2
    planes = 2 * groups
    column_groups = [[e for e in range(experts) if pair_of(e) == pair] for pair in range(2)]
    ring_groups = [
        [g * experts + column // 2 * 4 + pair * 2 + column % 2 for g in range(groups) for pair in range(2)]
        for column in range(columns)
    ]
    everyone = ("dp", "expert")
    group = lax.axis_index("dp")
    place = lax.axis_index("expert")
    z = group * 2 + pair_of(place)

    own, send_cot, chosen = prepare(tokens, routes, combine, cotangent, experts)
    pair = pair_of(place)
    got = lax.all_to_all(
        send_cot.reshape(columns, 2 * PADDED, width),
        "expert",
        split_axis=0,
        concat_axis=0,
        tiled=True,
        axis_index_groups=column_groups,
    )
    got = [got[:, k * PADDED : k * PADDED + capacity].reshape(slot_total // 2, width) for k in range(2)]
    kept, passed = jnp.where(pair == 0, got[0], got[1]), jnp.where(pair == 0, got[1], got[0])
    got_cot = jnp.concatenate([kept, pair_swap(passed)], axis=0)
    cot = cotangent.astype(jnp.float32)
    target_row = (column_of(chosen[:2]) * 2 + (pair_of(chosen[:2]) != pair)) * capacity + chosen[2:]
    positions = jnp.arange(slot_total, dtype=jnp.int32)[:, None]
    pick_first = (positions == target_row[0:1]).astype(jnp.bfloat16)
    pick_second = (positions == target_row[1:2]).astype(jnp.bfloat16)

    held_count = count + 16
    ring = lax.all_gather(own, everyone, axis_index_groups=ring_groups, axis=0, tiled=True)

    half_rows = slot_total // 2
    cot_rows = lax.all_gather(got_cot, "dp", axis=0, tiled=True)

    held = ring.reshape(planes, held_count, width)[:, count : count + 4, :count].astype(jnp.int32)
    block = jnp.arange(planes, dtype=jnp.int32)[:, None, None]
    ring_expert, ring_slot = held[:, 0:2], held[:, 2:4]
    ring_row = column_of(ring_expert) * (planes * capacity) + block * capacity + ring_slot
    here = pair_of(ring_expert) == pair_of(place)
    ring_row = jnp.where(here, ring_row, -1)
    held_row = jnp.pad(ring_row, ((0, 0), (0, 0), (0, held_count - count)), constant_values=-1)
    held_row = held_row.transpose(1, 0, 2).reshape(2, 1, planes * held_count)
    row_ids = jnp.arange(row_total, dtype=jnp.int32)[:, None]
    select = ((row_ids == held_row[0]) | (row_ids == held_row[1])).astype(jnp.bfloat16)
    send_tokens = dot_plain(select, ring).astype(jnp.bfloat16)
    token_rows = lax.all_to_all(
        send_tokens.reshape(columns, planes * capacity, width),
        "expert",
        split_axis=0,
        concat_axis=0,
        tiled=True,
        axis_index_groups=column_groups,
    ).reshape(row_total, width)

    ids = jnp.arange(row_total, dtype=jnp.int32)
    column, plane, slot = ids // (planes * capacity), ids // capacity % planes, ids % capacity
    cot_place = (plane // 2 * 2 + (plane % 2 != pair)) * (slot_total // 2) + column * capacity + slot
    to_token_order = (cot_place[:, None] == ids[None, :]).astype(jnp.bfloat16)

    down_w = w_down[0]
    up_gate_w = jnp.concatenate([w_gate[0], w_up[0]], axis=1)
    up_gate_wt = jnp.concatenate([w_gate[0].T, w_up[0].T], axis=0)
    pre, hidden = forward(token_rows, up_gate_w)
    hidden_cot = dot_first(to_token_order, hidden).astype(jnp.bfloat16)
    part_out = dot_plain(hidden_cot, down_w).astype(jnp.bfloat16)
    expert_out = lax.psum_scatter(part_out, "dp", scatter_dimension=0, tiled=True)

    d_hidden = dot_last(cot_rows, down_w).astype(jnp.bfloat16)
    d_hidden, _ = lax.optimization_barrier((d_hidden, part_out))
    d_both, back_rows = backward(cot_place[:, None], d_hidden, pre, up_gate_wt)
    d_gate, d_up = d_both[:, : down_w.shape[0]], d_both[:, down_w.shape[0] :]
    arrived = lax.all_to_all(
        back_rows.reshape(columns, planes * capacity, width),
        "expert",
        split_axis=0,
        concat_axis=0,
        tiled=True,
        axis_index_groups=column_groups,
    ).reshape(row_total, width)
    token_row = ring_row.transpose(1, 0, 2).reshape(2, planes * count, 1)
    add_up = ((token_row[0] == ids[None, :]) | (token_row[1] == ids[None, :])).astype(jnp.bfloat16)
    d_ring = dot_plain(add_up, arrived).astype(jnp.bfloat16)
    d_tokens = lax.psum_scatter(
        d_ring, everyone, axis_index_groups=ring_groups, scatter_dimension=0, tiled=True
    )

    half_rows = slot_total // 2
    from_pair = [expert_out[:half_rows], pair_swap(expert_out[half_rows:])]
    from_pair = [rows.reshape(columns, 1, capacity, width) for rows in from_pair]
    returned = lax.all_to_all(
        jnp.concatenate(from_pair, axis=1).reshape(columns, 2 * capacity, width),
        "expert",
        split_axis=0,
        concat_axis=0,
        tiled=True,
        axis_index_groups=column_groups,
    ).reshape(slot_total, width)
    first_out = dot_first(pick_first, returned)
    second_out = dot_first(pick_second, returned)
    out = (combine[:, 0:1] * first_out + combine[:, 1:2] * second_out).astype(jnp.bfloat16)
    d_combine = jnp.stack(
        [jnp.sum(cot * first_out, axis=1), jnp.sum(cot * second_out, axis=1)], axis=1
    )

    grad_gate = dot_first(token_rows, d_gate).astype(jnp.bfloat16)
    grad_up = dot_first(token_rows, d_up).astype(jnp.bfloat16)
    grad_down = dot_first(hidden_cot, cot_rows).astype(jnp.bfloat16)
    return (out, d_tokens, d_combine, grad_gate[None], grad_up[None], grad_down[None])


def solution(mesh):
    placed = (
        P(("dp", "expert"), None),
        P(("dp", "expert"), None),
        P(("dp", "expert"), None),
        P("expert", None, "dp"),
        P("expert", None, "dp"),
        P("expert", "dp", None),
        P(("dp", "expert"), None),
    )
    return jax.shard_map(
        on_device,
        mesh=mesh,
        in_specs=placed,
        out_specs=(
            P(("dp", "expert"), None),
            P(("dp", "expert"), None),
            P(("dp", "expert"), None),
            P("expert", None, "dp"),
            P("expert", None, "dp"),
            P("expert", "dp", None),
        ),
        check_vma=False,
    )
```

time: 312 us -> 306 us (0.981)
  waiting for transfers between devices: 181 us -> 154 us
  matrix products: 66.9 us -> 45.2 us
  local copies, waits for them, and re-layouts: 9.66 us -> 26.6 us
  Pallas kernels: 0 us -> 15.3 us
  other arithmetic: 4.85 us -> 11 us
  starting transfers between devices: 34.3 us -> 38 us
    all_to_all x2, waiting for transfers between devices: 62.5 us -> 35 us  [the longest x1 22.6 us: on_device(): lax.all_to_all(send_cot.reshape(columns, 2 * PADDED, width), 'expert', sp...]
    ppermute x0 -> x2, waiting for transfers between devices: none -> 26.6 us  [pair_swap(): lax.ppermute(x, 'expert', [(e, e + 2 - pair_of(e) * 4) for e in range(exp...]
    dot_general x8 -> x3, matrix products: 39.3 us -> 21 us  [dot_plain(): return jnp.dot(left, right, preferred_element_type=jnp.float32)]
    pallas_call x0 -> x3, Pallas kernels: none -> 15.3 us  [the longest x1 7.1 us: backward(): pl.pallas_call(backward_kernel, grid=(total // ROWS,), in_specs=[pl.Block...]
    unnamed x45 -> x42, local copies, waits for them, and re-layouts: 1.93 us -> 12.7 us
    all_gather x1, waiting for transfers between devices: 12.8 us -> 2.78 us  [on_device(): lax.all_gather(own, everyone, axis_index_groups=ring_groups, axis=0, tile...]
    all_to_all x1, waiting for transfers between devices: 48.9 us -> 40.7 us  [on_device(): lax.all_to_all(send_tokens.reshape(columns, planes * capacity, width), 'e...]
    reduce_scatter x1, waiting for transfers between devices: 6.39 us -> 0.01 us  [on_device(): lax.psum_scatter(d_ring, everyone, axis_index_groups=ring_groups, scatter...]
  transfers between devices with their start and end apart: 8 -> 10, of which waited for: 7 -> 8; matrix products, arithmetic and copies ran while one was open for 24% -> 24% of each run, Pallas kernels for 0% -> 4%
where the time goes in v2:
time: 306 us; the launch traced here: 305 us
  waiting for transfers between devices  154 us (50%)
  matrix products  45.2 us (15%)
  starting transfers between devices  38 us (12%)
  local copies, waits for them, and re-layouts  26.6 us (9%)
  Pallas kernels  15.3 us (5%)
  between operations  14.1 us (5%)
  other arithmetic  11 us (4%)
    all_to_all x1, waiting for transfers between devices, on_device(): lax.all_to_all(back_rows.reshape(columns, planes * capacity, width), 'exp...  48.8 us
    all_to_all x1, waiting for transfers between devices, on_device(): lax.all_to_all(send_tokens.reshape(columns, planes * capacity, width), 'e...  40.7 us
    ppermute x2, waiting for transfers between devices, pair_swap(): lax.ppermute(x, 'expert', [(e, e + 2 - pair_of(e) * 4) for e in range(exp...  26.6 us
    all_to_all x1, waiting for transfers between devices, on_device(): lax.all_to_all(send_cot.reshape(columns, 2 * PADDED, width), 'expert', sp...  22.6 us
    dot_general x3, matrix products, dot_plain(): return jnp.dot(left, right, preferred_element_type=jnp.float32)  21 us
    dot_general x6, matrix products, dot_first(): lax.dot_general(left, right, (((0,), (0,)), ((), ())), preferred_element_...  19.7 us
    unnamed x42, local copies, waits for them, and re-layouts  12.7 us
    all_to_all x1, waiting for transfers between devices, on_device(): lax.all_to_all(jnp.concatenate(from_pair, axis=1).reshape(columns, 2 * ca...  12.4 us
  transfers between devices with their start and end apart: 10, of which 8 were waited for; matrix products, arithmetic and copies ran while one was open for 24% of the time, Pallas kernels for 4%

profile of v2, /device:TPU:1, one launch (start us, length us, event | category | flops | bytes accessed | tf_op | source)
XLA Modules:
  0.0 304.5 jit_solution(6173701158450949804)
XLA Ops:
  10.9 2.4 prepare_rows.1
  13.3 8.6 %all-to-all-start.2 = ((bf16[32,16,1536]{2,1,0:T(8,128)(2,1)}), bf16[32,16,1536]{2,1,0:T(8,128)(2,1)S(1)}, u32[]{:S(2)}, u32[]{:S(2)}) async-start(bf16[32,16,1536]{2,1,0:T(8,128)(2,1)} %bitcast.15), calls=%async_computation.3 | async-start | bytes 3145728 | tf_op jit(solution)/shard_map/all_to_all | solution.py:217
  22.0 22.6 %all-to-all-done.2 = bf16[32,16,1536]{2,1,0:T(8,128)(2,1)S(1)} async-done(((bf16[32,16,1536]{2,1,0:T(8,128)(2,1)}), bf16[32,16,1536]{2,1,0:T(8,128)(2,1)S(1)}, u32[]{:S(2)}, u32[]{:S(2)}) %all-to-all-start.2) | async-done | bytes 1572896 | tf_op jit(solution)/shard_map/all_to_all | solution.py:217
  47.0 1.7 collective-permute-start.1
  48.9 21.5 %collective-permute-done.1 = bf16[160,1536]{1,0:T(8,128)(2,1)S(1)} collective-permute-done((bf16[160,1536]{1,0:T(8,128)(2,1)S(1)}, bf16[160,1536]{1,0:T(8,128)(2,1)S(1)}, u32[]{:S(2)}, u32[]{:S(2)}) %collective-permute-start.1) | collective-permute-done | bytes 491552 | tf_op jit(solution)/shard_map/ppermute | solution.py:178
  71.5 2.8 all-gather.3.cloned.1.call-done
  75.9 8.7 %convolution_convert_fusion = bf16[1280,1536]{1,0:T(8,128)(2,1)} fusion(bf16[1152,1536]{1,0:T(8,128)(2,1)} %all-gather.3.cloned.1.call-done, s32[1152]{0:T(1024)S(1)} %eq.140, s32[1152]{0:T(1024)S(1)} %eq.136), kind=kOutput, calls=%fused_computation | convolution fusion | flops 4536238080 | bytes 7480320 | tf_op jit(solution)/shard_map/dot_general | solution.py:10
  84.6 9.1 %all-to-all-start = ((bf16[32,40,1536]{2,1,0:T(8,128)(2,1)}), bf16[32,40,1536]{2,1,0:T(8,128)(2,1)}, u32[]{:S(2)}, u32[]{:S(2)}) async-start(bf16[32,40,1536]{2,1,0:T(8,128)(2,1)} %bitcast.56), calls=%async_computation | async-start | bytes 7864320 | tf_op jit(solution)/shard_map/all_to_all | solution.py:251
  94.7 2.0 copy.28
  99.3 2.8 copy.29.w_ref
  102.2 40.7 %all-to-all-done = bf16[32,40,1536]{2,1,0:T(8,128)(2,1)} async-done(((bf16[32,40,1536]{2,1,0:T(8,128)(2,1)}), bf16[32,40,1536]{2,1,0:T(8,128)(2,1)}, u32[]{:S(2)}, u32[]{:S(2)}) %all-to-all-start) | async-done | bytes 3932192 | tf_op jit(solution)/shard_map/all_to_all | solution.py:251
  142.9 5.8 %forward_rows.1 = (f32[1280,768]{1,0:T(8,128)S(1)}, bf16[1280,384]{1,0:T(8,128)(2,1)S(1)}) custom-call(bf16[1280,1536]{1,0:T(8,128)(2,1)} %bitcast.5.x_ref, bf16[1536,768]{1,0:T(8,128)(2,1)S(1)} %copy.29.w_ref), custom_call_target="tpu_custom_call" | custom-call | tf_op jit(solution)/shard_map/forward_rows/pallas_call | solution.py:39
  148.7 2.2 fusion.12
  152.0 4.1 %convolution_convert_fusion.1 = bf16[1280,1536]{1,0:T(8,128)(2,1)} fusion(bf16[1280,384]{1,0:T(8,128)(2,1)S(1)} %fusion.12, bf16[1,384,1536]{2,1,0:T(8,128)(2,1)S(1)} %copy-done), kind=kOutput, calls=%fused_computation.1 | convolution fusion | flops 1511915520 | bytes 6094848 | tf_op jit(solution)/shard_map/dot_general | solution.py:10
  156.1 1.8 pad_maximum_fusion.1.w_ref
  157.9 2.6 fusion.32.place_ref
  160.5 4.5 %convolution_convert_fusion.5.d_ref = bf16[1280,384]{1,0:T(8,128)(2,1)S(1)} fusion(bf16[1280,1536]{1,0:T(8,128)(2,1)} %all-gather.5.cloned.1.call-done, bf16[1,384,1536]{2,1,0:T(8,128)(2,1)S(1)} %copy-done), kind=kOutput, calls=%fused_computation.19 | convolution fusion | flops 1510440960 | bytes 6094848 | tf_op jit(solution)/shard_map/dot_general | solution.py:14
  165.0 7.1 %backward_rows.1 = (bf16[1280,768]{1,0:T(8,128)(2,1)S(1)}, bf16[1280,1536]{1,0:T(8,128)(2,1)S(1)}) custom-call(s32[1280,1]{1,0:T(8,128)S(1)} %copy-done.5, bf16[1280,384]{1,0:T(8,128)(2,1)S(1)} %convolution_convert_fusion.5.d_ref, f32[1280,768]{1,0:T(8,128)S(1)} %copy-done.3, bf16[768,1536]{1,0:T(8,128)(2,1)S(1)} %pad_maximum_fusion.1.w_ref), custom_call_target="tpu_custom_call" | custom-call | tf_op jit(solution)/shard_map/backward_rows/pallas_call | solution.py:77
  172.1 1.9 copy-done.4
  175.3 7.1 %all-to-all-start.3 = ((bf16[32,40,1536]{2,1,0:T(8,128)(2,1)}), bf16[32,40,1536]{2,1,0:T(8,128)(2,1)}, u32[]{:S(2)}, u32[]{:S(2)}) async-start(bf16[32,40,1536]{2,1,0:T(8,128)(2,1)} %bitcast.51), calls=%async_computation.4 | async-start | bytes 7864320 | tf_op jit(solution)/shard_map/all_to_all | solution.py:277
  182.8 48.8 %all-to-all-done.3 = bf16[32,40,1536]{2,1,0:T(8,128)(2,1)} async-done(((bf16[32,40,1536]{2,1,0:T(8,128)(2,1)}), bf16[32,40,1536]{2,1,0:T(8,128)(2,1)}, u32[]{:S(2)}, u32[]{:S(2)}) %all-to-all-start.3) | async-done | bytes 3932192 | tf_op jit(solution)/shard_map/all_to_all | solution.py:277
  231.6 8.2 %fusion.6 = bf16[1024,1536]{1,0:T(8,128)(2,1)} fusion(bf16[1280,1536]{1,0:T(8,128)(2,1)} %bitcast.19, s32[1024]{0:T(1024)S(1)} %bitcast.59, s32[1024]{0:T(1024)S(1)} %bitcast.58), kind=kOutput, calls=%fused_computation.11 | convolution fusion | flops 4032036864 | bytes 7086080 | tf_op jit(solution)/shard_map/dot_general | solution.py:10
  240.8 2.2 fusion.71
  243.7 5.4 %fusion.16 = bf16[1,1536,384]{2,1,0:T(8,128)(2,1)} fusion(bf16[1280,1536]{1,0:T(8,128)(2,1)} %bitcast.5.x_ref, bf16[1280,768]{1,0:T(8,128)(2,1)S(1)} %copy-done.10), kind=kOutput, calls=%fused_computation.23 | convolution fusion | flops 1510539264 | bytes 6094848 | tf_op jit(solution)/shard_map/dot_general | solution.py:20
  250.3 5.1 %collective-permute-done = bf16[160,1536]{1,0:T(8,128)(2,1)} collective-permute-done((bf16[160,1536]{1,0:T(8,128)(2,1)}, bf16[160,1536]{1,0:T(8,128)(2,1)}, u32[]{:S(2)}, u32[]{:S(2)}) %collective-permute-start) | collective-permute-done | bytes 491552 | tf_op jit(solution)/shard_map/ppermute | solution.py:178
  255.4 2.1 reshape.263
  259.4 1.7 copy.31
  261.1 10.1 %all-to-all-start.1 = ((bf16[32,10,1536]{2,1,0:T(8,128)(2,1)}), bf16[32,10,1536]{2,1,0:T(8,128)(2,1)}, u32[]{:S(2)}, u32[]{:S(2)}) async-start(bf16[32,10,1536]{2,1,0:T(8,128)(2,1)} %copy.31), calls=%async_computation.2 | async-start | bytes 3145728 | tf_op jit(solution)/shard_map/all_to_all | solution.py:295
  271.2 4.9 %fusion.17 = bf16[1,384,1536]{2,1,0:T(8,128)(2,1)} fusion(bf16[1280,384]{1,0:T(8,128)(2,1)S(1)} %copy-done.18, bf16[1280,1536]{1,0:T(8,128)(2,1)} %all-gather.5.cloned.1.call-done), kind=kOutput, calls=%fused_computation.24 | convolution fusion | flops 1510539264 | bytes 6094848 | tf_op jit(solution)/shard_map/dot_general | solution.py:20
  276.1 5.4 %fusion.15 = bf16[1,1536,384]{2,1,0:T(8,128)(2,1)} fusion(bf16[1280,1536]{1,0:T(8,128)(2,1)} %bitcast.5.x_ref, bf16[1280,768]{1,0:T(8,128)(2,1)S(1)} %copy-done.10), kind=kOutput, calls=%fused_computation.22 | convolution fusion | flops 1510539264 | bytes 6094848 | tf_op jit(solution)/shard_map/dot_general | solution.py:20
  281.6 12.4 %all-to-all-done.1 = bf16[32,10,1536]{2,1,0:T(8,128)(2,1)} async-done(((bf16[32,10,1536]{2,1,0:T(8,128)(2,1)}), bf16[32,10,1536]{2,1,0:T(8,128)(2,1)}, u32[]{:S(2)}, u32[]{:S(2)}) %all-to-all-start.1) | async-done | bytes 983072 | tf_op jit(solution)/shard_map/all_to_all | solution.py:295
  294.0 1.7 reshape.265
  (76 shorter events, 22.2 us)
Async XLA Ops:
  7.2 144.8 %copy-start = (bf16[1,384,1536]{2,1,0:T(8,128)(2,1)S(1)}, bf16[1,384,1536]{2,1,0:T(8,128)(2,1)}, u32[]{:S(2)}) copy-start(bf16[1,384,1536]{2,1,0:T(8,128)(2,1)} %param.12) | copy-start | bytes 3538948
  7.2 67.1 %all-gather.3.cloned.1.call-start = ((), (), s32[]{:S(2)}) async-start(), calls=%async_computation.6 | async-start | bytes 3981312 | tf_op jit(solution)/shard_map/all_gather | solution.py:235
  8.9 1.0 copy-start.6
  9.9 1.0 copy-start.8
  13.3 31.3 %all-to-all-start.2 = ((bf16[32,16,1536]{2,1,0:T(8,128)(2,1)}), bf16[32,16,1536]{2,1,0:T(8,128)(2,1)S(1)}, u32[]{:S(2)}, u32[]{:S(2)}) async-start(bf16[32,16,1536]{2,1,0:T(8,128)(2,1)} %bitcast.15), calls=%async_computation.3 | async-start | bytes 3145728 | tf_op jit(solution)/shard_map/all_to_all | solution.py:217
  21.9 138.5 %all-gather.5.cloned.1.call-start = ((), (), s32[]{:S(2)}) async-start(), calls=%async_computation.8 | async-start | bytes 4915200 | tf_op jit(solution)/shard_map/all_gather | solution.py:238
  47.0 23.5 %collective-permute-start.1 = (bf16[160,1536]{1,0:T(8,128)(2,1)S(1)}, bf16[160,1536]{1,0:T(8,128)(2,1)S(1)}, u32[]{:S(2)}, u32[]{:S(2)}) collective-permute-start(bf16[160,1536]{1,0:T(8,128)(2,1)S(1)} %select_n.192), channel_id=1, source_target_pairs={{0,2},{1,3},{2,0},{3,1},{4,6},{5,7},{6,4},{7,5},{8,10},{9,11},{10,... | collective-permute-start | bytes 1474568 | tf_op jit(solution)/shard_map/ppermute | solution.py:178
  75.0 0.6 copy-start.14
  84.6 9.4 %copy-start.13 = (bf16[1,1536,384]{2,1,0:T(8,128)(2,1)S(1)}, bf16[1,1536,384]{2,1,0:T(8,128)(2,1)}, u32[]{:S(2)}) copy-start(bf16[1,1536,384]{2,1,0:T(8,128)(2,1)} %param.10) | copy-start | bytes 3538948
  84.6 58.3 %all-to-all-start = ((bf16[32,40,1536]{2,1,0:T(8,128)(2,1)}), bf16[32,40,1536]{2,1,0:T(8,128)(2,1)}, u32[]{:S(2)}, u32[]{:S(2)}) async-start(bf16[32,40,1536]{2,1,0:T(8,128)(2,1)} %bitcast.56), calls=%async_computation | async-start | bytes 7864320 | tf_op jit(solution)/shard_map/all_to_all | solution.py:251
  93.8 147.0 %reduce-scatter.3.cloned.1.call-start = ((), (), s32[]{:S(2)}) async-start(), calls=%async_computation.7 | async-start | bytes 4915200 | tf_op jit(solution)/shard_map/reduce_scatter | solution.py:271
  94.7 2.0 copy-start.11
  96.7 1.0 copy-start.12
  148.7 2.3 copy-start.2
  151.0 1.0 copy-start.17
  160.5 4.5 %copy-start.3 = (f32[1280,768]{1,0:T(8,128)S(1)}, f32[1280,768]{1,0:T(8,128)}, u32[]{:S(2)}) copy-start(f32[1280,768]{1,0:T(8,128)} %copy-done.2) | copy-start | bytes 11796484
  160.5 4.5 %copy-start.5 = (s32[1280,1]{1,0:T(8,128)S(1)}, s32[1280,1]{1,0:T(8,128)}, u32[]{:S(2)}) copy-start(s32[1280,1]{1,0:T(8,128)} %fusion.32.place_ref) | copy-start | bytes 15364
  172.1 1.9 copy-start.4
  174.0 1.3 copy-start.9
  175.3 7.4 %copy-start.15 = (s32[8,4,128]{2,1,0:T(4,128)S(1)}, s32[8,4,128]{2,1,0:T(4,128)}, u32[]{:S(2)}) copy-start(s32[8,4,128]{2,1,0:T(4,128)} %copy-done.14) | copy-start | bytes 49156
  175.3 56.3 %all-to-all-start.3 = ((bf16[32,40,1536]{2,1,0:T(8,128)(2,1)}), bf16[32,40,1536]{2,1,0:T(8,128)(2,1)}, u32[]{:S(2)}, u32[]{:S(2)}) async-start(bf16[32,40,1536]{2,1,0:T(8,128)(2,1)} %bitcast.51), calls=%async_computation.4 | async-start | bytes 7864320 | tf_op jit(solution)/shard_map/all_to_all | solution.py:277
  182.4 115.6 %reduce-scatter.5.cloned.1.call-start = ((), (), s32[]{:S(2)}) async-start(), calls=%async_computation.9 | async-start | bytes 3538944 | tf_op jit(solution)/shard_map/reduce_scatter | solution.py:288
  239.8 0.7 copy-start.16
  239.8 3.9 %copy-start.10 = (bf16[1280,768]{1,0:T(8,128)(2,1)S(1)}, bf16[1280,768]{1,0:T(8,128)(2,1)}, u32[]{:S(2)}) copy-start(bf16[1280,768]{1,0:T(8,128)(2,1)} %copy-done.9) | copy-start | bytes 5898244
  243.0 12.4 %collective-permute-start = (bf16[160,1536]{1,0:T(8,128)(2,1)}, bf16[160,1536]{1,0:T(8,128)(2,1)}, u32[]{:S(2)}, u32[]{:S(2)}) collective-permute-start(bf16[160,1536]{1,0:T(8,128)(2,1)} %get-tuple-element.30), channel_id=1, source_target_pairs={{0,2},{1,3},{2,0},{3,1},{4,6},{5,7},{6,4},{7,5},{8,10},{9,11},{10,... | collective-permute-start | bytes 1474568 | tf_op jit(solution)/shard_map/ppermute | solution.py:178
  261.1 10.1 %copy-start.18 = (bf16[1280,384]{1,0:T(8,128)(2,1)S(1)}, bf16[1280,384]{1,0:T(8,128)(2,1)}, u32[]{:S(2)}) copy-start(bf16[1280,384]{1,0:T(8,128)(2,1)} %copy-done.17) | copy-start | bytes 2949124
  261.1 32.9 %all-to-all-start.1 = ((bf16[32,10,1536]{2,1,0:T(8,128)(2,1)}), bf16[32,10,1536]{2,1,0:T(8,128)(2,1)}, u32[]{:S(2)}, u32[]{:S(2)}) async-start(bf16[32,10,1536]{2,1,0:T(8,128)(2,1)} %copy.31), calls=%async_computation.2 | async-start | bytes 3145728 | tf_op jit(solution)/shard_map/all_to_all | solution.py:295
  281.6 14.5 %copy-start.7 = (bf16[128,1536]{1,0:T(8,128)(2,1)S(1)}, bf16[128,1536]{1,0:T(8,128)(2,1)}, u32[]{:S(2)}) copy-start(bf16[128,1536]{1,0:T(8,128)(2,1)} %cot_ref.1) | copy-start | bytes 1179652
  294.0 4.0 %copy-start.1 = (bf16[1,384,1536]{2,1,0:T(8,128)(2,1)S(1)}, bf16[1,384,1536]{2,1,0:T(8,128)(2,1)}, u32[]{:S(2)}) copy-start(bf16[1,384,1536]{2,1,0:T(8,128)(2,1)} %param.12) | copy-start | bytes 3538948
Sparse Core Ops, SparseCore 0:
  13.5 60.7 all-gather.2
  76.6 75.3 all-gather.4
  156.2 84.5 reduce-scatter.2
  243.8 42.6 reduce-scatter.4

commit v3 on v2

--- a/solution.py
+++ b/solution.py
@@ -94,6 +94,32 @@
         compiler_params=pltpu.CompilerParams(vmem_limit_bytes=24 << 20),
         name="backward_rows",
     )(places, d_hidden, pre, weights)
+
+
+def outward_kernel(place_ref, hidden_ref, w_ref, out_ref):
+    total = hidden_ref.shape[0]
+    places = jnp.broadcast_to(place_ref[...], (ROWS, total))
+    select = jnp.where(places == lax.broadcasted_iota(jnp.int32, (ROWS, total), 1), 1.0, 0.0)
+    hidden = dot_plain(select.astype(jnp.bfloat16), hidden_ref[...]).astype(jnp.bfloat16)
+    out_ref[...] = dot_plain(hidden, w_ref[...]).astype(jnp.bfloat16)
+
+
+def outward(places, hidden, weights):
+    total, part = hidden.shape
+    width = weights.shape[1]
+    return pl.pallas_call(
+        outward_kernel,
+        grid=(total // ROWS,),
+        in_specs=[
+            pl.BlockSpec((ROWS, 1), lambda i: (i, 0)),
+            pl.BlockSpec((total, part), lambda i: (0, 0), pipeline_mode=pl.Buffered(1)),
+            pl.BlockSpec((part, width), lambda i: (0, 0), pipeline_mode=pl.Buffered(1)),
+        ],
+        out_specs=pl.BlockSpec((ROWS, width), lambda i: (i, 0)),
+        out_shape=jax.ShapeDtypeStruct((total, width), jnp.bfloat16),
+        compiler_params=pltpu.CompilerParams(vmem_limit_bytes=24 << 20),
+        name="outward_rows",
+    )(places, hidden, weights)
 
 
 PADDED = 8
@@ -224,7 +250,6 @@
     )
     got = [got[:, k * PADDED : k * PADDED + capacity].reshape(slot_total // 2, width) for k in range(2)]
     kept, passed = jnp.where(pair == 0, got[0], got[1]), jnp.where(pair == 0, got[1], got[0])
-    got_cot = jnp.concatenate([kept, pair_swap(passed)], axis=0)
     cot = cotangent.astype(jnp.float32)
     target_row = (column_of(chosen[:2]) * 2 + (pair_of(chosen[:2]) != pair)) * capacity + chosen[2:]
     positions = jnp.arange(slot_total, dtype=jnp.int32)[:, None]
@@ -235,7 +260,23 @@
     ring = lax.all_gather(own, everyone, axis_index_groups=ring_groups, axis=0, tiled=True)
 
     half_rows = slot_total // 2
-    cot_rows = lax.all_gather(got_cot, "dp", axis=0, tiled=True)
+    far_rows = half_rows // 2
+    ring, kept, passed = lax.optimization_barrier((ring, kept, passed))
+    passed = pair_swap(passed)
+    cot_ahead, cot_behind = group_shift(kept, 1), group_shift(kept, -1)
+    cot_far_a = group_shift(cot_ahead[:far_rows], 1)
+    cot_far_b = group_shift(cot_behind[far_rows:], -1)
+    far = (group + 2) % groups * half_rows
+    cot_rows = join(
+        row_total // 2,
+        [
+            (group * half_rows, kept),
+            ((group - 1) % groups * half_rows, cot_ahead),
+            ((group + 1) % groups * half_rows, cot_behind),
+            (far, cot_far_a),
+            (far + far_rows, cot_far_b),
+        ],
+    )
 
     held = ring.reshape(planes, held_count, width)[:, count : count + 4, :count].astype(jnp.int32)
     block = jnp.arange(planes, dtype=jnp.int32)[:, None, None]
@@ -248,6 +289,7 @@
     row_ids = jnp.arange(row_total, dtype=jnp.int32)[:, None]
     select = ((row_ids == held_row[0]) | (row_ids == held_row[1])).astype(jnp.bfloat16)
     send_tokens = dot_plain(select, ring).astype(jnp.bfloat16)
+    send_tokens, passed = lax.optimization_barrier((send_tokens, passed))
     token_rows = lax.all_to_all(
         send_tokens.reshape(columns, planes * capacity, width),
         "expert",
@@ -257,20 +299,24 @@
         axis_index_groups=column_groups,
     ).reshape(row_total, width)
 
+    token_rows, cot_rows = lax.optimization_barrier((token_rows, cot_rows))
+    cot_rows = (cot_rows, lax.all_gather(passed, "dp", axis=0, tiled=True))
+
     ids = jnp.arange(row_total, dtype=jnp.int32)
     column, plane, slot = ids // (planes * capacity), ids // capacity % planes, ids % capacity
-    cot_place = (plane // 2 * 2 + (plane % 2 != pair)) * (slot_total // 2) + column * capacity + slot
-    to_token_order = (cot_place[:, None] == ids[None, :]).astype(jnp.bfloat16)
+    cot_place = ((plane % 2 != pair) * groups + plane // 2) * half_rows + column * capacity + slot
+    side = ids // half_rows % 2
+    out_plane = ids // slot_total * 2 + jnp.where(side == 1, 1 - pair, pair)
+    out_place = (ids % half_rows // capacity * planes + out_plane) * capacity + ids % capacity
 
     down_w = w_down[0]
     up_gate_w = jnp.concatenate([w_gate[0], w_up[0]], axis=1)
     up_gate_wt = jnp.concatenate([w_gate[0].T, w_up[0].T], axis=0)
     pre, hidden = forward(token_rows, up_gate_w)
-    hidden_cot = dot_first(to_token_order, hidden).astype(jnp.bfloat16)
-    part_out = dot_plain(hidden_cot, down_w).astype(jnp.bfloat16)
+    part_out = outward(out_place[:, None], hidden, down_w)
     expert_out = lax.psum_scatter(part_out, "dp", scatter_dimension=0, tiled=True)
 
-    d_hidden = dot_last(cot_rows, down_w).astype(jnp.bfloat16)
+    d_hidden = jnp.concatenate([dot_last(rows, down_w).astype(jnp.bfloat16) for rows in cot_rows], axis=0)
     d_hidden, _ = lax.optimization_barrier((d_hidden, part_out))
     d_both, back_rows = backward(cot_place[:, None], d_hidden, pre, up_gate_wt)
     d_gate, d_up = d_both[:, : down_w.shape[0]], d_both[:, down_w.shape[0] :]
@@ -309,7 +355,11 @@
 
     grad_gate = dot_first(token_rows, d_gate).astype(jnp.bfloat16)
     grad_up = dot_first(token_rows, d_up).astype(jnp.bfloat16)
-    grad_down = dot_first(hidden_cot, cot_rows).astype(jnp.bfloat16)
+    to_token_order = (cot_place[:, None] == ids[None, :]).astype(jnp.bfloat16)
+    hidden_cot = dot_first(to_token_order, hidden).astype(jnp.bfloat16)
+    grad_down = (
+        dot_first(hidden_cot[: row_total // 2], cot_rows[0]) + dot_first(hidden_cot[row_total // 2 :], cot_rows[1])
+    ).astype(jnp.bfloat16)
     return (out, d_tokens, d_combine, grad_gate[None], grad_up[None], grad_down[None])
 
 

time: 306 us -> 333 us (1.088)
  waiting for transfers between devices: 154 us -> 163 us
  starting transfers between devices: 38 us -> 46.5 us
  local copies, waits for them, and re-layouts: 26.6 us -> 34.3 us
  Pallas kernels: 15.3 us -> 21.1 us
  other arithmetic: 11 us -> 7.58 us
    ppermute x0 -> x4, waiting for transfers between devices: none -> 46.6 us  [group_shift(): lax.ppermute(x, 'dp', [(g, (g + step) % groups) for g in range(groups)])]
    all_to_all x1, waiting for transfers between devices: 40.7 us -> 0.01 us  [on_device(): lax.all_to_all(send_tokens.reshape(columns, planes * capacity, width), 'e...]
    all_gather x1, waiting for transfers between devices: 2.78 us -> 20.8 us  [on_device(): lax.all_gather(own, everyone, axis_index_groups=ring_groups, axis=0, tile...]
    ppermute x2, waiting for transfers between devices: 26.6 us -> 11.8 us  [pair_swap(): lax.ppermute(x, 'expert', [(e, e + 2 - pair_of(e) * 4) for e in range(exp...]
    dynamic_update_slice x0 -> x5, local copies, waits for them, and re-layouts: none -> 5.95 us  [join(): whole = lax.dynamic_update_slice_in_dim(whole, block, start, 0)]
    pallas_call x0 -> x1, Pallas kernels: none -> 5.65 us  [outward(): pl.pallas_call(outward_kernel, grid=(total // ROWS,), in_specs=[pl.BlockS...]
    ppermute x0 -> x4, starting transfers between devices: none -> 5.42 us  [group_shift(): lax.ppermute(x, 'dp', [(g, (g + step) % groups) for g in range(groups)])]
    unnamed x42 -> x50, local copies, waits for them, and re-layouts: 12.7 us -> 17.3 us
  transfers between devices with their start and end apart: 10 -> 14, of which waited for: 8 -> 8; matrix products, arithmetic and copies ran while one was open for 24% -> 21% of each run, Pallas kernels for 4% -> 6%
where the time goes in v3:
time: 333 us; the launch traced here: 332 us
  waiting for transfers between devices  163 us (49%)
  starting transfers between devices  46.5 us (14%)
  matrix products  44.6 us (13%)
  local copies, waits for them, and re-layouts  34.3 us (10%)
  Pallas kernels  21.1 us (6%)
  between operations  14.3 us (4%)
  other arithmetic  7.58 us (2%)
    all_to_all x1, waiting for transfers between devices, on_device(): lax.all_to_all(back_rows.reshape(columns, planes * capacity, width), 'exp...  49 us
    ppermute x4, waiting for transfers between devices, group_shift(): lax.ppermute(x, 'dp', [(g, (g + step) % groups) for g in range(groups)])  46.6 us
    all_to_all x1, waiting for transfers between devices, on_device(): lax.all_to_all(send_cot.reshape(columns, 2 * PADDED, width), 'expert', sp...  22.6 us
    dot_general x7, matrix products, dot_first(): lax.dot_general(left, right, (((0,), (0,)), ((), ())), preferred_element_...  21.6 us
    all_gather x1, waiting for transfers between devices, on_device(): lax.all_gather(own, everyone, axis_index_groups=ring_groups, axis=0, tile...  20.8 us
    unnamed x50, local copies, waits for them, and re-layouts  17.3 us
    dot_general x2, matrix products, dot_plain(): return jnp.dot(left, right, preferred_element_type=jnp.float32)  17 us
    ppermute x2, waiting for transfers between devices, pair_swap(): lax.ppermute(x, 'expert', [(e, e + 2 - pair_of(e) * 4) for e in range(exp...  11.8 us
  transfers between devices with their start and end apart: 14, of which 8 were waited for; matrix products, arithmetic and copies ran while one was open for 21% of the time, Pallas kernels for 6%

profile of v3, /device:TPU:1, one launch (start us, length us, event | category | flops | bytes accessed | tf_op | source)
XLA Modules:
  0.0 331.8 jit_solution(13928003949592981101)
XLA Ops:
  10.8 2.4 prepare_rows.1
  13.2 8.6 %all-to-all-start = ((bf16[32,16,1536]{2,1,0:T(8,128)(2,1)}), bf16[32,16,1536]{2,1,0:T(8,128)(2,1)S(1)}, u32[]{:S(2)}, u32[]{:S(2)}) async-start(bf16[32,16,1536]{2,1,0:T(8,128)(2,1)} %bitcast.2), calls=%async_computation | async-start | bytes 3145728 | tf_op jit(solution)/shard_map/all_to_all | solution.py:243
  21.9 22.6 %all-to-all-done = bf16[32,16,1536]{2,1,0:T(8,128)(2,1)S(1)} async-done(((bf16[32,16,1536]{2,1,0:T(8,128)(2,1)}), bf16[32,16,1536]{2,1,0:T(8,128)(2,1)S(1)}, u32[]{:S(2)}, u32[]{:S(2)}) %all-to-all-start) | async-done | bytes 1572896 | tf_op jit(solution)/shard_map/all_to_all | solution.py:243
  45.1 20.8 %all-gather.3.cloned.1.call-done = bf16[1152,1536]{1,0:T(8,128)(2,1)} async-done(((bf16[144,1536]{1,0:T(8,128)(2,1)}), bf16[1152,1536]{1,0:T(8,128)(2,1)}) %all-gather.3.cloned.1.call-update) | async-done | bytes 3538960 | tf_op jit(solution)/shard_map/all_gather | solution.py:260
  67.0 8.7 %convolution_convert_fusion = bf16[1280,1536]{1,0:T(8,128)(2,1)} fusion(bf16[1152,1536]{1,0:T(8,128)(2,1)} %all-gather.3.cloned.1.call-done, s32[1152]{0:T(1024)S(1)} %eq.156, s32[1152]{0:T(1024)S(1)} %eq.152), kind=kOutput, calls=%fused_computation | convolution fusion | flops 4536238080 | bytes 7480320 | tf_op jit(solution)/shard_map/dot_general | solution.py:10
  75.8 3.3 %collective-permute-done = bf16[160,1536]{1,0:T(8,128)(2,1)S(1)} collective-permute-done((bf16[160,1536]{1,0:T(8,128)(2,1)S(1)}, bf16[160,1536]{1,0:T(8,128)(2,1)S(1)}, u32[]{:S(2)}, u32[]{:S(2)}) %collective-permute-start) | collective-permute-done | bytes 491552 | tf_op jit(solution)/shard_map/ppermute | solution.py:204
  79.9 8.5 %all-to-all-start.1 = ((bf16[32,40,1536]{2,1,0:T(8,128)(2,1)}), bf16[32,40,1536]{2,1,0:T(8,128)(2,1)}, u32[]{:S(2)}, u32[]{:S(2)}) async-start(bf16[32,40,1536]{2,1,0:T(8,128)(2,1)} %bitcast.57), calls=%async_computation.1 | async-start | bytes 7864320 | tf_op jit(solution)/shard_map/all_to_all | solution.py:293
  89.9 2.0 copy.28
  93.2 2.0 collective-permute-start.2
  97.2 2.8 copy.29.w_ref
  102.3 30.9 %collective-permute-done.2 = bf16[160,1536]{1,0:T(8,128)(2,1)} collective-permute-done((bf16[160,1536]{1,0:T(8,128)(2,1)S(1)}, bf16[160,1536]{1,0:T(8,128)(2,1)}, u32[]{:S(2)}, u32[]{:S(2)}) %collective-permute-start.2) | collective-permute-done | bytes 491552 | tf_op jit(solution)/shard_map/ppermute | solution.py:199
  134.2 2.7 collective-permute-start.4
  138.1 1.9 constant_dynamic-update-slice_fusion.3
  141.8 15.8 %collective-permute-done.3 = bf16[80,1536]{1,0:T(8,128)(2,1)S(1)} collective-permute-done((bf16[80,1536]{1,0:T(8,128)(2,1)S(1)}, bf16[80,1536]{1,0:T(8,128)(2,1)S(1)}, u32[]{:S(2)}, u32[]{:S(2)}) %collective-permute-start.3) | collective-permute-done | bytes 245792 | tf_op jit(solution)/shard_map/ppermute | solution.py:199
  159.0 5.9 %forward_rows.1 = (f32[1280,768]{1,0:T(8,128)S(1)}, bf16[1280,384]{1,0:T(8,128)(2,1)S(1)}) custom-call(bf16[1280,1536]{1,0:T(8,128)(2,1)} %bitcast.6.x_ref, bf16[1536,768]{1,0:T(8,128)(2,1)S(1)} %copy.29.w_ref), custom_call_target="tpu_custom_call" | custom-call | tf_op jit(solution)/shard_map/forward_rows/pallas_call | solution.py:39
  166.8 5.6 %outward_rows.1 = bf16[1280,1536]{1,0:T(8,128)(2,1)S(1)} custom-call(s32[1280,1]{1,0:T(8,128)S(1)} %fusion.30.place_ref, bf16[1280,384]{1,0:T(8,128)(2,1)S(1)} %get-tuple-element.29.hidden_ref, bf16[384,1536]{1,0:T(8,128)(2,1)S(1)} %bitcast.52), custom_call_target="tpu_custom_call" | custom-call | tf_op jit(solution)/shard_map/outward_rows/pallas_call | solution.py:110
  172.5 1.9 copy-done
  179.3 3.1 convolution_convert_fusion.3
  182.4 2.9 convolution_convert_fusion.4
  185.4 7.1 %backward_rows.1 = (bf16[1280,768]{1,0:T(8,128)(2,1)S(1)}, bf16[1280,1536]{1,0:T(8,128)(2,1)S(1)}) custom-call(s32[1280,1]{1,0:T(8,128)S(1)} %fusion.27.place_ref, bf16[1280,384]{1,0:T(8,128)(2,1)S(1)} %pad_maximum_fusion.3.d_ref, f32[1280,768]{1,0:T(8,128)S(1)} %copy-done.2, bf16[768,1536]{1,0:T(8,128)(2,1)S(1)} %pad_maximum_fusion.1.w_ref), custom_call_target="tpu_custom_call" | custom-call | tf_op jit(solution)/shard_map/backward_rows/pallas_call | solution.py:77
  195.7 9.9 %all-to-all-start.3 = ((bf16[32,40,1536]{2,1,0:T(8,128)(2,1)}), bf16[32,40,1536]{2,1,0:T(8,128)(2,1)}, u32[]{:S(2)}, u32[]{:S(2)}) async-start(bf16[32,40,1536]{2,1,0:T(8,128)(2,1)} %bitcast.51), calls=%async_computation.4 | async-start | bytes 7864320 | tf_op jit(solution)/shard_map/all_to_all | solution.py:323
  205.7 49.0 %all-to-all-done.3 = bf16[32,40,1536]{2,1,0:T(8,128)(2,1)} async-done(((bf16[32,40,1536]{2,1,0:T(8,128)(2,1)}), bf16[32,40,1536]{2,1,0:T(8,128)(2,1)}, u32[]{:S(2)}, u32[]{:S(2)}) %all-to-all-start.3) | async-done | bytes 3932192 | tf_op jit(solution)/shard_map/all_to_all | solution.py:323
  254.7 8.2 %fusion.6 = bf16[1024,1536]{1,0:T(8,128)(2,1)} fusion(bf16[1280,1536]{1,0:T(8,128)(2,1)} %bitcast.19, s32[1024]{0:T(1024)S(1)} %bitcast.60, s32[1024]{0:T(1024)S(1)} %bitcast.59), kind=kOutput, calls=%fused_computation.10 | convolution fusion | flops 4032036864 | bytes 7086080 | tf_op jit(solution)/shard_map/dot_general | solution.py:10
  264.1 3.2 fusion.12
  268.7 3.9 %collective-permute-start.5 = (bf16[160,1536]{1,0:T(8,128)(2,1)S(1)}, bf16[160,1536]{1,0:T(8,128)(2,1)S(1)}, u32[]{:S(2)}, u32[]{:S(2)}) collective-permute-start(bf16[160,1536]{1,0:T(8,128)(2,1)S(1)} %get-tuple-element.44), channel_id=1, source_target_pairs={{0,2},{1,3},{2,0},{3,1},{4,6},{5,7},{6,4},{7,5},{8,10},{9,11},{10,... | collective-permute-start | bytes 1474568 | tf_op jit(solution)/shard_map/ppermute | solution.py:204
  272.7 2.1 fusion.54
  274.8 3.7 %fusion.16 = bf16[1,384,1536]{2,1,0:T(8,128)(2,1)} fusion(f32[384,1536]{1,0:T(8,128)S(1)} %fusion.54, bf16[640,1536]{1,0:T(8,128)(2,1)} %constant_dynamic-update-slice_fusion, bf16[1280,384]{1,0:T(8,128)(2,1)S(1)} %copy-done.19), kind=kOutput, calls=%fused_computation.21 | convolution fusion | flops 756154368 | bytes 5996544 | tf_op jit(solution)/shard_map/dot_general | solution.py:20
  278.7 8.5 %collective-permute-done.5 = bf16[160,1536]{1,0:T(8,128)(2,1)S(1)} collective-permute-done((bf16[160,1536]{1,0:T(8,128)(2,1)S(1)}, bf16[160,1536]{1,0:T(8,128)(2,1)S(1)}, u32[]{:S(2)}, u32[]{:S(2)}) %collective-permute-start.5) | collective-permute-done | bytes 491552 | tf_op jit(solution)/shard_map/ppermute | solution.py:204
  289.9 10.0 %all-to-all-start.2 = ((bf16[32,10,1536]{2,1,0:T(8,128)(2,1)}), bf16[32,10,1536]{2,1,0:T(8,128)(2,1)S(1)}, u32[]{:S(2)}, u32[]{:S(2)}) async-start(bf16[32,10,1536]{2,1,0:T(8,128)(2,1)} %copy.31), calls=%async_computation.3 | async-start | bytes 3145728 | tf_op jit(solution)/shard_map/all_to_all | solution.py:341
  299.9 5.4 %fusion.18 = bf16[1,1536,384]{2,1,0:T(8,128)(2,1)} fusion(bf16[1280,1536]{1,0:T(8,128)(2,1)} %bitcast.6.x_ref, bf16[1280,768]{1,0:T(8,128)(2,1)S(1)} %copy-done.12), kind=kOutput, calls=%fused_computation.23 | convolution fusion | flops 1510539264 | bytes 6094848 | tf_op jit(solution)/shard_map/dot_general | solution.py:20
  305.3 5.4 %fusion.17 = bf16[1,1536,384]{2,1,0:T(8,128)(2,1)} fusion(bf16[1280,1536]{1,0:T(8,128)(2,1)} %bitcast.6.x_ref, bf16[1280,768]{1,0:T(8,128)(2,1)S(1)} %copy-done.12), kind=kOutput, calls=%fused_computation.22 | convolution fusion | flops 1510539264 | bytes 6094848 | tf_op jit(solution)/shard_map/dot_general | solution.py:20
  310.7 11.8 %all-to-all-done.2 = bf16[32,10,1536]{2,1,0:T(8,128)(2,1)S(1)} async-done(((bf16[32,10,1536]{2,1,0:T(8,128)(2,1)}), bf16[32,10,1536]{2,1,0:T(8,128)(2,1)S(1)}, u32[]{:S(2)}, u32[]{:S(2)}) %all-to-all-start.2) | async-done | bytes 983072 | tf_op jit(solution)/shard_map/all_to_all | solution.py:341
  (103 shorter events, 36.8 us)
Async XLA Ops:
  7.2 58.7 %all-gather.3.cloned.1.call-start = ((), (), s32[]{:S(2)}) async-start(), calls=%async_computation.6 | async-start | bytes 3981312 | tf_op jit(solution)/shard_map/all_gather | solution.py:260
  13.2 31.3 %all-to-all-start = ((bf16[32,16,1536]{2,1,0:T(8,128)(2,1)}), bf16[32,16,1536]{2,1,0:T(8,128)(2,1)S(1)}, u32[]{:S(2)}, u32[]{:S(2)}) async-start(bf16[32,16,1536]{2,1,0:T(8,128)(2,1)} %bitcast.2), calls=%async_computation | async-start | bytes 3145728 | tf_op jit(solution)/shard_map/all_to_all | solution.py:243
  66.6 9.2 %copy-start.20 = (s32[8,4,128]{2,1,0:T(4,128)}, s32[8,4,128]{2,1,0:T(4,128)S(1)}, u32[]{:S(2)}) copy-start(s32[8,4,128]{2,1,0:T(4,128)S(1)} %slice_convert_fusion) | copy-start | bytes 49156
  66.9 12.2 %collective-permute-start = (bf16[160,1536]{1,0:T(8,128)(2,1)S(1)}, bf16[160,1536]{1,0:T(8,128)(2,1)S(1)}, u32[]{:S(2)}, u32[]{:S(2)}) collective-permute-start(bf16[160,1536]{1,0:T(8,128)(2,1)S(1)} %select_n.280), channel_id=1, source_target_pairs={{0,2},{1,3},{2,0},{3,1},{4,6},{5,7},{6,4},{7,5},{8,10},{9,11},{10,... | collective-permute-start | bytes 1474568 | tf_op jit(solution)/shard_map/ppermute | solution.py:204
  79.1 10.1 %copy-start.17 = (bf16[1,1536,384]{2,1,0:T(8,128)(2,1)S(1)}, bf16[1,1536,384]{2,1,0:T(8,128)(2,1)}, u32[]{:S(2)}) copy-start(bf16[1,1536,384]{2,1,0:T(8,128)(2,1)} %param.10) | copy-start | bytes 3538948
  79.9 79.1 %all-to-all-start.1 = ((bf16[32,40,1536]{2,1,0:T(8,128)(2,1)}), bf16[32,40,1536]{2,1,0:T(8,128)(2,1)}, u32[]{:S(2)}, u32[]{:S(2)}) async-start(bf16[32,40,1536]{2,1,0:T(8,128)(2,1)} %bitcast.57), calls=%async_computation.1 | async-start | bytes 7864320 | tf_op jit(solution)/shard_map/all_to_all | solution.py:293
  88.4 90.9 %all-gather.5.cloned.1.call-start = ((), (), s32[]{:S(2)}) async-start(), calls=%async_computation.8 | async-start | bytes 2457600 | tf_op jit(solution)/shard_map/all_gather | solution.py:303
  89.1 178.2 %reduce-scatter.3.cloned.1.call-start = ((), (), s32[]{:S(2)}) async-start(), calls=%async_computation.7 | async-start | bytes 4915200 | tf_op jit(solution)/shard_map/reduce_scatter | solution.py:317
  89.9 5.7 %copy-start.13 = (bf16[1,1536,384]{1,2,0:T(8,128)(2,1)}, bf16[1,1536,384]{1,2,0:T(8,128)(2,1)S(1)}, u32[]{:S(2)}) copy-start(bf16[1,1536,384]{1,2,0:T(8,128)(2,1)S(1)} %copy.27) | copy-start | bytes 3538948
  91.9 3.7 %copy-start.15 = (bf16[1,1536,384]{1,2,0:T(8,128)(2,1)}, bf16[1,1536,384]{1,2,0:T(8,128)(2,1)S(1)}, u32[]{:S(2)}) copy-start(bf16[1,1536,384]{1,2,0:T(8,128)(2,1)S(1)} %copy.28) | copy-start | bytes 3538948
  93.2 40.0 %collective-permute-start.2 = (bf16[160,1536]{1,0:T(8,128)(2,1)S(1)}, bf16[160,1536]{1,0:T(8,128)(2,1)}, u32[]{:S(2)}, u32[]{:S(2)}) collective-permute-start(bf16[160,1536]{1,0:T(8,128)(2,1)S(1)} %select_n.278), channel_id=1, source_target_pairs={{0,192},{64,0},{128,64},{192,128},{1,193},{65,1},{129,65},{193,129... | collective-permute-start | bytes 1474568 | tf_op jit(solution)/shard_map/ppermute | solution.py:199
  95.1 41.7 %collective-permute-start.1 = (bf16[160,1536]{1,0:T(8,128)(2,1)S(1)}, bf16[160,1536]{1,0:T(8,128)(2,1)}, u32[]{:S(2)}, u32[]{:S(2)}) collective-permute-start(bf16[160,1536]{1,0:T(8,128)(2,1)S(1)} %select_n.278), channel_id=1, source_target_pairs={{0,64},{64,128},{128,192},{192,0},{1,65},{65,129},{129,193},{193,1... | collective-permute-start | bytes 1474568 | tf_op jit(solution)/shard_map/ppermute | solution.py:199
  134.2 24.2 %collective-permute-start.4 = (bf16[80,1536]{1,0:T(8,128)(2,1)S(1)}, bf16[80,1536]{1,0:T(8,128)(2,1)S(1)}, u32[]{:S(2)}, u32[]{:S(2)}) collective-permute-start(bf16[80,1536]{1,0:T(8,128)(2,1)S(1)} %slice.105), channel_id=1, source_target_pairs={{0,192},{64,0},{128,64},{192,128},{1,193},{65,1},{129,65},{193,129... | collective-permute-start | bytes 737288 | tf_op jit(solution)/shard_map/ppermute | solution.py:199
  137.8 19.7 %collective-permute-start.3 = (bf16[80,1536]{1,0:T(8,128)(2,1)S(1)}, bf16[80,1536]{1,0:T(8,128)(2,1)S(1)}, u32[]{:S(2)}, u32[]{:S(2)}) collective-permute-start(bf16[80,1536]{1,0:T(8,128)(2,1)S(1)} %slice.104), channel_id=1, source_target_pairs={{0,64},{64,128},{128,192},{192,0},{1,65},{65,129},{129,193},{193,1... | collective-permute-start | bytes 737288 | tf_op jit(solution)/shard_map/ppermute | solution.py:199
  159.0 7.8 %copy-start.6 = (bf16[1,384,1536]{2,1,0:T(8,128)(2,1)S(1)}, bf16[1,384,1536]{2,1,0:T(8,128)(2,1)}, u32[]{:S(2)}) copy-start(bf16[1,384,1536]{2,1,0:T(8,128)(2,1)} %param.12) | copy-start | bytes 3538948
  164.9 1.9 copy-start.1
  172.5 1.9 copy-start
  175.3 1.3 copy-start.14
  179.2 3.2 copy-start.7
  182.4 3.0 copy-start.2
  192.5 1.9 copy-start.3
  194.4 1.3 copy-start.11
  195.7 9.9 %copy-start.21 = (s32[8,4,128]{2,1,0:T(4,128)S(1)}, s32[8,4,128]{2,1,0:T(4,128)}, u32[]{:S(2)}) copy-start(s32[8,4,128]{2,1,0:T(4,128)} %copy-done.20) | copy-start | bytes 49156
  195.7 59.0 %all-to-all-start.3 = ((bf16[32,40,1536]{2,1,0:T(8,128)(2,1)}), bf16[32,40,1536]{2,1,0:T(8,128)(2,1)}, u32[]{:S(2)}, u32[]{:S(2)}) async-start(bf16[32,40,1536]{2,1,0:T(8,128)(2,1)} %bitcast.51), calls=%async_computation.4 | async-start | bytes 7864320 | tf_op jit(solution)/shard_map/all_to_all | solution.py:323
  205.6 119.7 %reduce-scatter.5.cloned.1.call-start = ((), (), s32[]{:S(2)}) async-start(), calls=%async_computation.9 | async-start | bytes 3538944 | tf_op jit(solution)/shard_map/reduce_scatter | solution.py:334
  262.9 1.2 copy-start.9
  267.3 5.3 %copy-start.16 = (bf16[640,1536]{1,0:T(8,128)(2,1)S(1)}, bf16[640,1536]{1,0:T(8,128)(2,1)}, u32[]{:S(2)}) copy-start(bf16[640,1536]{1,0:T(8,128)(2,1)} %all-gather.5.cloned.1.call-done) | copy-start | bytes 5898244
  268.7 6.1 %copy-start.19 = (bf16[1280,384]{1,0:T(8,128)(2,1)S(1)}, bf16[1280,384]{1,0:T(8,128)(2,1)}, u32[]{:S(2)}) copy-start(bf16[1280,384]{1,0:T(8,128)(2,1)} %fusion.12) | copy-start | bytes 2949124
  268.7 18.5 %collective-permute-start.5 = (bf16[160,1536]{1,0:T(8,128)(2,1)S(1)}, bf16[160,1536]{1,0:T(8,128)(2,1)S(1)}, u32[]{:S(2)}, u32[]{:S(2)}) collective-permute-start(bf16[160,1536]{1,0:T(8,128)(2,1)S(1)} %get-tuple-element.44), channel_id=1, source_target_pairs={{0,2},{1,3},{2,0},{3,1},{4,6},{5,7},{6,4},{7,5},{8,10},{9,11},{10,... | collective-permute-start | bytes 1474568 | tf_op jit(solution)/shard_map/ppermute | solution.py:204
  289.9 10.0 %copy-start.12 = (bf16[1280,768]{1,0:T(8,128)(2,1)S(1)}, bf16[1280,768]{1,0:T(8,128)(2,1)}, u32[]{:S(2)}) copy-start(bf16[1280,768]{1,0:T(8,128)(2,1)} %copy-done.11) | copy-start | bytes 5898244
  289.9 32.7 %all-to-all-start.2 = ((bf16[32,10,1536]{2,1,0:T(8,128)(2,1)}), bf16[32,10,1536]{2,1,0:T(8,128)(2,1)S(1)}, u32[]{:S(2)}, u32[]{:S(2)}) async-start(bf16[32,10,1536]{2,1,0:T(8,128)(2,1)} %copy.31), calls=%async_computation.3 | async-start | bytes 3145728 | tf_op jit(solution)/shard_map/all_to_all | solution.py:341
  310.7 12.6 %copy-start.5 = (bf16[128,1536]{1,0:T(8,128)(2,1)S(1)}, bf16[128,1536]{1,0:T(8,128)(2,1)}, u32[]{:S(2)}) copy-start(bf16[128,1536]{1,0:T(8,128)(2,1)} %cot_ref.1) | copy-start | bytes 1179652
  (5 other events, 4.4 us)
Sparse Core Ops, SparseCore 0:
  13.3 52.4 all-gather.2
  91.0 69.8 all-gather.4
  175.5 86.0 reduce-scatter.2
  264.6 50.8 reduce-scatter.4

commit v4 on v2

--- a/solution.py
+++ b/solution.py
@@ -1,3 +1,4 @@
+import functools
 import jax
 import jax.numpy as jnp
 from jax import lax
@@ -48,7 +49,7 @@
             pl.BlockSpec((ROWS, both // 2), lambda i: (i, 0)),
         ],
         out_shape=[
-            jax.ShapeDtypeStruct((total, both), jnp.float32),
+            pltpu.HBM((total, both), jnp.float32),
             jax.ShapeDtypeStruct((total, both // 2), jnp.bfloat16),
         ],
         compiler_params=pltpu.CompilerParams(vmem_limit_bytes=24 << 20),
@@ -88,15 +89,72 @@
             pl.BlockSpec((ROWS, width), lambda i: (i, 0)),
         ],
         out_shape=[
-            jax.ShapeDtypeStruct((total, both), jnp.bfloat16),
-            jax.ShapeDtypeStruct((total, width), jnp.bfloat16),
+            pltpu.HBM((total, both), jnp.bfloat16),
+            pltpu.HBM((total, width), jnp.bfloat16),
         ],
         compiler_params=pltpu.CompilerParams(vmem_limit_bytes=24 << 20),
         name="backward_rows",
     )(places, d_hidden, pre, weights)
 
 
+def outward_kernel(place_ref, hidden_ref, w_ref, hidden_out_ref, out_ref):
+    total = hidden_ref.shape[0]
+    places = jnp.broadcast_to(place_ref[...], (ROWS, total))
+    select = jnp.where(places == lax.broadcasted_iota(jnp.int32, (ROWS, total), 1), 1.0, 0.0)
+    hidden = dot_plain(select.astype(jnp.bfloat16), hidden_ref[...]).astype(jnp.bfloat16)
+    hidden_out_ref[...] = hidden
+    out_ref[...] = dot_plain(hidden, w_ref[...]).astype(jnp.bfloat16)
+
+
+def outward(places, hidden, weights):
+    total, part = hidden.shape
+    width = weights.shape[1]
+    return pl.pallas_call(
+        outward_kernel,
+        grid=(total // ROWS,),
+        in_specs=[
+            pl.BlockSpec((ROWS, 1), lambda i: (i, 0)),
+            pl.BlockSpec((total, part), lambda i: (0, 0), pipeline_mode=pl.Buffered(1)),
+            pl.BlockSpec((part, width), lambda i: (0, 0), pipeline_mode=pl.Buffered(1)),
+        ],
+        out_specs=[
+            pl.BlockSpec((ROWS, part), lambda i: (i, 0)),
+            pl.BlockSpec((ROWS, width), lambda i: (i, 0)),
+        ],
+        out_shape=[
+            jax.ShapeDtypeStruct((total, part), jnp.bfloat16),
+            pltpu.HBM((total, width), jnp.bfloat16),
+        ],
+        compiler_params=pltpu.CompilerParams(vmem_limit_bytes=24 << 20),
+        name="outward_rows",
+    )(places, hidden, weights)
+
+
 PADDED = 8
+INFO = 8
+
+
+def spread_kernel(capacity, mine_ref, other_ref, out_ref):
+    half, total = other_ref.shape[0], out_ref.shape[0]
+    row, col = (lax.broadcasted_iota(jnp.int32, (total, half), axis) for axis in range(2))
+    slot = lax.bitwise_and(row, PADDED - 1)
+    source = lax.shift_right_logical(row, 4) * capacity + slot
+    side = lax.bitwise_and(lax.shift_right_logical(row, 3), 1)
+    found = (source == col) & (slot < capacity)
+    parts = [
+        dot_plain(jnp.where(found & (side == k), 1.0, 0.0).astype(jnp.bfloat16), rows)
+        for k, rows in enumerate((mine_ref[:half, :], other_ref[...]))
+    ]
+    out_ref[...] = (parts[0] + parts[1]).astype(jnp.bfloat16)
+
+
+def spread(mine, other, columns, capacity):
+    return pl.pallas_call(
+        functools.partial(spread_kernel, capacity),
+        out_shape=jax.ShapeDtypeStruct((columns * 2 * PADDED, mine.shape[1]), jnp.bfloat16),
+        compiler_params=pltpu.CompilerParams(vmem_limit_bytes=24 << 20),
+        name="spread_rows",
+    )(mine, other)
 
 
 def prepare_kernel(tokens_ref, routes_ref, combine_ref, cot_ref, own_ref, send_ref, chosen_ref):
@@ -116,7 +174,7 @@
     ]
     own_ref[:count, :] = tokens_ref[...]
     own_ref[count:, :] = jnp.zeros((own_ref.shape[0] - count, own_ref.shape[1]), jnp.bfloat16)
-    lines = [across[0][:1], across[1][:1], slots[0], slots[1], jnp.zeros((12, count), jnp.float32)]
+    lines = [across[0][:1], across[1][:1], slots[0], slots[1], jnp.zeros((INFO - 4, count), jnp.float32)]
     own_ref[count:, :count] = jnp.concatenate(lines, axis=0).astype(jnp.bfloat16)
     cot = cot_ref[...].astype(jnp.float32)
     total = None
@@ -140,7 +198,7 @@
     return pl.pallas_call(
         prepare_kernel,
         out_shape=[
-            jax.ShapeDtypeStruct((count + 16, width), jnp.bfloat16),
+            jax.ShapeDtypeStruct((count + INFO, width), jnp.bfloat16),
             jax.ShapeDtypeStruct((experts * PADDED, width), jnp.bfloat16),
             jax.ShapeDtypeStruct((4, count), jnp.int32),
         ],
@@ -226,12 +284,12 @@
     kept, passed = jnp.where(pair == 0, got[0], got[1]), jnp.where(pair == 0, got[1], got[0])
     got_cot = jnp.concatenate([kept, pair_swap(passed)], axis=0)
     cot = cotangent.astype(jnp.float32)
-    target_row = (column_of(chosen[:2]) * 2 + (pair_of(chosen[:2]) != pair)) * capacity + chosen[2:]
-    positions = jnp.arange(slot_total, dtype=jnp.int32)[:, None]
+    target_row = (column_of(chosen[:2]) * 2 + (pair_of(chosen[:2]) != pair)) * PADDED + chosen[2:]
+    positions = jnp.arange(columns * 2 * PADDED, dtype=jnp.int32)[:, None]
     pick_first = (positions == target_row[0:1]).astype(jnp.bfloat16)
     pick_second = (positions == target_row[1:2]).astype(jnp.bfloat16)
 
-    held_count = count + 16
+    held_count = count + INFO
     ring = lax.all_gather(own, everyone, axis_index_groups=ring_groups, axis=0, tiled=True)
 
     half_rows = slot_total // 2
@@ -260,14 +318,15 @@
     ids = jnp.arange(row_total, dtype=jnp.int32)
     column, plane, slot = ids // (planes * capacity), ids // capacity % planes, ids % capacity
     cot_place = (plane // 2 * 2 + (plane % 2 != pair)) * (slot_total // 2) + column * capacity + slot
-    to_token_order = (cot_place[:, None] == ids[None, :]).astype(jnp.bfloat16)
+    side = ids // half_rows % 2
+    out_plane = ids // slot_total * 2 + jnp.where(side == 1, 1 - pair, pair)
+    out_place = (ids % half_rows // capacity * planes + out_plane) * capacity + ids % capacity
 
     down_w = w_down[0]
     up_gate_w = jnp.concatenate([w_gate[0], w_up[0]], axis=1)
     up_gate_wt = jnp.concatenate([w_gate[0].T, w_up[0].T], axis=0)
     pre, hidden = forward(token_rows, up_gate_w)
-    hidden_cot = dot_first(to_token_order, hidden).astype(jnp.bfloat16)
-    part_out = dot_plain(hidden_cot, down_w).astype(jnp.bfloat16)
+    hidden_cot, part_out = outward(out_place[:, None], hidden, down_w)
     expert_out = lax.psum_scatter(part_out, "dp", scatter_dimension=0, tiled=True)
 
     d_hidden = dot_last(cot_rows, down_w).astype(jnp.bfloat16)
@@ -289,17 +348,14 @@
         d_ring, everyone, axis_index_groups=ring_groups, scatter_dimension=0, tiled=True
     )
 
-    half_rows = slot_total // 2
-    from_pair = [expert_out[:half_rows], pair_swap(expert_out[half_rows:])]
-    from_pair = [rows.reshape(columns, 1, capacity, width) for rows in from_pair]
     returned = lax.all_to_all(
-        jnp.concatenate(from_pair, axis=1).reshape(columns, 2 * capacity, width),
+        spread(expert_out, pair_swap(expert_out[half_rows:]), columns, capacity).reshape(columns, 2 * PADDED, width),
         "expert",
         split_axis=0,
         concat_axis=0,
         tiled=True,
         axis_index_groups=column_groups,
-    ).reshape(slot_total, width)
+    ).reshape(columns * 2 * PADDED, width)
     first_out = dot_first(pick_first, returned)
     second_out = dot_first(pick_second, returned)
     out = (combine[:, 0:1] * first_out + combine[:, 1:2] * second_out).astype(jnp.bfloat16)

time: 306 us -> 297 us (0.971)
  local copies, waits for them, and re-layouts: 26.6 us -> 14.9 us
  Pallas kernels: 15.3 us -> 26.3 us
  matrix products: 45.2 us -> 39.4 us
    pallas_call x1 -> x3, Pallas kernels: 2.44 us -> 11.1 us  [the longest x1 6.47 us: outward(): pl.pallas_call(outward_kernel, grid=(total // ROWS,), in_specs=[pl.BlockS...]
    ppermute x2, waiting for transfers between devices: 26.6 us -> 33.7 us  [pair_swap(): lax.ppermute(x, 'expert', [(e, e + 2 - pair_of(e) * 4) for e in range(exp...]
    reshape x4 -> x0, local copies, waits for them, and re-layouts: 6.72 us -> none  [the longest x2 3.32 us: on_device(): rows.reshape(columns, 1, capacity, width)]
    all_to_all x1, waiting for transfers between devices: 12.4 us -> 6.76 us  [on_device(): lax.all_to_all(spread(expert_out, pair_swap(expert_out[half_rows:]), colu...]
    all_to_all x1, waiting for transfers between devices: 40.7 us -> 35.6 us  [on_device(): lax.all_to_all(send_tokens.reshape(columns, planes * capacity, width), 'e...]
    reduce_scatter x1, waiting for transfers between devices: 0.28 us -> 5.09 us  [on_device(): lax.psum_scatter(part_out, 'dp', scatter_dimension=0, tiled=True)]
    dot_general x3 -> x2, matrix products: 21 us -> 17 us  [dot_plain(): return jnp.dot(left, right, preferred_element_type=jnp.float32)]
    unnamed x42 -> x30, local copies, waits for them, and re-layouts: 12.7 us -> 9.22 us
  transfers between devices with their start and end apart: 10 -> 10, of which waited for: 8 -> 8; matrix products, arithmetic and copies ran while one was open for 24% -> 21% of each run, Pallas kernels for 4% -> 8%
where the time goes in v4:
time: 297 us; the launch traced here: 296 us
  waiting for transfers between devices  153 us (52%)
  matrix products  39.4 us (13%)
  starting transfers between devices  35.3 us (12%)
  Pallas kernels  26.3 us (9%)
  local copies, waits for them, and re-layouts  14.9 us (5%)
  between operations  14 us (5%)
  other arithmetic  12.2 us (4%)
    all_to_all x1, waiting for transfers between devices, on_device(): lax.all_to_all(back_rows.reshape(columns, planes * capacity, width), 'exp...  49 us
    all_to_all x1, waiting for transfers between devices, on_device(): lax.all_to_all(send_tokens.reshape(columns, planes * capacity, width), 'e...  35.6 us
    ppermute x2, waiting for transfers between devices, pair_swap(): lax.ppermute(x, 'expert', [(e, e + 2 - pair_of(e) * 4) for e in range(exp...  33.7 us
    all_to_all x1, waiting for transfers between devices, on_device(): lax.all_to_all(send_cot.reshape(columns, 2 * PADDED, width), 'expert', sp...  22.6 us
    dot_general x5, matrix products, dot_first(): lax.dot_general(left, right, (((0,), (0,)), ((), ())), preferred_element_...  17.6 us
    dot_general x2, matrix products, dot_plain(): return jnp.dot(left, right, preferred_element_type=jnp.float32)  17 us
    unnamed x30, local copies, waits for them, and re-layouts  9.22 us
    all_to_all x1, starting transfers between devices, on_device(): lax.all_to_all(send_tokens.reshape(columns, planes * capacity, width), 'e...  9.02 us
  transfers between devices with their start and end apart: 10, of which 8 were waited for; matrix products, arithmetic and copies ran while one was open for 21% of the time, Pallas kernels for 8%

profile of v4, /device:TPU:1, one launch (start us, length us, event | category | flops | bytes accessed | tf_op | source)
XLA Modules:
  0.0 295.5 jit_solution(4820969780487646)
XLA Ops:
  10.8 2.4 prepare_rows.1
  13.2 8.6 %all-to-all-start.2 = ((bf16[32,16,1536]{2,1,0:T(8,128)(2,1)}), bf16[32,16,1536]{2,1,0:T(8,128)(2,1)S(1)}, u32[]{:S(2)}, u32[]{:S(2)}) async-start(bf16[32,16,1536]{2,1,0:T(8,128)(2,1)} %bitcast.16), calls=%async_computation.3 | async-start | bytes 3145728 | tf_op jit(solution)/shard_map/all_to_all | solution.py:275
  21.9 22.6 %all-to-all-done.2 = bf16[32,16,1536]{2,1,0:T(8,128)(2,1)S(1)} async-done(((bf16[32,16,1536]{2,1,0:T(8,128)(2,1)}), bf16[32,16,1536]{2,1,0:T(8,128)(2,1)S(1)}, u32[]{:S(2)}, u32[]{:S(2)}) %all-to-all-start.2) | async-done | bytes 1572896 | tf_op jit(solution)/shard_map/all_to_all | solution.py:275
  45.5 1.3 select_n.241
  46.8 1.7 collective-permute-start.1
  48.8 21.6 %collective-permute-done.1 = bf16[160,1536]{1,0:T(8,128)(2,1)S(1)} collective-permute-done((bf16[160,1536]{1,0:T(8,128)(2,1)S(1)}, bf16[160,1536]{1,0:T(8,128)(2,1)S(1)}, u32[]{:S(2)}, u32[]{:S(2)}) %collective-permute-start.1) | collective-permute-done | bytes 491552 | tf_op jit(solution)/shard_map/ppermute | solution.py:236
  73.0 8.7 %convolution_convert_fusion = bf16[1280,1536]{1,0:T(8,128)(2,1)} fusion(bf16[1088,1536]{1,0:T(8,128)(2,1)} %all-gather.3.cloned.1.call-done, s32[1088]{0:T(1024)S(1)} %eq.139, s32[1088]{0:T(1024)S(1)} %eq.135), kind=kOutput, calls=%fused_computation | convolution fusion | flops 4284334080 | bytes 7283200 | tf_op jit(solution)/shard_map/dot_general | solution.py:11
  81.7 9.0 %all-to-all-start = ((bf16[32,40,1536]{2,1,0:T(8,128)(2,1)}), bf16[32,40,1536]{2,1,0:T(8,128)(2,1)}, u32[]{:S(2)}, u32[]{:S(2)}) async-start(bf16[32,40,1536]{2,1,0:T(8,128)(2,1)} %bitcast.53), calls=%async_computation | async-start | bytes 7864320 | tf_op jit(solution)/shard_map/all_to_all | solution.py:309
  91.6 2.8 copy.21
  94.4 2.9 pad_maximum_fusion
  97.3 2.8 copy.22.w_ref
  100.1 4.1 %fusion.23 = (s32[1280,1]{1,0:T(8,128)}, s32[1280,1]{1,0:T(8,128)S(1)}) fusion(s32[]{:T(128)S(6)} %select_n.219, s32[]{:T(128)S(6)} %sub.62), kind=kLoop, calls=%fused_computation.59 | loop fusion | flops 126720 | bytes 10248 | tf_op jit(solution)/shard_map/add | solution.py:320
  104.2 35.6 %all-to-all-done = bf16[32,40,1536]{2,1,0:T(8,128)(2,1)} async-done(((bf16[32,40,1536]{2,1,0:T(8,128)(2,1)}), bf16[32,40,1536]{2,1,0:T(8,128)(2,1)}, u32[]{:S(2)}, u32[]{:S(2)}) %all-to-all-start) | async-done | bytes 3932192 | tf_op jit(solution)/shard_map/all_to_all | solution.py:309
  139.8 7.3 %forward_rows.1 = (f32[1280,768]{1,0:T(8,128)}, bf16[1280,384]{1,0:T(8,128)(2,1)S(1)}) custom-call(bf16[1280,1536]{1,0:T(8,128)(2,1)} %bitcast.5.x_ref, bf16[1536,768]{1,0:T(8,128)(2,1)S(1)} %copy.22.w_ref), custom_call_target="tpu_custom_call" | custom-call | tf_op jit(solution)/shard_map/forward_rows/pallas_call | solution.py:40
  147.2 6.5 %outward_rows.1 = (bf16[1280,384]{1,0:T(8,128)(2,1)S(1)}, bf16[1280,1536]{1,0:T(8,128)(2,1)}) custom-call(s32[1280,1]{1,0:T(8,128)S(1)} %get-tuple-element.40.place_ref, bf16[1280,384]{1,0:T(8,128)(2,1)S(1)} %get-tuple-element.18.hidden_ref, bf16[384,1536]{1,0:T(8,128)(2,1)S(1)} %bitcast.48), custom_call_target="tpu_custom_call" | custom-call | tf_op jit(solution)/shard_map/outward_rows/pallas_call | solution.py:112
  154.6 1.8 pad_maximum_fusion.1.w_ref
  156.5 4.8 %convolution_convert_fusion.4.d_ref = bf16[1280,384]{1,0:T(8,128)(2,1)S(1)} fusion(bf16[1280,1536]{1,0:T(8,128)(2,1)} %all-gather.5.cloned.1.call-done, bf16[1,384,1536]{2,1,0:T(8,128)(2,1)} %param.12), kind=kOutput, calls=%fused_computation.14 | convolution fusion | flops 1510440960 | bytes 6094848 | tf_op jit(solution)/shard_map/dot_general | solution.py:15
  161.3 7.9 %backward_rows.1 = (bf16[1280,768]{1,0:T(8,128)(2,1)}, bf16[1280,1536]{1,0:T(8,128)(2,1)}) custom-call(s32[1280,1]{1,0:T(8,128)S(1)} %copy-done.1, bf16[1280,384]{1,0:T(8,128)(2,1)S(1)} %convolution_convert_fusion.4.d_ref, f32[1280,768]{1,0:T(8,128)S(1)} %copy-done, bf16[768,1536]{1,0:T(8,128)(2,1)S(1)} %pad_maximum_fusion.1.w_ref), custom_call_target="tpu_custom_call" | custom-call | tf_op jit(solution)/shard_map/backward_rows/pallas_call | solution.py:78
  169.2 7.0 %all-to-all-start.3 = ((bf16[32,40,1536]{2,1,0:T(8,128)(2,1)}), bf16[32,40,1536]{2,1,0:T(8,128)(2,1)}, u32[]{:S(2)}, u32[]{:S(2)}) async-start(bf16[32,40,1536]{2,1,0:T(8,128)(2,1)} %bitcast.54), calls=%async_computation.4 | async-start | bytes 7864320 | tf_op jit(solution)/shard_map/all_to_all | solution.py:336
  176.4 49.0 %all-to-all-done.3 = bf16[32,40,1536]{2,1,0:T(8,128)(2,1)} async-done(((bf16[32,40,1536]{2,1,0:T(8,128)(2,1)}), bf16[32,40,1536]{2,1,0:T(8,128)(2,1)}, u32[]{:S(2)}, u32[]{:S(2)}) %all-to-all-start.3) | async-done | bytes 3932192 | tf_op jit(solution)/shard_map/all_to_all | solution.py:336
  225.4 8.3 %fusion.5 = bf16[1024,1536]{1,0:T(8,128)(2,1)} fusion(bf16[1280,1536]{1,0:T(8,128)(2,1)} %bitcast.20, s32[1024]{0:T(1024)S(1)} %bitcast.56, s32[1024]{0:T(1024)S(1)} %bitcast.55), kind=kOutput, calls=%fused_computation.8 | convolution fusion | flops 4032036864 | bytes 7086080 | tf_op jit(solution)/shard_map/dot_general | solution.py:11
  233.7 5.1 %reduce-scatter.3.cloned.1.call-done.mine_ref = bf16[320,1536]{1,0:T(8,128)(2,1)} async-done(((bf16[1280,1536]{1,0:T(8,128)(2,1)}), bf16[320,1536]{1,0:T(8,128)(2,1)}) %reduce-scatter.3.cloned.1.call-update) | async-done | bytes 983056 | tf_op jit(solution)/shard_map/reduce_scatter | solution.py:330
  238.8 1.1 slice.82
  240.0 12.1 %collective-permute-done.other_ref = bf16[160,1536]{1,0:T(8,128)(2,1)S(1)} collective-permute-done((bf16[160,1536]{1,0:T(8,128)(2,1)S(1)}, bf16[160,1536]{1,0:T(8,128)(2,1)S(1)}, u32[]{:S(2)}, u32[]{:S(2)}) %collective-permute-start) | collective-permute-done | bytes 491552 | tf_op jit(solution)/shard_map/ppermute | solution.py:236
  252.1 1.2 copy-done.2
  253.3 2.2 spread_rows.1
  255.5 8.4 %all-to-all-start.1 = ((bf16[32,16,1536]{2,1,0:T(8,128)(2,1)}), bf16[32,16,1536]{2,1,0:T(8,128)(2,1)S(1)}, u32[]{:S(2)}, u32[]{:S(2)}) async-start(bf16[32,16,1536]{2,1,0:T(8,128)(2,1)} %bitcast.9), calls=%async_computation.2 | async-start | bytes 3145728 | tf_op jit(solution)/shard_map/all_to_all | solution.py:351
  264.0 5.0 %fusion.14 = bf16[1,384,1536]{2,1,0:T(8,128)(2,1)} fusion(bf16[1280,384]{1,0:T(8,128)(2,1)S(1)} %copy-done.8, bf16[1280,1536]{1,0:T(8,128)(2,1)} %all-gather.5.cloned.1.call-done), kind=kOutput, calls=%fused_computation.19 | convolution fusion | flops 1510539264 | bytes 6094848 | tf_op jit(solution)/shard_map/dot_general | solution.py:21
  269.1 5.4 %fusion.13 = bf16[1,1536,384]{2,1,0:T(8,128)(2,1)} fusion(bf16[1280,1536]{1,0:T(8,128)(2,1)} %bitcast.5.x_ref, bf16[1280,768]{1,0:T(8,128)(2,1)S(1)} %copy-done.12), kind=kOutput, calls=%fused_computation.18 | convolution fusion | flops 1510539264 | bytes 6094848 | tf_op jit(solution)/shard_map/dot_general | solution.py:21
  274.5 5.4 %fusion.12 = bf16[1,1536,384]{2,1,0:T(8,128)(2,1)} fusion(bf16[1280,1536]{1,0:T(8,128)(2,1)} %bitcast.5.x_ref, bf16[1280,768]{1,0:T(8,128)(2,1)S(1)} %copy-done.12), kind=kOutput, calls=%fused_computation.17 | convolution fusion | flops 1510539264 | bytes 6094848 | tf_op jit(solution)/shard_map/dot_general | solution.py:21
  279.9 6.8 %all-to-all-done.1 = bf16[32,16,1536]{2,1,0:T(8,128)(2,1)S(1)} async-done(((bf16[32,16,1536]{2,1,0:T(8,128)(2,1)}), bf16[32,16,1536]{2,1,0:T(8,128)(2,1)S(1)}, u32[]{:S(2)}, u32[]{:S(2)}) %all-to-all-start.1) | async-done | bytes 1572896 | tf_op jit(solution)/shard_map/all_to_all | solution.py:351
  287.1 1.4 fusion.17
  (57 shorter events, 10.6 us)
Async XLA Ops:
  7.2 64.8 %all-gather.3.cloned.1.call-start = ((), (), s32[]{:S(2)}) async-start(), calls=%async_computation.6 | async-start | bytes 3760128 | tf_op jit(solution)/shard_map/all_gather | solution.py:293
  8.8 1.0 copy-start.3
  9.8 1.0 copy-start.6
  13.2 31.3 %all-to-all-start.2 = ((bf16[32,16,1536]{2,1,0:T(8,128)(2,1)}), bf16[32,16,1536]{2,1,0:T(8,128)(2,1)S(1)}, u32[]{:S(2)}, u32[]{:S(2)}) async-start(bf16[32,16,1536]{2,1,0:T(8,128)(2,1)} %bitcast.16), calls=%async_computation.3 | async-start | bytes 3145728 | tf_op jit(solution)/shard_map/all_to_all | solution.py:275
  21.8 134.6 %all-gather.5.cloned.1.call-start = ((), (), s32[]{:S(2)}) async-start(), calls=%async_computation.8 | async-start | bytes 4915200 | tf_op jit(solution)/shard_map/all_gather | solution.py:296
  46.8 23.6 %collective-permute-start.1 = (bf16[160,1536]{1,0:T(8,128)(2,1)S(1)}, bf16[160,1536]{1,0:T(8,128)(2,1)S(1)}, u32[]{:S(2)}, u32[]{:S(2)}) collective-permute-start(bf16[160,1536]{1,0:T(8,128)(2,1)S(1)} %select_n.241), channel_id=1, source_target_pairs={{0,2},{1,3},{2,0},{3,1},{4,6},{5,7},{6,4},{7,5},{8,10},{9,11},{10,... | collective-permute-start | bytes 1474568 | tf_op jit(solution)/shard_map/ppermute | solution.py:236
  81.7 9.3 %copy-start.10 = (bf16[1,1536,384]{2,1,0:T(8,128)(2,1)S(1)}, bf16[1,1536,384]{2,1,0:T(8,128)(2,1)}, u32[]{:S(2)}) copy-start(bf16[1,1536,384]{2,1,0:T(8,128)(2,1)} %param.10) | copy-start | bytes 3538948
  81.7 58.2 %all-to-all-start = ((bf16[32,40,1536]{2,1,0:T(8,128)(2,1)}), bf16[32,40,1536]{2,1,0:T(8,128)(2,1)}, u32[]{:S(2)}, u32[]{:S(2)}) async-start(bf16[32,40,1536]{2,1,0:T(8,128)(2,1)} %bitcast.53), calls=%async_computation | async-start | bytes 7864320 | tf_op jit(solution)/shard_map/all_to_all | solution.py:309
  90.7 148.1 %reduce-scatter.3.cloned.1.call-start = ((), (), s32[]{:S(2)}) async-start(), calls=%async_computation.7 | async-start | bytes 4915200 | tf_op jit(solution)/shard_map/reduce_scatter | solution.py:330
  91.6 2.8 copy-start.9
  139.8 7.3 %copy-start.5 = (bf16[1,384,1536]{2,1,0:T(8,128)(2,1)S(1)}, bf16[1,384,1536]{2,1,0:T(8,128)(2,1)}, u32[]{:S(2)}) copy-start(bf16[1,384,1536]{2,1,0:T(8,128)(2,1)} %param.12) | copy-start | bytes 3538948
  153.6 1.0 copy-start.7
  156.4 4.9 %copy-start.1 = (s32[1280,1]{1,0:T(8,128)S(1)}, s32[1280,1]{1,0:T(8,128)}, u32[]{:S(2)}) copy-start(s32[1280,1]{1,0:T(8,128)} %get-tuple-element.39.place_ref) | copy-start | bytes 15364
  156.4 4.9 %copy-start = (f32[1280,768]{1,0:T(8,128)S(1)}, f32[1280,768]{1,0:T(8,128)}, u32[]{:S(2)}) copy-start(f32[1280,768]{1,0:T(8,128)} %get-tuple-element.22.pre_ref) | copy-start | bytes 11796484
  169.2 56.2 %all-to-all-start.3 = ((bf16[32,40,1536]{2,1,0:T(8,128)(2,1)}), bf16[32,40,1536]{2,1,0:T(8,128)(2,1)}, u32[]{:S(2)}, u32[]{:S(2)}) async-start(bf16[32,40,1536]{2,1,0:T(8,128)(2,1)} %bitcast.54), calls=%async_computation.4 | async-start | bytes 7864320 | tf_op jit(solution)/shard_map/all_to_all | solution.py:336
  176.3 112.8 %reduce-scatter.5.cloned.1.call-start = ((), (), s32[]{:S(2)}) async-start(), calls=%async_computation.9 | async-start | bytes 3538944 | tf_op jit(solution)/shard_map/reduce_scatter | solution.py:347
  233.7 6.3 %copy-start.11 = (f32[128,2]{0,1:T(2,128)S(1)}, f32[128,2]{0,1:T(2,128)}, u32[]{:S(2)}) copy-start(f32[128,2]{0,1:T(2,128)} %param.9) | copy-start | bytes 3076
  239.9 12.2 %collective-permute-start = (bf16[160,1536]{1,0:T(8,128)(2,1)S(1)}, bf16[160,1536]{1,0:T(8,128)(2,1)S(1)}, u32[]{:S(2)}, u32[]{:S(2)}) collective-permute-start(bf16[160,1536]{1,0:T(8,128)(2,1)S(1)} %slice.82), channel_id=1, source_target_pairs={{0,2},{1,3},{2,0},{3,1},{4,6},{5,7},{6,4},{7,5},{8,10},{9,11},{10,... | collective-permute-start | bytes 1474568 | tf_op jit(solution)/shard_map/ppermute | solution.py:236
  252.1 1.2 copy-start.2
  253.3 10.7 %copy-start.8 = (bf16[1280,384]{1,0:T(8,128)(2,1)S(1)}, bf16[1280,384]{1,0:T(8,128)(2,1)}, u32[]{:S(2)}) copy-start(bf16[1280,384]{1,0:T(8,128)(2,1)} %copy-done.7) | copy-start | bytes 2949124
  255.5 31.1 %all-to-all-start.1 = ((bf16[32,16,1536]{2,1,0:T(8,128)(2,1)}), bf16[32,16,1536]{2,1,0:T(8,128)(2,1)S(1)}, u32[]{:S(2)}, u32[]{:S(2)}) async-start(bf16[32,16,1536]{2,1,0:T(8,128)(2,1)} %bitcast.9), calls=%async_computation.2 | async-start | bytes 3145728 | tf_op jit(solution)/shard_map/all_to_all | solution.py:351
  264.0 5.1 %copy-start.12 = (bf16[1280,768]{1,0:T(8,128)(2,1)S(1)}, bf16[1280,768]{1,0:T(8,128)(2,1)}, u32[]{:S(2)}) copy-start(bf16[1280,768]{1,0:T(8,128)(2,1)} %get-tuple-element.24) | copy-start | bytes 5898244
  279.9 7.2 %copy-start.4 = (bf16[128,1536]{1,0:T(8,128)(2,1)S(1)}, bf16[128,1536]{1,0:T(8,128)(2,1)}, u32[]{:S(2)}) copy-start(bf16[128,1536]{1,0:T(8,128)(2,1)} %cot_ref.1) | copy-start | bytes 1179652
Sparse Core Ops, SparseCore 0:
  13.3 58.5 all-gather.2
  74.3 75.7 all-gather.4
  153.8 84.9 reduce-scatter.2
  241.8 42.6 reduce-scatter.4

commit v5 on v4

--- a/solution.py
+++ b/solution.py
@@ -24,6 +24,29 @@
 
 
 ROWS = 256
+
+
+def select_kernel(code_ref, x_ref, out_ref):
+    row = pl.program_id(0) * ROWS + lax.broadcasted_iota(jnp.int32, (ROWS, x_ref.shape[0]), 0)
+    found = (row == code_ref[:1]) | (row == code_ref[1:])
+    select = jnp.where(found, 1.0, 0.0).astype(jnp.bfloat16)
+    out_ref[...] = dot_plain(select, x_ref[...]).astype(jnp.bfloat16)
+
+
+def select_rows(codes, x, total):
+    held, width = x.shape
+    return pl.pallas_call(
+        select_kernel,
+        grid=(total // ROWS,),
+        in_specs=[
+            pl.BlockSpec((2, held), lambda i: (0, 0), pipeline_mode=pl.Buffered(1)),
+            pl.BlockSpec((held, width), lambda i: (0, 0), pipeline_mode=pl.Buffered(1)),
+        ],
+        out_specs=pl.BlockSpec((ROWS, width), lambda i: (i, 0)),
+        out_shape=pltpu.HBM((total, width), jnp.bfloat16),
+        compiler_params=pltpu.CompilerParams(vmem_limit_bytes=24 << 20),
+        name="select_rows",
+    )(codes, x)
 
 
 def forward_kernel(x_ref, w_ref, pre_ref, hidden_ref):
@@ -162,8 +185,8 @@
     square = (count, count)
     row, col = lax.broadcasted_iota(jnp.int32, square, 0), lax.broadcasted_iota(jnp.int32, square, 1)
     chosen = routes_ref[...].astype(jnp.float32)
-    down = [jnp.broadcast_to(chosen[:, k : k + 1], square) for k in range(2)]
-    across = [expert.T for expert in down]
+    across = [jnp.broadcast_to(chosen[k : k + 1], square) for k in range(2)]
+    down = [expert.T for expert in across]
     slots = [
         jnp.sum(
             jnp.where((row < col) & ((down[0] == expert) | (down[1] == expert)), 1.0, 0.0),
@@ -187,7 +210,8 @@
         places = ((quarter * 2 + last) * 2 + pair) * PADDED + slot
         places = jnp.broadcast_to(places, (send_ref.shape[0], count))
         pick = jnp.where(lax.broadcasted_iota(jnp.int32, places.shape, 0) == places, 1.0, 0.0)
-        weighted = (combine_ref[:, k : k + 1] * cot).astype(jnp.bfloat16)
+        weight = jnp.broadcast_to(combine_ref[k : k + 1], square).T[:, :1]
+        weighted = (weight * cot).astype(jnp.bfloat16)
         part = dot_plain(pick.astype(jnp.bfloat16), weighted)
         total = part if total is None else total + part
     send_ref[...] = total.astype(jnp.bfloat16)
@@ -270,7 +294,7 @@
     place = lax.axis_index("expert")
     z = group * 2 + pair_of(place)
 
-    own, send_cot, chosen = prepare(tokens, routes, combine, cotangent, experts)
+    own, send_cot, chosen = prepare(tokens, routes.T, combine.T, cotangent, experts)
     pair = pair_of(place)
     got = lax.all_to_all(
         send_cot.reshape(columns, 2 * PADDED, width),
@@ -302,10 +326,8 @@
     here = pair_of(ring_expert) == pair_of(place)
     ring_row = jnp.where(here, ring_row, -1)
     held_row = jnp.pad(ring_row, ((0, 0), (0, 0), (0, held_count - count)), constant_values=-1)
-    held_row = held_row.transpose(1, 0, 2).reshape(2, 1, planes * held_count)
-    row_ids = jnp.arange(row_total, dtype=jnp.int32)[:, None]
-    select = ((row_ids == held_row[0]) | (row_ids == held_row[1])).astype(jnp.bfloat16)
-    send_tokens = dot_plain(select, ring).astype(jnp.bfloat16)
+    held_row = held_row.transpose(1, 0, 2).reshape(2, planes * held_count)
+    send_tokens = select_rows(held_row, ring, row_total)
     token_rows = lax.all_to_all(
         send_tokens.reshape(columns, planes * capacity, width),
         "expert",

time: 297 us -> 296 us (level)
  matrix products: 39.4 us -> 30.8 us
  Pallas kernels: 26.3 us -> 33.2 us
    dot_general x2 -> x1, matrix products: 17 us -> 8.29 us  [dot_plain(): return jnp.dot(left, right, preferred_element_type=jnp.float32)]
    pallas_call x0 -> x1, Pallas kernels: none -> 6.84 us  [select_rows(): pl.pallas_call(select_kernel, grid=(total // ROWS,), in_specs=[pl.BlockSp...]
    unnamed x30 -> x36, local copies, waits for them, and re-layouts: 9.22 us -> 11.1 us
  transfers between devices with their start and end apart: 10 -> 10, of which waited for: 8 -> 8; matrix products, arithmetic and copies ran while one was open for 21% -> 17% of each run, Pallas kernels for 8% -> 10%
where the time goes in v5:
time: 296 us; the launch traced here: 295 us
  waiting for transfers between devices  154 us (52%)
  starting transfers between devices  35.3 us (12%)
  Pallas kernels  33.2 us (11%)
  matrix products  30.8 us (10%)
  local copies, waits for them, and re-layouts  16.7 us (6%)
  between operations  14.1 us (5%)
  other arithmetic  10.9 us (4%)
    all_to_all x1, waiting for transfers between devices, on_device(): lax.all_to_all(back_rows.reshape(columns, planes * capacity, width), 'exp...  48.8 us
    all_to_all x1, waiting for transfers between devices, on_device(): lax.all_to_all(send_tokens.reshape(columns, planes * capacity, width), 'e...  36.9 us
    ppermute x2, waiting for transfers between devices, pair_swap(): lax.ppermute(x, 'expert', [(e, e + 2 - pair_of(e) * 4) for e in range(exp...  33.7 us
    all_to_all x1, waiting for transfers between devices, on_device(): lax.all_to_all(send_cot.reshape(columns, 2 * PADDED, width), 'expert', sp...  22.6 us
    dot_general x5, matrix products, dot_first(): lax.dot_general(left, right, (((0,), (0,)), ((), ())), preferred_element_...  17.6 us
    unnamed x36, local copies, waits for them, and re-layouts  11.1 us
    all_to_all x1, starting transfers between devices, on_device(): lax.all_to_all(send_tokens.reshape(columns, planes * capacity, width), 'e...  9.01 us
    all_to_all x1, starting transfers between devices, on_device(): lax.all_to_all(send_cot.reshape(columns, 2 * PADDED, width), 'expert', sp...  8.6 us
  transfers between devices with their start and end apart: 10, of which 8 were waited for; matrix products, arithmetic and copies ran while one was open for 17% of the time, Pallas kernels for 10%

profile of v5, /device:TPU:1, one launch (start us, length us, event | category | flops | bytes accessed | tf_op | source)
XLA Modules:
  0.0 295.3 jit_solution(11655583492010014217)
XLA Ops:
  10.6 2.4 prepare_rows.1
  13.0 8.6 %all-to-all-start.2 = ((bf16[32,16,1536]{2,1,0:T(8,128)(2,1)}), bf16[32,16,1536]{2,1,0:T(8,128)(2,1)S(1)}, u32[]{:S(2)}, u32[]{:S(2)}) async-start(bf16[32,16,1536]{2,1,0:T(8,128)(2,1)} %bitcast.18), calls=%async_computation.3 | async-start | bytes 3145728 | tf_op jit(solution)/shard_map/all_to_all | solution.py:299
  21.7 22.6 %all-to-all-done.2 = bf16[32,16,1536]{2,1,0:T(8,128)(2,1)S(1)} async-done(((bf16[32,16,1536]{2,1,0:T(8,128)(2,1)}), bf16[32,16,1536]{2,1,0:T(8,128)(2,1)S(1)}, u32[]{:S(2)}, u32[]{:S(2)}) %all-to-all-start.2) | async-done | bytes 1572896 | tf_op jit(solution)/shard_map/all_to_all | solution.py:299
  45.3 1.3 select_n.241
  46.6 1.7 collective-permute-start.1
  48.6 21.6 %collective-permute-done.1 = bf16[160,1536]{1,0:T(8,128)(2,1)S(1)} collective-permute-done((bf16[160,1536]{1,0:T(8,128)(2,1)S(1)}, bf16[160,1536]{1,0:T(8,128)(2,1)S(1)}, u32[]{:S(2)}, u32[]{:S(2)}) %collective-permute-start.1) | collective-permute-done | bytes 491552 | tf_op jit(solution)/shard_map/ppermute | solution.py:260
  72.7 1.9 copy-done.1
  74.6 6.8 %select_rows.1 = bf16[1280,1536]{1,0:T(8,128)(2,1)} custom-call(s32[2,1088]{1,0:T(2,128)S(1)} %reshape.391.code_ref, bf16[1088,1536]{1,0:T(8,128)(2,1)S(1)} %copy-done.1), custom_call_target="tpu_custom_call" | custom-call | tf_op jit(solution)/shard_map/select_rows/pallas_call | solution.py:38
  81.5 9.0 %all-to-all-start = ((bf16[32,40,1536]{2,1,0:T(8,128)(2,1)}), bf16[32,40,1536]{2,1,0:T(8,128)(2,1)}, u32[]{:S(2)}, u32[]{:S(2)}) async-start(bf16[32,40,1536]{2,1,0:T(8,128)(2,1)} %bitcast.53), calls=%async_computation | async-start | bytes 7864320 | tf_op jit(solution)/shard_map/all_to_all | solution.py:331
  91.2 2.0 copy.19
  94.2 1.6 pad_maximum_fusion
  95.8 2.8 copy.20.w_ref
  98.7 4.1 %fusion.19 = (s32[1280,1]{1,0:T(8,128)}, s32[1280,1]{1,0:T(8,128)S(1)}) fusion(s32[]{:T(128)S(6)} %select_n.219, s32[]{:T(128)S(6)} %sub.62), kind=kLoop, calls=%fused_computation.53 | loop fusion | flops 126720 | bytes 10248 | tf_op jit(solution)/shard_map/add | solution.py:342
  102.8 36.9 %all-to-all-done = bf16[32,40,1536]{2,1,0:T(8,128)(2,1)} async-done(((bf16[32,40,1536]{2,1,0:T(8,128)(2,1)}), bf16[32,40,1536]{2,1,0:T(8,128)(2,1)}, u32[]{:S(2)}, u32[]{:S(2)}) %all-to-all-start) | async-done | bytes 3932192 | tf_op jit(solution)/shard_map/all_to_all | solution.py:331
  139.6 7.3 %forward_rows.1 = (f32[1280,768]{1,0:T(8,128)}, bf16[1280,384]{1,0:T(8,128)(2,1)S(1)}) custom-call(bf16[1280,1536]{1,0:T(8,128)(2,1)} %bitcast.7.x_ref, bf16[1536,768]{1,0:T(8,128)(2,1)S(1)} %copy.20.w_ref), custom_call_target="tpu_custom_call" | custom-call | tf_op jit(solution)/shard_map/forward_rows/pallas_call | solution.py:63
  146.9 6.5 %outward_rows.1 = (bf16[1280,384]{1,0:T(8,128)(2,1)S(1)}, bf16[1280,1536]{1,0:T(8,128)(2,1)}) custom-call(s32[1280,1]{1,0:T(8,128)S(1)} %get-tuple-element.38.place_ref, bf16[1280,384]{1,0:T(8,128)(2,1)S(1)} %get-tuple-element.18.hidden_ref, bf16[384,1536]{1,0:T(8,128)(2,1)S(1)} %bitcast.50), custom_call_target="tpu_custom_call" | custom-call | tf_op jit(solution)/shard_map/outward_rows/pallas_call | solution.py:135
  154.4 1.8 pad_maximum_fusion.1.w_ref
  156.3 4.8 %convolution_convert_fusion.3.d_ref = bf16[1280,384]{1,0:T(8,128)(2,1)S(1)} fusion(bf16[1280,1536]{1,0:T(8,128)(2,1)} %all-gather.5.cloned.1.call-done, bf16[1,384,1536]{2,1,0:T(8,128)(2,1)} %param.12), kind=kOutput, calls=%fused_computation.8 | convolution fusion | flops 1510440960 | bytes 6094848 | tf_op jit(solution)/shard_map/dot_general | solution.py:15
  161.1 7.9 %backward_rows.1 = (bf16[1280,768]{1,0:T(8,128)(2,1)}, bf16[1280,1536]{1,0:T(8,128)(2,1)}) custom-call(s32[1280,1]{1,0:T(8,128)S(1)} %copy-done.2, bf16[1280,384]{1,0:T(8,128)(2,1)S(1)} %convolution_convert_fusion.3.d_ref, f32[1280,768]{1,0:T(8,128)S(1)} %copy-done, bf16[768,1536]{1,0:T(8,128)(2,1)S(1)} %pad_maximum_fusion.1.w_ref), custom_call_target="tpu_custom_call" | custom-call | tf_op jit(solution)/shard_map/backward_rows/pallas_call | solution.py:101
  169.0 7.0 %all-to-all-start.3 = ((bf16[32,40,1536]{2,1,0:T(8,128)(2,1)}), bf16[32,40,1536]{2,1,0:T(8,128)(2,1)}, u32[]{:S(2)}, u32[]{:S(2)}) async-start(bf16[32,40,1536]{2,1,0:T(8,128)(2,1)} %bitcast.60), calls=%async_computation.4 | async-start | bytes 7864320 | tf_op jit(solution)/shard_map/all_to_all | solution.py:358
  176.3 48.8 %all-to-all-done.3 = bf16[32,40,1536]{2,1,0:T(8,128)(2,1)} async-done(((bf16[32,40,1536]{2,1,0:T(8,128)(2,1)}), bf16[32,40,1536]{2,1,0:T(8,128)(2,1)}, u32[]{:S(2)}, u32[]{:S(2)}) %all-to-all-start.3) | async-done | bytes 3932192 | tf_op jit(solution)/shard_map/all_to_all | solution.py:358
  225.2 8.3 %fusion.3 = bf16[1024,1536]{1,0:T(8,128)(2,1)} fusion(bf16[1280,1536]{1,0:T(8,128)(2,1)} %bitcast.22, s32[1024]{0:T(1024)S(1)} %bitcast.62, s32[1024]{0:T(1024)S(1)} %bitcast.61), kind=kOutput, calls=%fused_computation.4 | convolution fusion | flops 4032036864 | bytes 7086080 | tf_op jit(solution)/shard_map/dot_general | solution.py:11
  233.5 5.1 %reduce-scatter.3.cloned.1.call-done.mine_ref = bf16[320,1536]{1,0:T(8,128)(2,1)} async-done(((bf16[1280,1536]{1,0:T(8,128)(2,1)}), bf16[320,1536]{1,0:T(8,128)(2,1)}) %reduce-scatter.3.cloned.1.call-update) | async-done | bytes 983056 | tf_op jit(solution)/shard_map/reduce_scatter | solution.py:352
  239.8 12.1 %collective-permute-done.other_ref = bf16[160,1536]{1,0:T(8,128)(2,1)S(1)} collective-permute-done((bf16[160,1536]{1,0:T(8,128)(2,1)S(1)}, bf16[160,1536]{1,0:T(8,128)(2,1)S(1)}, u32[]{:S(2)}, u32[]{:S(2)}) %collective-permute-start) | collective-permute-done | bytes 491552 | tf_op jit(solution)/shard_map/ppermute | solution.py:260
  251.9 1.2 copy-done.3
  253.1 2.2 spread_rows.1
  255.3 8.5 %all-to-all-start.1 = ((bf16[32,16,1536]{2,1,0:T(8,128)(2,1)}), bf16[32,16,1536]{2,1,0:T(8,128)(2,1)S(1)}, u32[]{:S(2)}, u32[]{:S(2)}) async-start(bf16[32,16,1536]{2,1,0:T(8,128)(2,1)} %bitcast.11), calls=%async_computation.2 | async-start | bytes 3145728 | tf_op jit(solution)/shard_map/all_to_all | solution.py:373
  263.8 5.0 %fusion.10 = bf16[1,384,1536]{2,1,0:T(8,128)(2,1)} fusion(bf16[1280,384]{1,0:T(8,128)(2,1)S(1)} %copy-done.12, bf16[1280,1536]{1,0:T(8,128)(2,1)} %all-gather.5.cloned.1.call-done), kind=kOutput, calls=%fused_computation.13 | convolution fusion | flops 1510539264 | bytes 6094848 | tf_op jit(solution)/shard_map/dot_general | solution.py:21
  268.8 5.4 %fusion.9 = bf16[1,1536,384]{2,1,0:T(8,128)(2,1)} fusion(bf16[1280,1536]{1,0:T(8,128)(2,1)} %bitcast.7.x_ref, bf16[1280,768]{1,0:T(8,128)(2,1)S(1)} %copy-done.16), kind=kOutput, calls=%fused_computation.12 | convolution fusion | flops 1510539264 | bytes 6094848 | tf_op jit(solution)/shard_map/dot_general | solution.py:21
  274.3 5.4 %fusion.8 = bf16[1,1536,384]{2,1,0:T(8,128)(2,1)} fusion(bf16[1280,1536]{1,0:T(8,128)(2,1)} %bitcast.7.x_ref, bf16[1280,768]{1,0:T(8,128)(2,1)S(1)} %copy-done.16), kind=kOutput, calls=%fused_computation.11 | convolution fusion | flops 1510539264 | bytes 6094848 | tf_op jit(solution)/shard_map/dot_general | solution.py:21
  279.7 6.8 %all-to-all-done.1 = bf16[32,16,1536]{2,1,0:T(8,128)(2,1)S(1)} async-done(((bf16[32,16,1536]{2,1,0:T(8,128)(2,1)}), bf16[32,16,1536]{2,1,0:T(8,128)(2,1)S(1)}, u32[]{:S(2)}, u32[]{:S(2)}) %all-to-all-start.1) | async-done | bytes 1572896 | tf_op jit(solution)/shard_map/all_to_all | solution.py:373
  286.9 1.4 fusion.13
  (62 shorter events, 12.3 us)
Async XLA Ops:
  7.2 64.6 %all-gather.3.cloned.1.call-start = ((), (), s32[]{:S(2)}) async-start(), calls=%async_computation.6 | async-start | bytes 3760128 | tf_op jit(solution)/shard_map/all_gather | solution.py:317
  7.2 1.0 copy-start.4
  8.2 1.0 copy-start.7
  9.2 0.7 copy-start.8
  9.9 0.7 copy-start.10
  13.0 31.3 %all-to-all-start.2 = ((bf16[32,16,1536]{2,1,0:T(8,128)(2,1)}), bf16[32,16,1536]{2,1,0:T(8,128)(2,1)S(1)}, u32[]{:S(2)}, u32[]{:S(2)}) async-start(bf16[32,16,1536]{2,1,0:T(8,128)(2,1)} %bitcast.18), calls=%async_computation.3 | async-start | bytes 3145728 | tf_op jit(solution)/shard_map/all_to_all | solution.py:299
  21.6 134.6 %all-gather.5.cloned.1.call-start = ((), (), s32[]{:S(2)}) async-start(), calls=%async_computation.8 | async-start | bytes 4915200 | tf_op jit(solution)/shard_map/all_gather | solution.py:320
  46.6 23.6 %collective-permute-start.1 = (bf16[160,1536]{1,0:T(8,128)(2,1)S(1)}, bf16[160,1536]{1,0:T(8,128)(2,1)S(1)}, u32[]{:S(2)}, u32[]{:S(2)}) collective-permute-start(bf16[160,1536]{1,0:T(8,128)(2,1)S(1)} %select_n.241), channel_id=1, source_target_pairs={{0,2},{1,3},{2,0},{3,1},{4,6},{5,7},{6,4},{7,5},{8,10},{9,11},{10,... | collective-permute-start | bytes 1474568 | tf_op jit(solution)/shard_map/ppermute | solution.py:260
  72.7 1.9 copy-start.1
  81.5 9.1 %copy-start.15 = (bf16[1,1536,384]{2,1,0:T(8,128)(2,1)S(1)}, bf16[1,1536,384]{2,1,0:T(8,128)(2,1)}, u32[]{:S(2)}) copy-start(bf16[1,1536,384]{2,1,0:T(8,128)(2,1)} %param.10) | copy-start | bytes 3538948
  81.5 58.2 %all-to-all-start = ((bf16[32,40,1536]{2,1,0:T(8,128)(2,1)}), bf16[32,40,1536]{2,1,0:T(8,128)(2,1)}, u32[]{:S(2)}, u32[]{:S(2)}) async-start(bf16[32,40,1536]{2,1,0:T(8,128)(2,1)} %bitcast.53), calls=%async_computation | async-start | bytes 7864320 | tf_op jit(solution)/shard_map/all_to_all | solution.py:331
  90.5 148.0 %reduce-scatter.3.cloned.1.call-start = ((), (), s32[]{:S(2)}) async-start(), calls=%async_computation.7 | async-start | bytes 4915200 | tf_op jit(solution)/shard_map/reduce_scatter | solution.py:352
  91.2 2.0 copy-start.13
  93.2 1.0 copy-start.14
  139.6 7.3 %copy-start.6 = (bf16[1,384,1536]{2,1,0:T(8,128)(2,1)S(1)}, bf16[1,384,1536]{2,1,0:T(8,128)(2,1)}, u32[]{:S(2)}) copy-start(bf16[1,384,1536]{2,1,0:T(8,128)(2,1)} %param.12) | copy-start | bytes 3538948
  153.5 1.0 copy-start.11
  156.2 4.9 %copy-start.2 = (s32[1280,1]{1,0:T(8,128)S(1)}, s32[1280,1]{1,0:T(8,128)}, u32[]{:S(2)}) copy-start(s32[1280,1]{1,0:T(8,128)} %get-tuple-element.37.place_ref) | copy-start | bytes 15364
  156.2 4.9 %copy-start = (f32[1280,768]{1,0:T(8,128)S(1)}, f32[1280,768]{1,0:T(8,128)}, u32[]{:S(2)}) copy-start(f32[1280,768]{1,0:T(8,128)} %get-tuple-element.22.pre_ref) | copy-start | bytes 11796484
  169.0 56.1 %all-to-all-start.3 = ((bf16[32,40,1536]{2,1,0:T(8,128)(2,1)}), bf16[32,40,1536]{2,1,0:T(8,128)(2,1)}, u32[]{:S(2)}, u32[]{:S(2)}) async-start(bf16[32,40,1536]{2,1,0:T(8,128)(2,1)} %bitcast.60), calls=%async_computation.4 | async-start | bytes 7864320 | tf_op jit(solution)/shard_map/all_to_all | solution.py:358
  176.0 112.8 %reduce-scatter.5.cloned.1.call-start = ((), (), s32[]{:S(2)}) async-start(), calls=%async_computation.9 | async-start | bytes 3538944 | tf_op jit(solution)/shard_map/reduce_scatter | solution.py:369
  233.4 6.3 %copy-start.9 = (f32[128,2]{0,1:T(2,128)S(1)}, f32[128,2]{0,1:T(2,128)}, u32[]{:S(2)}) copy-start(f32[128,2]{0,1:T(2,128)} %param.9) | copy-start | bytes 3076
  239.6 12.2 %collective-permute-start = (bf16[160,1536]{1,0:T(8,128)(2,1)S(1)}, bf16[160,1536]{1,0:T(8,128)(2,1)S(1)}, u32[]{:S(2)}, u32[]{:S(2)}) collective-permute-start(bf16[160,1536]{1,0:T(8,128)(2,1)S(1)} %slice.70), channel_id=1, source_target_pairs={{0,2},{1,3},{2,0},{3,1},{4,6},{5,7},{6,4},{7,5},{8,10},{9,11},{10,... | collective-permute-start | bytes 1474568 | tf_op jit(solution)/shard_map/ppermute | solution.py:260
  251.9 1.2 copy-start.3
  253.1 10.7 %copy-start.12 = (bf16[1280,384]{1,0:T(8,128)(2,1)S(1)}, bf16[1280,384]{1,0:T(8,128)(2,1)}, u32[]{:S(2)}) copy-start(bf16[1280,384]{1,0:T(8,128)(2,1)} %copy-done.11) | copy-start | bytes 2949124
  255.3 31.2 %all-to-all-start.1 = ((bf16[32,16,1536]{2,1,0:T(8,128)(2,1)}), bf16[32,16,1536]{2,1,0:T(8,128)(2,1)S(1)}, u32[]{:S(2)}, u32[]{:S(2)}) async-start(bf16[32,16,1536]{2,1,0:T(8,128)(2,1)} %bitcast.11), calls=%async_computation.2 | async-start | bytes 3145728 | tf_op jit(solution)/shard_map/all_to_all | solution.py:373
  263.8 5.1 %copy-start.16 = (bf16[1280,768]{1,0:T(8,128)(2,1)S(1)}, bf16[1280,768]{1,0:T(8,128)(2,1)}, u32[]{:S(2)}) copy-start(bf16[1280,768]{1,0:T(8,128)(2,1)} %get-tuple-element.24) | copy-start | bytes 5898244
  279.7 7.2 %copy-start.5 = (bf16[128,1536]{1,0:T(8,128)(2,1)S(1)}, bf16[128,1536]{1,0:T(8,128)(2,1)}, u32[]{:S(2)}) copy-start(bf16[128,1536]{1,0:T(8,128)(2,1)} %cot_ref.1) | copy-start | bytes 1179652
Sparse Core Ops, SparseCore 0:
  13.1 58.5 all-gather.2
  74.1 75.7 all-gather.4
  153.6 84.8 reduce-scatter.2
  241.5 42.7 reduce-scatter.4

commit v6 on v5

--- a/solution.py
+++ b/solution.py
@@ -46,12 +46,11 @@
         out_shape=pltpu.HBM((total, width), jnp.bfloat16),
         compiler_params=pltpu.CompilerParams(vmem_limit_bytes=24 << 20),
         name="select_rows",
-    )(codes, x)
-
-
-def forward_kernel(x_ref, w_ref, pre_ref, hidden_ref):
+    )(codes, pltpu.with_memory_space_constraint(x, pltpu.HBM))
+
+
+def forward_kernel(x_ref, w_ref, hidden_ref):
     pre = dot_plain(x_ref[...], w_ref[...])
-    pre_ref[...] = pre
     half = pre.shape[1] // 2
     gate_pre, up_pre = pre[:, :half], pre[:, half:]
     hidden_ref[...] = (gate_pre * jax.nn.sigmoid(gate_pre) * up_pre).astype(jnp.bfloat16)
@@ -67,44 +66,40 @@
             pl.BlockSpec((ROWS, width), lambda i: (i, 0)),
             pl.BlockSpec((width, both), lambda i: (0, 0), pipeline_mode=pl.Buffered(1)),
         ],
-        out_specs=[
-            pl.BlockSpec((ROWS, both), lambda i: (i, 0)),
-            pl.BlockSpec((ROWS, both // 2), lambda i: (i, 0)),
-        ],
-        out_shape=[
-            pltpu.HBM((total, both), jnp.float32),
-            jax.ShapeDtypeStruct((total, both // 2), jnp.bfloat16),
-        ],
+        out_specs=pl.BlockSpec((ROWS, both // 2), lambda i: (i, 0)),
+        out_shape=jax.ShapeDtypeStruct((total, both // 2), jnp.bfloat16),
         compiler_params=pltpu.CompilerParams(vmem_limit_bytes=24 << 20),
         name="forward_rows",
     )(rows, weights)
 
 
-def backward_kernel(place_ref, d_ref, pre_ref, w_ref, grads_ref, back_ref):
+def backward_kernel(place_ref, d_ref, x_ref, w_ref, wt_ref, grads_ref, back_ref):
     total = d_ref.shape[0]
     places = jnp.broadcast_to(place_ref[...], (ROWS, total))
     select = jnp.where(places == lax.broadcasted_iota(jnp.int32, (ROWS, total), 1), 1.0, 0.0)
     d_hidden = dot_plain(select.astype(jnp.bfloat16), d_ref[...])
     half = d_hidden.shape[1]
-    gate_pre, up_pre = pre_ref[:, :half], pre_ref[:, half:]
+    pre = dot_plain(x_ref[...], w_ref[...])
+    gate_pre, up_pre = pre[:, :half], pre[:, half:]
     sigmoid_gate = jax.nn.sigmoid(gate_pre)
     d_gate = d_hidden * up_pre * sigmoid_gate * (1.0 + gate_pre * (1.0 - sigmoid_gate))
     d_up = d_hidden * gate_pre * sigmoid_gate
     grads_ref[:, :half] = d_gate.astype(jnp.bfloat16)
     grads_ref[:, half:] = d_up.astype(jnp.bfloat16)
-    back_ref[...] = dot_plain(grads_ref[...], w_ref[...]).astype(jnp.bfloat16)
-
-
-def backward(places, d_hidden, pre, weights):
-    total, both = pre.shape
-    width = weights.shape[1]
+    back_ref[...] = dot_plain(grads_ref[...], wt_ref[...]).astype(jnp.bfloat16)
+
+
+def backward(places, d_hidden, rows, weights, weights_t):
+    total, width = rows.shape
+    both = weights.shape[1]
     return pl.pallas_call(
         backward_kernel,
         grid=(total // ROWS,),
         in_specs=[
             pl.BlockSpec((ROWS, 1), lambda i: (i, 0)),
             pl.BlockSpec((total, both // 2), lambda i: (0, 0), pipeline_mode=pl.Buffered(1)),
-            pl.BlockSpec((ROWS, both), lambda i: (i, 0)),
+            pl.BlockSpec((ROWS, width), lambda i: (i, 0)),
+            pl.BlockSpec((width, both), lambda i: (0, 0), pipeline_mode=pl.Buffered(1)),
             pl.BlockSpec((both, width), lambda i: (0, 0), pipeline_mode=pl.Buffered(1)),
         ],
         out_specs=[
@@ -117,7 +112,7 @@
         ],
         compiler_params=pltpu.CompilerParams(vmem_limit_bytes=24 << 20),
         name="backward_rows",
-    )(places, d_hidden, pre, weights)
+    )(places, d_hidden, rows, weights, weights_t)
 
 
 def outward_kernel(place_ref, hidden_ref, w_ref, hidden_out_ref, out_ref):
@@ -228,7 +223,7 @@
         ],
         compiler_params=pltpu.CompilerParams(vmem_limit_bytes=24 << 20),
         name="prepare_rows",
-    )(tokens, routes, combine, cotangent)
+    )(*(pltpu.with_memory_space_constraint(x, pltpu.HBM) for x in (tokens, routes, combine, cotangent)))
 
 
 def column_of(expert):
@@ -347,13 +342,13 @@
     down_w = w_down[0]
     up_gate_w = jnp.concatenate([w_gate[0], w_up[0]], axis=1)
     up_gate_wt = jnp.concatenate([w_gate[0].T, w_up[0].T], axis=0)
-    pre, hidden = forward(token_rows, up_gate_w)
+    hidden = forward(token_rows, up_gate_w)
     hidden_cot, part_out = outward(out_place[:, None], hidden, down_w)
     expert_out = lax.psum_scatter(part_out, "dp", scatter_dimension=0, tiled=True)
 
     d_hidden = dot_last(cot_rows, down_w).astype(jnp.bfloat16)
     d_hidden, _ = lax.optimization_barrier((d_hidden, part_out))
-    d_both, back_rows = backward(cot_place[:, None], d_hidden, pre, up_gate_wt)
+    d_both, back_rows = backward(cot_place[:, None], d_hidden, token_rows, up_gate_w, up_gate_wt)
     d_gate, d_up = d_both[:, : down_w.shape[0]], d_both[:, down_w.shape[0] :]
     arrived = lax.all_to_all(
         back_rows.reshape(columns, planes * capacity, width),

time: 296 us -> 298 us (level)
  Pallas kernels: 33.2 us -> 40.9 us
  local copies, waits for them, and re-layouts: 16.7 us -> 10 us
  starting transfers between devices: 35.3 us -> 38.3 us
    pallas_call x1, Pallas kernels: 7.91 us -> 13.8 us  [backward(): pl.pallas_call(backward_kernel, grid=(total // ROWS,), in_specs=[pl.Block...]
    unnamed x36 -> x32, local copies, waits for them, and re-layouts: 11.1 us -> 5.57 us
    reduce_scatter x1, waiting for transfers between devices: 5.06 us -> 0.02 us  [on_device(): lax.psum_scatter(part_out, 'dp', scatter_dimension=0, tiled=True)]
  transfers between devices with their start and end apart: 10 -> 10, of which waited for: 8 -> 7; matrix products, arithmetic and copies ran while one was open for 17% -> 16% of each run, Pallas kernels for 10% -> 13%
where the time goes in v6:
time: 298 us; the launch traced here: 297 us
  waiting for transfers between devices  152 us (51%)
  Pallas kernels  40.9 us (14%)
  starting transfers between devices  38.3 us (13%)
  matrix products  30.8 us (10%)
  between operations  14 us (5%)
  other arithmetic  11.5 us (4%)
  local copies, waits for them, and re-layouts  10 us (3%)
    all_to_all x1, waiting for transfers between devices, on_device(): lax.all_to_all(back_rows.reshape(columns, planes * capacity, width), 'exp...  48.8 us
    all_to_all x1, waiting for transfers between devices, on_device(): lax.all_to_all(send_tokens.reshape(columns, planes * capacity, width), 'e...  37.7 us
    ppermute x2, waiting for transfers between devices, pair_swap(): lax.ppermute(x, 'expert', [(e, e + 2 - pair_of(e) * 4) for e in range(exp...  33.1 us
    all_to_all x1, waiting for transfers between devices, on_device(): lax.all_to_all(send_cot.reshape(columns, 2 * PADDED, width), 'expert', sp...  22.6 us
    dot_general x5, matrix products, dot_first(): lax.dot_general(left, right, (((0,), (0,)), ((), ())), preferred_element_...  17.6 us
    pallas_call x1, Pallas kernels, backward(): pl.pallas_call(backward_kernel, grid=(total // ROWS,), in_specs=[pl.Block...  13.8 us
    all_to_all x1, starting transfers between devices, on_device(): lax.all_to_all(spread(expert_out, pair_swap(expert_out[half_rows:]), colu...  9.79 us
    all_to_all x1, starting transfers between devices, on_device(): lax.all_to_all(send_tokens.reshape(columns, planes * capacity, width), 'e...  9.69 us
  transfers between devices with their start and end apart: 10, of which 7 were waited for; matrix products, arithmetic and copies ran while one was open for 16% of the time, Pallas kernels for 13%

profile of v6, /device:TPU:1, one launch (start us, length us, event | category | flops | bytes accessed | tf_op | source)
XLA Modules:
  0.0 297.1 jit_solution(15159568500169140310)
XLA Ops:
  7.2 3.6 %prepare_rows.1 = (bf16[136,1536]{1,0:T(8,128)(2,1)}, bf16[512,1536]{1,0:T(8,128)(2,1)}, s32[4,128]{1,0:T(4,128)S(1)}) custom-call(bf16[128,1536]{1,0:T(8,128)(2,1)} %tokens_ref.1, s32[2,128]{1,0:T(2,128)} %bitcast.64, f32[2,128]{1,0:T(2,128)} %bitcast.59, bf16[128,1536]{1,0:T(8,128)(2,1)} %cot_ref.1), custom_call_target="tpu_custom_call" | custom-call | tf_op jit(solution)/shard_map/prepare_rows/pallas_call | solution.py:217
  10.8 8.6 %all-to-all-start.2 = ((bf16[32,16,1536]{2,1,0:T(8,128)(2,1)}), bf16[32,16,1536]{2,1,0:T(8,128)(2,1)S(1)}, u32[]{:S(2)}, u32[]{:S(2)}) async-start(bf16[32,16,1536]{2,1,0:T(8,128)(2,1)} %bitcast.18), calls=%async_computation.3 | async-start | bytes 3145728 | tf_op jit(solution)/shard_map/all_to_all | solution.py:294
  19.5 22.6 %all-to-all-done.2 = bf16[32,16,1536]{2,1,0:T(8,128)(2,1)S(1)} async-done(((bf16[32,16,1536]{2,1,0:T(8,128)(2,1)}), bf16[32,16,1536]{2,1,0:T(8,128)(2,1)S(1)}, u32[]{:S(2)}, u32[]{:S(2)}) %all-to-all-start.2) | async-done | bytes 1572896 | tf_op jit(solution)/shard_map/all_to_all | solution.py:294
  42.4 1.7 collective-permute-start.1
  44.4 21.7 %collective-permute-done.1 = bf16[160,1536]{1,0:T(8,128)(2,1)S(1)} collective-permute-done((bf16[160,1536]{1,0:T(8,128)(2,1)S(1)}, bf16[160,1536]{1,0:T(8,128)(2,1)S(1)}, u32[]{:S(2)}, u32[]{:S(2)}) %collective-permute-start.1) | collective-permute-done | bytes 491552 | tf_op jit(solution)/shard_map/ppermute | solution.py:255
  66.1 1.0 pad_maximum_fusion.2
  67.1 2.6 all-gather.3.cloned.1.call-done.x_ref
  71.1 8.8 %select_rows.1 = bf16[1280,1536]{1,0:T(8,128)(2,1)} custom-call(s32[2,1088]{1,0:T(2,128)S(1)} %reshape.391.code_ref, bf16[1088,1536]{1,0:T(8,128)(2,1)} %all-gather.3.cloned.1.call-done.x_ref), custom_call_target="tpu_custom_call" | custom-call | tf_op jit(solution)/shard_map/select_rows/pallas_call | solution.py:38
  80.0 9.7 %all-to-all-start = ((bf16[32,40,1536]{2,1,0:T(8,128)(2,1)}), bf16[32,40,1536]{2,1,0:T(8,128)(2,1)}, u32[]{:S(2)}, u32[]{:S(2)}) async-start(bf16[32,40,1536]{2,1,0:T(8,128)(2,1)} %bitcast.50), calls=%async_computation | async-start | bytes 7864320 | tf_op jit(solution)/shard_map/all_to_all | solution.py:326
  92.6 1.6 pad_maximum_fusion
  94.2 2.8 copy.21.w_ref
  97.1 4.1 %fusion.19 = (s32[1280,1]{1,0:T(8,128)S(1)}, s32[1280,1]{1,0:T(8,128)}) fusion(s32[]{:T(128)S(6)} %select_n.219, s32[]{:T(128)S(6)} %sub.62), kind=kLoop, calls=%fused_computation.53 | loop fusion | flops 126720 | bytes 10248 | tf_op jit(solution)/shard_map/add | solution.py:337
  101.1 37.7 %all-to-all-done = bf16[32,40,1536]{2,1,0:T(8,128)(2,1)} async-done(((bf16[32,40,1536]{2,1,0:T(8,128)(2,1)}), bf16[32,40,1536]{2,1,0:T(8,128)(2,1)}, u32[]{:S(2)}, u32[]{:S(2)}) %all-to-all-start) | async-done | bytes 3932192 | tf_op jit(solution)/shard_map/all_to_all | solution.py:326
  138.8 5.9 %forward_rows.1.hidden_ref = bf16[1280,384]{1,0:T(8,128)(2,1)S(1)} custom-call(bf16[1280,1536]{1,0:T(8,128)(2,1)} %bitcast.7.x_ref, bf16[1536,768]{1,0:T(8,128)(2,1)S(1)} %copy.21.w_ref), custom_call_target="tpu_custom_call" | custom-call | tf_op jit(solution)/shard_map/forward_rows/pallas_call | solution.py:62
  144.8 6.6 %outward_rows.1 = (bf16[1280,384]{1,0:T(8,128)(2,1)S(1)}, bf16[1280,1536]{1,0:T(8,128)(2,1)}) custom-call(s32[1280,1]{1,0:T(8,128)S(1)} %copy-done.1, bf16[1280,384]{1,0:T(8,128)(2,1)S(1)} %forward_rows.1.hidden_ref, bf16[384,1536]{1,0:T(8,128)(2,1)S(1)} %bitcast.49), custom_call_target="tpu_custom_call" | custom-call | tf_op jit(solution)/shard_map/outward_rows/pallas_call | solution.py:130
  152.4 3.2 %pad_maximum_fusion.1.wt_ref = bf16[768,1536]{1,0:T(8,128)(2,1)} fusion(bf16[384,1536]{1,0:T(8,128)(2,1)} %bitcast.56, bf16[384,1536]{1,0:T(8,128)(2,1)} %bitcast.54), kind=kLoop, calls=%fused_computation.15 | loop fusion | flops 4718592 | bytes 4718592 | tf_op jit(solution)/shard_map/concatenate | solution.py:344
  155.6 4.8 %convolution_convert_fusion.3.d_ref = bf16[1280,384]{1,0:T(8,128)(2,1)S(1)} fusion(bf16[1280,1536]{1,0:T(8,128)(2,1)} %all-gather.5.cloned.1.call-done, bf16[1,384,1536]{2,1,0:T(8,128)(2,1)} %param.12), kind=kOutput, calls=%fused_computation.8 | convolution fusion | flops 1510440960 | bytes 6094848 | tf_op jit(solution)/shard_map/dot_general | solution.py:15
  160.4 13.8 %backward_rows.1 = (bf16[1280,768]{1,0:T(8,128)(2,1)}, bf16[1280,1536]{1,0:T(8,128)(2,1)}) custom-call(s32[1280,1]{1,0:T(8,128)S(1)} %get-tuple-element.33.place_ref, bf16[1280,384]{1,0:T(8,128)(2,1)S(1)} %convolution_convert_fusion.3.d_ref, bf16[1280,1536]{1,0:T(8,128)(2,1)} %bitcast.7.x_ref, bf16[1536,768]{1,0:T(8,128)(2,1)S(1)} %copy.21.w_ref, ...), custom_call_target="tpu_custom_call" | custom-call | tf_op jit(solution)/shard_map/backward_rows/pallas_call | solution.py:95
  174.2 7.1 %all-to-all-start.3 = ((bf16[32,40,1536]{2,1,0:T(8,128)(2,1)}), bf16[32,40,1536]{2,1,0:T(8,128)(2,1)}, u32[]{:S(2)}, u32[]{:S(2)}) async-start(bf16[32,40,1536]{2,1,0:T(8,128)(2,1)} %bitcast.57), calls=%async_computation.4 | async-start | bytes 7864320 | tf_op jit(solution)/shard_map/all_to_all | solution.py:353
  181.7 48.8 %all-to-all-done.3 = bf16[32,40,1536]{2,1,0:T(8,128)(2,1)} async-done(((bf16[32,40,1536]{2,1,0:T(8,128)(2,1)}), bf16[32,40,1536]{2,1,0:T(8,128)(2,1)}, u32[]{:S(2)}, u32[]{:S(2)}) %all-to-all-start.3) | async-done | bytes 3932192 | tf_op jit(solution)/shard_map/all_to_all | solution.py:353
  230.5 8.3 %fusion.3 = bf16[1024,1536]{1,0:T(8,128)(2,1)} fusion(bf16[1280,1536]{1,0:T(8,128)(2,1)} %bitcast.22, s32[1024]{0:T(1024)S(1)} %bitcast.61, s32[1024]{0:T(1024)S(1)} %bitcast.60), kind=kOutput, calls=%fused_computation.4 | convolution fusion | flops 4032036864 | bytes 7086080 | tf_op jit(solution)/shard_map/dot_general | solution.py:11
  238.8 1.1 slice.70
  239.9 1.0 collective-permute-start
  241.0 11.4 %collective-permute-done.other_ref = bf16[160,1536]{1,0:T(8,128)(2,1)S(1)} collective-permute-done((bf16[160,1536]{1,0:T(8,128)(2,1)S(1)}, bf16[160,1536]{1,0:T(8,128)(2,1)S(1)}, u32[]{:S(2)}, u32[]{:S(2)}) %collective-permute-start) | collective-permute-done | bytes 491552 | tf_op jit(solution)/shard_map/ppermute | solution.py:255
  252.4 1.2 copy-done.2
  253.6 2.2 spread_rows.1
  255.8 9.8 %all-to-all-start.1 = ((bf16[32,16,1536]{2,1,0:T(8,128)(2,1)}), bf16[32,16,1536]{2,1,0:T(8,128)(2,1)S(1)}, u32[]{:S(2)}, u32[]{:S(2)}) async-start(bf16[32,16,1536]{2,1,0:T(8,128)(2,1)} %bitcast.11), calls=%async_computation.2 | async-start | bytes 3145728 | tf_op jit(solution)/shard_map/all_to_all | solution.py:368
  265.6 5.0 %fusion.10 = bf16[1,384,1536]{2,1,0:T(8,128)(2,1)} fusion(bf16[1280,384]{1,0:T(8,128)(2,1)S(1)} %copy-done.5, bf16[1280,1536]{1,0:T(8,128)(2,1)} %all-gather.5.cloned.1.call-done), kind=kOutput, calls=%fused_computation.13 | convolution fusion | flops 1510539264 | bytes 6094848 | tf_op jit(solution)/shard_map/dot_general | solution.py:21
  270.6 5.4 %fusion.9 = bf16[1,1536,384]{2,1,0:T(8,128)(2,1)} fusion(bf16[1280,1536]{1,0:T(8,128)(2,1)} %bitcast.7.x_ref, bf16[1280,768]{1,0:T(8,128)(2,1)S(1)} %copy-done.14), kind=kOutput, calls=%fused_computation.12 | convolution fusion | flops 1510539264 | bytes 6094848 | tf_op jit(solution)/shard_map/dot_general | solution.py:21
  276.1 5.4 %fusion.8 = bf16[1,1536,384]{2,1,0:T(8,128)(2,1)} fusion(bf16[1280,1536]{1,0:T(8,128)(2,1)} %bitcast.7.x_ref, bf16[1280,768]{1,0:T(8,128)(2,1)S(1)} %copy-done.14), kind=kOutput, calls=%fused_computation.11 | convolution fusion | flops 1510539264 | bytes 6094848 | tf_op jit(solution)/shard_map/dot_general | solution.py:21
  281.5 6.8 %all-to-all-done.1 = bf16[32,16,1536]{2,1,0:T(8,128)(2,1)S(1)} async-done(((bf16[32,16,1536]{2,1,0:T(8,128)(2,1)}), bf16[32,16,1536]{2,1,0:T(8,128)(2,1)S(1)}, u32[]{:S(2)}, u32[]{:S(2)}) %all-to-all-start.1) | async-done | bytes 1572896 | tf_op jit(solution)/shard_map/all_to_all | solution.py:368
  288.7 1.4 fusion.13
  (58 shorter events, 7.3 us)
Async XLA Ops:
  7.2 62.6 %all-gather.3.cloned.1.call-start = ((), (), s32[]{:S(2)}) async-start(), calls=%async_computation.6 | async-start | bytes 3760128 | tf_op jit(solution)/shard_map/all_gather | solution.py:312
  10.8 31.3 %all-to-all-start.2 = ((bf16[32,16,1536]{2,1,0:T(8,128)(2,1)}), bf16[32,16,1536]{2,1,0:T(8,128)(2,1)S(1)}, u32[]{:S(2)}, u32[]{:S(2)}) async-start(bf16[32,16,1536]{2,1,0:T(8,128)(2,1)} %bitcast.18), calls=%async_computation.3 | async-start | bytes 3145728 | tf_op jit(solution)/shard_map/all_to_all | solution.py:294
  19.4 136.2 %all-gather.5.cloned.1.call-start = ((), (), s32[]{:S(2)}) async-start(), calls=%async_computation.8 | async-start | bytes 4915200 | tf_op jit(solution)/shard_map/all_gather | solution.py:315
  42.4 23.7 %collective-permute-start.1 = (bf16[160,1536]{1,0:T(8,128)(2,1)S(1)}, bf16[160,1536]{1,0:T(8,128)(2,1)S(1)}, u32[]{:S(2)}, u32[]{:S(2)}) collective-permute-start(bf16[160,1536]{1,0:T(8,128)(2,1)S(1)} %select_n.241), channel_id=1, source_target_pairs={{0,2},{1,3},{2,0},{3,1},{4,6},{5,7},{6,4},{7,5},{8,10},{9,11},{10,... | collective-permute-start | bytes 1474568 | tf_op jit(solution)/shard_map/ppermute | solution.py:255
  70.4 0.6 copy-start.11
  80.0 9.8 %copy-start.9 = (bf16[1,1536,384]{2,1,0:T(8,128)(2,1)S(1)}, bf16[1,1536,384]{2,1,0:T(8,128)(2,1)}, u32[]{:S(2)}) copy-start(bf16[1,1536,384]{2,1,0:T(8,128)(2,1)} %param.10) | copy-start | bytes 3538948
  80.0 58.8 %all-to-all-start = ((bf16[32,40,1536]{2,1,0:T(8,128)(2,1)}), bf16[32,40,1536]{2,1,0:T(8,128)(2,1)}, u32[]{:S(2)}, u32[]{:S(2)}) async-start(bf16[32,40,1536]{2,1,0:T(8,128)(2,1)} %bitcast.50), calls=%async_computation | async-start | bytes 7864320 | tf_op jit(solution)/shard_map/all_to_all | solution.py:326
  89.7 1.3 copy-start.10
  89.7 149.1 %reduce-scatter.3.cloned.1.call-start = ((), (), s32[]{:S(2)}) async-start(), calls=%async_computation.7 | async-start | bytes 4915200 | tf_op jit(solution)/shard_map/reduce_scatter | solution.py:347
  91.0 1.0 copy-start.6
  91.6 1.0 copy-start.7
  138.8 5.9 %copy-start.1 = (s32[1280,1]{1,0:T(8,128)S(1)}, s32[1280,1]{1,0:T(8,128)}, u32[]{:S(2)}) copy-start(s32[1280,1]{1,0:T(8,128)} %get-tuple-element.34.place_ref) | copy-start | bytes 15364
  138.8 5.9 %copy-start.3 = (bf16[1,384,1536]{2,1,0:T(8,128)(2,1)S(1)}, bf16[1,384,1536]{2,1,0:T(8,128)(2,1)}, u32[]{:S(2)}) copy-start(bf16[1,384,1536]{2,1,0:T(8,128)(2,1)} %param.12) | copy-start | bytes 3538948
  151.4 1.0 copy-start.4
  155.6 4.8 %copy-start = (bf16[768,1536]{1,0:T(8,128)(2,1)S(1)}, bf16[768,1536]{1,0:T(8,128)(2,1)}, u32[]{:S(2)}) copy-start(bf16[768,1536]{1,0:T(8,128)(2,1)} %pad_maximum_fusion.1.wt_ref) | copy-start | bytes 7077892
  174.2 7.4 %copy-start.12 = (s32[8,4,128]{2,1,0:T(4,128)S(1)}, s32[8,4,128]{2,1,0:T(4,128)}, u32[]{:S(2)}) copy-start(s32[8,4,128]{2,1,0:T(4,128)} %copy-done.11) | copy-start | bytes 49156
  174.2 56.3 %all-to-all-start.3 = ((bf16[32,40,1536]{2,1,0:T(8,128)(2,1)}), bf16[32,40,1536]{2,1,0:T(8,128)(2,1)}, u32[]{:S(2)}, u32[]{:S(2)}) async-start(bf16[32,40,1536]{2,1,0:T(8,128)(2,1)} %bitcast.57), calls=%async_computation.4 | async-start | bytes 7864320 | tf_op jit(solution)/shard_map/all_to_all | solution.py:353
  181.3 109.3 %reduce-scatter.5.cloned.1.call-start = ((), (), s32[]{:S(2)}) async-start(), calls=%async_computation.9 | async-start | bytes 3538944 | tf_op jit(solution)/shard_map/reduce_scatter | solution.py:364
  238.8 2.2 copy-start.13
  239.9 12.5 %collective-permute-start = (bf16[160,1536]{1,0:T(8,128)(2,1)S(1)}, bf16[160,1536]{1,0:T(8,128)(2,1)S(1)}, u32[]{:S(2)}, u32[]{:S(2)}) collective-permute-start(bf16[160,1536]{1,0:T(8,128)(2,1)S(1)} %slice.70), channel_id=1, source_target_pairs={{0,2},{1,3},{2,0},{3,1},{4,6},{5,7},{6,4},{7,5},{8,10},{9,11},{10,... | collective-permute-start | bytes 1474568 | tf_op jit(solution)/shard_map/ppermute | solution.py:255
  252.4 1.2 copy-start.2
  253.6 12.0 %copy-start.5 = (bf16[1280,384]{1,0:T(8,128)(2,1)S(1)}, bf16[1280,384]{1,0:T(8,128)(2,1)}, u32[]{:S(2)}) copy-start(bf16[1280,384]{1,0:T(8,128)(2,1)} %copy-done.4) | copy-start | bytes 2949124
  255.8 32.5 %all-to-all-start.1 = ((bf16[32,16,1536]{2,1,0:T(8,128)(2,1)}), bf16[32,16,1536]{2,1,0:T(8,128)(2,1)S(1)}, u32[]{:S(2)}, u32[]{:S(2)}) async-start(bf16[32,16,1536]{2,1,0:T(8,128)(2,1)} %bitcast.11), calls=%async_computation.2 | async-start | bytes 3145728 | tf_op jit(solution)/shard_map/all_to_all | solution.py:368
  265.6 5.1 %copy-start.14 = (bf16[1280,768]{1,0:T(8,128)(2,1)S(1)}, bf16[1280,768]{1,0:T(8,128)(2,1)}, u32[]{:S(2)}) copy-start(bf16[1280,768]{1,0:T(8,128)(2,1)} %get-tuple-element.20) | copy-start | bytes 5898244
  281.5 7.2 %copy-start.8 = (bf16[128,1536]{1,0:T(8,128)(2,1)S(1)}, bf16[128,1536]{1,0:T(8,128)(2,1)}, u32[]{:S(2)}) copy-start(bf16[128,1536]{1,0:T(8,128)(2,1)} %cot_ref.1) | copy-start | bytes 1179652
Sparse Core Ops, SparseCore 0:
  10.9 58.7 all-gather.2
  72.1 75.5 all-gather.4
  152.5 83.9 reduce-scatter.2
  239.4 43.7 reduce-scatter.4

commit v7 on v5

--- a/solution.py
+++ b/solution.py
@@ -228,7 +228,7 @@
         ],
         compiler_params=pltpu.CompilerParams(vmem_limit_bytes=24 << 20),
         name="prepare_rows",
-    )(tokens, routes, combine, cotangent)
+    )(*(pltpu.with_memory_space_constraint(x, pltpu.HBM) for x in (tokens, routes, combine, cotangent)))
 
 
 def column_of(expert):

time: 296 us -> 294 us (level)
  local copies, waits for them, and re-layouts: 16.7 us -> 13.4 us
    unnamed x36 -> x28, local copies, waits for them, and re-layouts: 11.1 us -> 7.79 us
  transfers between devices with their start and end apart: 10 -> 10, of which waited for: 8 -> 8; matrix products, arithmetic and copies ran while one was open for 17% -> 17% of each run, Pallas kernels for 10% -> 11%
where the time goes in v7:
time: 294 us; the launch traced here: 293 us
  waiting for transfers between devices  154 us (52%)
  starting transfers between devices  35.2 us (12%)
  Pallas kernels  34.4 us (12%)
  matrix products  30.8 us (10%)
  between operations  14.1 us (5%)
  local copies, waits for them, and re-layouts  13.4 us (5%)
  other arithmetic  10.9 us (4%)
    all_to_all x1, waiting for transfers between devices, on_device(): lax.all_to_all(back_rows.reshape(columns, planes * capacity, width), 'exp...  48.8 us
    all_to_all x1, waiting for transfers between devices, on_device(): lax.all_to_all(send_tokens.reshape(columns, planes * capacity, width), 'e...  36.9 us
    ppermute x2, waiting for transfers between devices, pair_swap(): lax.ppermute(x, 'expert', [(e, e + 2 - pair_of(e) * 4) for e in range(exp...  33.7 us
    all_to_all x1, waiting for transfers between devices, on_device(): lax.all_to_all(send_cot.reshape(columns, 2 * PADDED, width), 'expert', sp...  22.6 us
    dot_general x5, matrix products, dot_first(): lax.dot_general(left, right, (((0,), (0,)), ((), ())), preferred_element_...  17.6 us
    all_to_all x1, starting transfers between devices, on_device(): lax.all_to_all(send_tokens.reshape(columns, planes * capacity, width), 'e...  9.01 us
    all_to_all x1, starting transfers between devices, on_device(): lax.all_to_all(send_cot.reshape(columns, 2 * PADDED, width), 'expert', sp...  8.6 us
    all_to_all x1, starting transfers between devices, on_device(): lax.all_to_all(spread(expert_out, pair_swap(expert_out[half_rows:]), colu...  8.35 us
  transfers between devices with their start and end apart: 10, of which 8 were waited for; matrix products, arithmetic and copies ran while one was open for 17% of the time, Pallas kernels for 11%

profile of v7, /device:TPU:1, one launch (start us, length us, event | category | flops | bytes accessed | tf_op | source)
XLA Modules:
  0.0 293.2 jit_solution(9658124129383682744)
XLA Ops:
  7.2 3.6 %prepare_rows.1 = (bf16[136,1536]{1,0:T(8,128)(2,1)}, bf16[512,1536]{1,0:T(8,128)(2,1)}, s32[4,128]{1,0:T(4,128)S(1)}) custom-call(bf16[128,1536]{1,0:T(8,128)(2,1)} %tokens_ref.1, s32[2,128]{1,0:T(2,128)} %bitcast.64, f32[2,128]{1,0:T(2,128)} %bitcast.59, bf16[128,1536]{1,0:T(8,128)(2,1)} %cot_ref.1), custom_call_target="tpu_custom_call" | custom-call | tf_op jit(solution)/shard_map/prepare_rows/pallas_call | solution.py:222
  10.8 8.6 %all-to-all-start.2 = ((bf16[32,16,1536]{2,1,0:T(8,128)(2,1)}), bf16[32,16,1536]{2,1,0:T(8,128)(2,1)S(1)}, u32[]{:S(2)}, u32[]{:S(2)}) async-start(bf16[32,16,1536]{2,1,0:T(8,128)(2,1)} %bitcast.18), calls=%async_computation.3 | async-start | bytes 3145728 | tf_op jit(solution)/shard_map/all_to_all | solution.py:299
  19.5 22.6 %all-to-all-done.2 = bf16[32,16,1536]{2,1,0:T(8,128)(2,1)S(1)} async-done(((bf16[32,16,1536]{2,1,0:T(8,128)(2,1)}), bf16[32,16,1536]{2,1,0:T(8,128)(2,1)S(1)}, u32[]{:S(2)}, u32[]{:S(2)}) %all-to-all-start.2) | async-done | bytes 1572896 | tf_op jit(solution)/shard_map/all_to_all | solution.py:299
  43.1 1.3 select_n.241
  44.4 1.7 collective-permute-start.1
  46.4 21.6 %collective-permute-done.1 = bf16[160,1536]{1,0:T(8,128)(2,1)S(1)} collective-permute-done((bf16[160,1536]{1,0:T(8,128)(2,1)S(1)}, bf16[160,1536]{1,0:T(8,128)(2,1)S(1)}, u32[]{:S(2)}, u32[]{:S(2)}) %collective-permute-start.1) | collective-permute-done | bytes 491552 | tf_op jit(solution)/shard_map/ppermute | solution.py:260
  70.5 1.9 copy-done.1
  72.4 6.9 %select_rows.1 = bf16[1280,1536]{1,0:T(8,128)(2,1)} custom-call(s32[2,1088]{1,0:T(2,128)S(1)} %reshape.391.code_ref, bf16[1088,1536]{1,0:T(8,128)(2,1)S(1)} %copy-done.1), custom_call_target="tpu_custom_call" | custom-call | tf_op jit(solution)/shard_map/select_rows/pallas_call | solution.py:38
  79.3 9.0 %all-to-all-start = ((bf16[32,40,1536]{2,1,0:T(8,128)(2,1)}), bf16[32,40,1536]{2,1,0:T(8,128)(2,1)}, u32[]{:S(2)}, u32[]{:S(2)}) async-start(bf16[32,40,1536]{2,1,0:T(8,128)(2,1)} %bitcast.51), calls=%async_computation | async-start | bytes 7864320 | tf_op jit(solution)/shard_map/all_to_all | solution.py:331
  89.1 2.0 copy.19
  92.1 1.6 pad_maximum_fusion
  93.7 2.8 copy.20.w_ref
  96.5 4.1 %fusion.19 = (s32[1280,1]{1,0:T(8,128)}, s32[1280,1]{1,0:T(8,128)S(1)}) fusion(s32[]{:T(128)S(6)} %select_n.219, s32[]{:T(128)S(6)} %sub.62), kind=kLoop, calls=%fused_computation.53 | loop fusion | flops 126720 | bytes 10248 | tf_op jit(solution)/shard_map/add | solution.py:342
  100.6 36.9 %all-to-all-done = bf16[32,40,1536]{2,1,0:T(8,128)(2,1)} async-done(((bf16[32,40,1536]{2,1,0:T(8,128)(2,1)}), bf16[32,40,1536]{2,1,0:T(8,128)(2,1)}, u32[]{:S(2)}, u32[]{:S(2)}) %all-to-all-start) | async-done | bytes 3932192 | tf_op jit(solution)/shard_map/all_to_all | solution.py:331
  137.5 7.3 %forward_rows.1 = (f32[1280,768]{1,0:T(8,128)}, bf16[1280,384]{1,0:T(8,128)(2,1)S(1)}) custom-call(bf16[1280,1536]{1,0:T(8,128)(2,1)} %bitcast.7.x_ref, bf16[1536,768]{1,0:T(8,128)(2,1)S(1)} %copy.20.w_ref), custom_call_target="tpu_custom_call" | custom-call | tf_op jit(solution)/shard_map/forward_rows/pallas_call | solution.py:63
  144.8 6.5 %outward_rows.1 = (bf16[1280,384]{1,0:T(8,128)(2,1)S(1)}, bf16[1280,1536]{1,0:T(8,128)(2,1)}) custom-call(s32[1280,1]{1,0:T(8,128)S(1)} %get-tuple-element.38.place_ref, bf16[1280,384]{1,0:T(8,128)(2,1)S(1)} %get-tuple-element.18.hidden_ref, bf16[384,1536]{1,0:T(8,128)(2,1)S(1)} %bitcast.50), custom_call_target="tpu_custom_call" | custom-call | tf_op jit(solution)/shard_map/outward_rows/pallas_call | solution.py:135
  152.3 1.8 pad_maximum_fusion.1.w_ref
  154.1 4.8 %convolution_convert_fusion.3.d_ref = bf16[1280,384]{1,0:T(8,128)(2,1)S(1)} fusion(bf16[1280,1536]{1,0:T(8,128)(2,1)} %all-gather.5.cloned.1.call-done, bf16[1,384,1536]{2,1,0:T(8,128)(2,1)} %param.12), kind=kOutput, calls=%fused_computation.8 | convolution fusion | flops 1510440960 | bytes 6094848 | tf_op jit(solution)/shard_map/dot_general | solution.py:15
  159.0 7.9 %backward_rows.1 = (bf16[1280,768]{1,0:T(8,128)(2,1)}, bf16[1280,1536]{1,0:T(8,128)(2,1)}) custom-call(s32[1280,1]{1,0:T(8,128)S(1)} %copy-done.2, bf16[1280,384]{1,0:T(8,128)(2,1)S(1)} %convolution_convert_fusion.3.d_ref, f32[1280,768]{1,0:T(8,128)S(1)} %copy-done, bf16[768,1536]{1,0:T(8,128)(2,1)S(1)} %pad_maximum_fusion.1.w_ref), custom_call_target="tpu_custom_call" | custom-call | tf_op jit(solution)/shard_map/backward_rows/pallas_call | solution.py:101
  166.9 7.0 %all-to-all-start.3 = ((bf16[32,40,1536]{2,1,0:T(8,128)(2,1)}), bf16[32,40,1536]{2,1,0:T(8,128)(2,1)}, u32[]{:S(2)}, u32[]{:S(2)}) async-start(bf16[32,40,1536]{2,1,0:T(8,128)(2,1)} %bitcast.58), calls=%async_computation.4 | async-start | bytes 7864320 | tf_op jit(solution)/shard_map/all_to_all | solution.py:358
  174.2 48.8 %all-to-all-done.3 = bf16[32,40,1536]{2,1,0:T(8,128)(2,1)} async-done(((bf16[32,40,1536]{2,1,0:T(8,128)(2,1)}), bf16[32,40,1536]{2,1,0:T(8,128)(2,1)}, u32[]{:S(2)}, u32[]{:S(2)}) %all-to-all-start.3) | async-done | bytes 3932192 | tf_op jit(solution)/shard_map/all_to_all | solution.py:358
  223.0 8.3 %fusion.3 = bf16[1024,1536]{1,0:T(8,128)(2,1)} fusion(bf16[1280,1536]{1,0:T(8,128)(2,1)} %bitcast.22, s32[1024]{0:T(1024)S(1)} %bitcast.61, s32[1024]{0:T(1024)S(1)} %bitcast.60), kind=kOutput, calls=%fused_computation.4 | convolution fusion | flops 4032036864 | bytes 7086080 | tf_op jit(solution)/shard_map/dot_general | solution.py:11
  231.4 5.1 %reduce-scatter.3.cloned.1.call-done.mine_ref = bf16[320,1536]{1,0:T(8,128)(2,1)} async-done(((bf16[1280,1536]{1,0:T(8,128)(2,1)}), bf16[320,1536]{1,0:T(8,128)(2,1)}) %reduce-scatter.3.cloned.1.call-update) | async-done | bytes 983056 | tf_op jit(solution)/shard_map/reduce_scatter | solution.py:352
  237.7 12.1 %collective-permute-done.other_ref = bf16[160,1536]{1,0:T(8,128)(2,1)S(1)} collective-permute-done((bf16[160,1536]{1,0:T(8,128)(2,1)S(1)}, bf16[160,1536]{1,0:T(8,128)(2,1)S(1)}, u32[]{:S(2)}, u32[]{:S(2)}) %collective-permute-start) | collective-permute-done | bytes 491552 | tf_op jit(solution)/shard_map/ppermute | solution.py:260
  249.8 1.2 copy-done.3
  251.0 2.2 spread_rows.1
  253.2 8.4 %all-to-all-start.1 = ((bf16[32,16,1536]{2,1,0:T(8,128)(2,1)}), bf16[32,16,1536]{2,1,0:T(8,128)(2,1)S(1)}, u32[]{:S(2)}, u32[]{:S(2)}) async-start(bf16[32,16,1536]{2,1,0:T(8,128)(2,1)} %bitcast.11), calls=%async_computation.2 | async-start | bytes 3145728 | tf_op jit(solution)/shard_map/all_to_all | solution.py:373
  261.6 5.0 %fusion.10 = bf16[1,384,1536]{2,1,0:T(8,128)(2,1)} fusion(bf16[1280,384]{1,0:T(8,128)(2,1)S(1)} %copy-done.6, bf16[1280,1536]{1,0:T(8,128)(2,1)} %all-gather.5.cloned.1.call-done), kind=kOutput, calls=%fused_computation.13 | convolution fusion | flops 1510539264 | bytes 6094848 | tf_op jit(solution)/shard_map/dot_general | solution.py:21
  266.7 5.4 %fusion.9 = bf16[1,1536,384]{2,1,0:T(8,128)(2,1)} fusion(bf16[1280,1536]{1,0:T(8,128)(2,1)} %bitcast.7.x_ref, bf16[1280,768]{1,0:T(8,128)(2,1)S(1)} %copy-done.12), kind=kOutput, calls=%fused_computation.12 | convolution fusion | flops 1510539264 | bytes 6094848 | tf_op jit(solution)/shard_map/dot_general | solution.py:21
  272.1 5.4 %fusion.8 = bf16[1,1536,384]{2,1,0:T(8,128)(2,1)} fusion(bf16[1280,1536]{1,0:T(8,128)(2,1)} %bitcast.7.x_ref, bf16[1280,768]{1,0:T(8,128)(2,1)S(1)} %copy-done.12), kind=kOutput, calls=%fused_computation.11 | convolution fusion | flops 1510539264 | bytes 6094848 | tf_op jit(solution)/shard_map/dot_general | solution.py:21
  277.5 6.8 %all-to-all-done.1 = bf16[32,16,1536]{2,1,0:T(8,128)(2,1)S(1)} async-done(((bf16[32,16,1536]{2,1,0:T(8,128)(2,1)}), bf16[32,16,1536]{2,1,0:T(8,128)(2,1)S(1)}, u32[]{:S(2)}, u32[]{:S(2)}) %all-to-all-start.1) | async-done | bytes 1572896 | tf_op jit(solution)/shard_map/all_to_all | solution.py:373
  284.7 1.4 fusion.13
  (54 shorter events, 9.0 us)
Async XLA Ops:
  7.2 62.4 %all-gather.3.cloned.1.call-start = ((), (), s32[]{:S(2)}) async-start(), calls=%async_computation.6 | async-start | bytes 3760128 | tf_op jit(solution)/shard_map/all_gather | solution.py:317
  10.8 31.3 %all-to-all-start.2 = ((bf16[32,16,1536]{2,1,0:T(8,128)(2,1)}), bf16[32,16,1536]{2,1,0:T(8,128)(2,1)S(1)}, u32[]{:S(2)}, u32[]{:S(2)}) async-start(bf16[32,16,1536]{2,1,0:T(8,128)(2,1)} %bitcast.18), calls=%async_computation.3 | async-start | bytes 3145728 | tf_op jit(solution)/shard_map/all_to_all | solution.py:299
  19.4 134.7 %all-gather.5.cloned.1.call-start = ((), (), s32[]{:S(2)}) async-start(), calls=%async_computation.8 | async-start | bytes 4915200 | tf_op jit(solution)/shard_map/all_gather | solution.py:320
  44.4 23.6 %collective-permute-start.1 = (bf16[160,1536]{1,0:T(8,128)(2,1)S(1)}, bf16[160,1536]{1,0:T(8,128)(2,1)S(1)}, u32[]{:S(2)}, u32[]{:S(2)}) collective-permute-start(bf16[160,1536]{1,0:T(8,128)(2,1)S(1)} %select_n.241), channel_id=1, source_target_pairs={{0,2},{1,3},{2,0},{3,1},{4,6},{5,7},{6,4},{7,5},{8,10},{9,11},{10,... | collective-permute-start | bytes 1474568 | tf_op jit(solution)/shard_map/ppermute | solution.py:260
  70.5 1.9 copy-start.1
  79.3 9.1 %copy-start.10 = (bf16[1,1536,384]{2,1,0:T(8,128)(2,1)S(1)}, bf16[1,1536,384]{2,1,0:T(8,128)(2,1)}, u32[]{:S(2)}) copy-start(bf16[1,1536,384]{2,1,0:T(8,128)(2,1)} %param.10) | copy-start | bytes 3538948
  79.3 58.2 %all-to-all-start = ((bf16[32,40,1536]{2,1,0:T(8,128)(2,1)}), bf16[32,40,1536]{2,1,0:T(8,128)(2,1)}, u32[]{:S(2)}, u32[]{:S(2)}) async-start(bf16[32,40,1536]{2,1,0:T(8,128)(2,1)} %bitcast.51), calls=%async_computation | async-start | bytes 7864320 | tf_op jit(solution)/shard_map/all_to_all | solution.py:331
  88.3 148.2 %reduce-scatter.3.cloned.1.call-start = ((), (), s32[]{:S(2)}) async-start(), calls=%async_computation.7 | async-start | bytes 4915200 | tf_op jit(solution)/shard_map/reduce_scatter | solution.py:352
  89.1 2.0 copy-start.7
  91.1 1.0 copy-start.8
  137.5 7.3 %copy-start.4 = (bf16[1,384,1536]{2,1,0:T(8,128)(2,1)S(1)}, bf16[1,384,1536]{2,1,0:T(8,128)(2,1)}, u32[]{:S(2)}) copy-start(bf16[1,384,1536]{2,1,0:T(8,128)(2,1)} %param.12) | copy-start | bytes 3538948
  151.3 1.0 copy-start.5
  154.1 4.9 %copy-start.2 = (s32[1280,1]{1,0:T(8,128)S(1)}, s32[1280,1]{1,0:T(8,128)}, u32[]{:S(2)}) copy-start(s32[1280,1]{1,0:T(8,128)} %get-tuple-element.37.place_ref) | copy-start | bytes 15364
  154.1 4.9 %copy-start = (f32[1280,768]{1,0:T(8,128)S(1)}, f32[1280,768]{1,0:T(8,128)}, u32[]{:S(2)}) copy-start(f32[1280,768]{1,0:T(8,128)} %get-tuple-element.22.pre_ref) | copy-start | bytes 11796484
  166.9 56.2 %all-to-all-start.3 = ((bf16[32,40,1536]{2,1,0:T(8,128)(2,1)}), bf16[32,40,1536]{2,1,0:T(8,128)(2,1)}, u32[]{:S(2)}, u32[]{:S(2)}) async-start(bf16[32,40,1536]{2,1,0:T(8,128)(2,1)} %bitcast.58), calls=%async_computation.4 | async-start | bytes 7864320 | tf_op jit(solution)/shard_map/all_to_all | solution.py:358
  173.9 112.7 %reduce-scatter.5.cloned.1.call-start = ((), (), s32[]{:S(2)}) async-start(), calls=%async_computation.9 | async-start | bytes 3538944 | tf_op jit(solution)/shard_map/reduce_scatter | solution.py:369
  231.4 6.3 %copy-start.11 = (f32[128,2]{0,1:T(2,128)S(1)}, f32[128,2]{0,1:T(2,128)}, u32[]{:S(2)}) copy-start(f32[128,2]{0,1:T(2,128)} %param.9) | copy-start | bytes 3076
  237.6 12.2 %collective-permute-start = (bf16[160,1536]{1,0:T(8,128)(2,1)S(1)}, bf16[160,1536]{1,0:T(8,128)(2,1)S(1)}, u32[]{:S(2)}, u32[]{:S(2)}) collective-permute-start(bf16[160,1536]{1,0:T(8,128)(2,1)S(1)} %slice.70), channel_id=1, source_target_pairs={{0,2},{1,3},{2,0},{3,1},{4,6},{5,7},{6,4},{7,5},{8,10},{9,11},{10,... | collective-permute-start | bytes 1474568 | tf_op jit(solution)/shard_map/ppermute | solution.py:260
  249.8 1.2 copy-start.3
  251.0 10.6 %copy-start.6 = (bf16[1280,384]{1,0:T(8,128)(2,1)S(1)}, bf16[1280,384]{1,0:T(8,128)(2,1)}, u32[]{:S(2)}) copy-start(bf16[1280,384]{1,0:T(8,128)(2,1)} %copy-done.5) | copy-start | bytes 2949124
  253.2 31.0 %all-to-all-start.1 = ((bf16[32,16,1536]{2,1,0:T(8,128)(2,1)}), bf16[32,16,1536]{2,1,0:T(8,128)(2,1)S(1)}, u32[]{:S(2)}, u32[]{:S(2)}) async-start(bf16[32,16,1536]{2,1,0:T(8,128)(2,1)} %bitcast.11), calls=%async_computation.2 | async-start | bytes 3145728 | tf_op jit(solution)/shard_map/all_to_all | solution.py:373
  261.6 5.1 %copy-start.12 = (bf16[1280,768]{1,0:T(8,128)(2,1)S(1)}, bf16[1280,768]{1,0:T(8,128)(2,1)}, u32[]{:S(2)}) copy-start(bf16[1280,768]{1,0:T(8,128)(2,1)} %get-tuple-element.24) | copy-start | bytes 5898244
  277.5 7.2 %copy-start.9 = (bf16[128,1536]{1,0:T(8,128)(2,1)S(1)}, bf16[128,1536]{1,0:T(8,128)(2,1)}, u32[]{:S(2)}) copy-start(bf16[128,1536]{1,0:T(8,128)(2,1)} %cot_ref.1) | copy-start | bytes 1179652
Sparse Core Ops, SparseCore 0:
  10.9 58.5 all-gather.2
  71.9 75.7 all-gather.4
  151.4 85.0 reduce-scatter.2
  239.5 42.6 reduce-scatter.4

commit v8 on v7

--- a/solution.py
+++ b/solution.py
@@ -23,7 +23,7 @@
     )
 
 
-ROWS = 256
+ROWS = 320
 
 
 def select_kernel(code_ref, x_ref, out_ref):

time: 294 us -> 294 us (level)
  transfers between devices with their start and end apart: 10 -> 10, of which waited for: 8 -> 8; matrix products, arithmetic and copies ran while one was open for 17% -> 17% of each run, Pallas kernels for 11% -> 10%
where the time goes in v8:
time: 294 us; the launch traced here: 293 us
  waiting for transfers between devices  156 us (53%)
  starting transfers between devices  35.5 us (12%)
  Pallas kernels  32.5 us (11%)
  matrix products  30.7 us (10%)
  between operations  14.1 us (5%)
  local copies, waits for them, and re-layouts  13.4 us (5%)
  other arithmetic  10.9 us (4%)
    all_to_all x1, waiting for transfers between devices, on_device(): lax.all_to_all(back_rows.reshape(columns, planes * capacity, width), 'exp...  48.8 us
    all_to_all x1, waiting for transfers between devices, on_device(): lax.all_to_all(send_tokens.reshape(columns, planes * capacity, width), 'e...  36.9 us
    ppermute x2, waiting for transfers between devices, pair_swap(): lax.ppermute(x, 'expert', [(e, e + 2 - pair_of(e) * 4) for e in range(exp...  33.6 us
    all_to_all x1, waiting for transfers between devices, on_device(): lax.all_to_all(send_cot.reshape(columns, 2 * PADDED, width), 'expert', sp...  22.6 us
    dot_general x5, matrix products, dot_first(): lax.dot_general(left, right, (((0,), (0,)), ((), ())), preferred_element_...  17.6 us
    all_to_all x1, starting transfers between devices, on_device(): lax.all_to_all(send_tokens.reshape(columns, planes * capacity, width), 'e...  9.01 us
    all_to_all x1, starting transfers between devices, on_device(): lax.all_to_all(spread(expert_out, pair_swap(expert_out[half_rows:]), colu...  8.73 us
    all_to_all x1, starting transfers between devices, on_device(): lax.all_to_all(send_cot.reshape(columns, 2 * PADDED, width), 'expert', sp...  8.6 us
  transfers between devices with their start and end apart: 10, of which 8 were waited for; matrix products, arithmetic and copies ran while one was open for 17% of the time, Pallas kernels for 10%

profile of v8, /device:TPU:1, one launch (start us, length us, event | category | flops | bytes accessed | tf_op | source)
XLA Modules:
  0.0 293.1 jit_solution(2977875457625966205)
XLA Ops:
  7.2 3.6 %prepare_rows.1 = (bf16[136,1536]{1,0:T(8,128)(2,1)}, bf16[512,1536]{1,0:T(8,128)(2,1)}, s32[4,128]{1,0:T(4,128)S(1)}) custom-call(bf16[128,1536]{1,0:T(8,128)(2,1)} %tokens_ref.1, s32[2,128]{1,0:T(2,128)} %bitcast.64, f32[2,128]{1,0:T(2,128)} %bitcast.59, bf16[128,1536]{1,0:T(8,128)(2,1)} %cot_ref.1), custom_call_target="tpu_custom_call" | custom-call | tf_op jit(solution)/shard_map/prepare_rows/pallas_call | solution.py:222
  10.8 8.6 %all-to-all-start.2 = ((bf16[32,16,1536]{2,1,0:T(8,128)(2,1)}), bf16[32,16,1536]{2,1,0:T(8,128)(2,1)S(1)}, u32[]{:S(2)}, u32[]{:S(2)}) async-start(bf16[32,16,1536]{2,1,0:T(8,128)(2,1)} %bitcast.18), calls=%async_computation.3 | async-start | bytes 3145728 | tf_op jit(solution)/shard_map/all_to_all | solution.py:299
  19.5 22.6 %all-to-all-done.2 = bf16[32,16,1536]{2,1,0:T(8,128)(2,1)S(1)} async-done(((bf16[32,16,1536]{2,1,0:T(8,128)(2,1)}), bf16[32,16,1536]{2,1,0:T(8,128)(2,1)S(1)}, u32[]{:S(2)}, u32[]{:S(2)}) %all-to-all-start.2) | async-done | bytes 1572896 | tf_op jit(solution)/shard_map/all_to_all | solution.py:299
  43.1 1.3 select_n.241
  44.4 1.7 collective-permute-start.1
  46.4 21.6 %collective-permute-done.1 = bf16[160,1536]{1,0:T(8,128)(2,1)S(1)} collective-permute-done((bf16[160,1536]{1,0:T(8,128)(2,1)S(1)}, bf16[160,1536]{1,0:T(8,128)(2,1)S(1)}, u32[]{:S(2)}, u32[]{:S(2)}) %collective-permute-start.1) | collective-permute-done | bytes 491552 | tf_op jit(solution)/shard_map/ppermute | solution.py:260
  70.5 1.9 copy-done.1
  72.4 6.8 %select_rows.1 = bf16[1280,1536]{1,0:T(8,128)(2,1)} custom-call(s32[2,1088]{1,0:T(2,128)S(1)} %reshape.391.code_ref, bf16[1088,1536]{1,0:T(8,128)(2,1)S(1)} %copy-done.1), custom_call_target="tpu_custom_call" | custom-call | tf_op jit(solution)/shard_map/select_rows/pallas_call | solution.py:38
  79.2 9.0 %all-to-all-start = ((bf16[32,40,1536]{2,1,0:T(8,128)(2,1)}), bf16[32,40,1536]{2,1,0:T(8,128)(2,1)}, u32[]{:S(2)}, u32[]{:S(2)}) async-start(bf16[32,40,1536]{2,1,0:T(8,128)(2,1)} %bitcast.51), calls=%async_computation | async-start | bytes 7864320 | tf_op jit(solution)/shard_map/all_to_all | solution.py:331
  89.0 2.0 copy.19
  92.0 1.6 pad_maximum_fusion
  93.6 2.8 copy.20.w_ref
  96.4 4.1 %fusion.19 = (s32[1280,1]{1,0:T(8,128)}, s32[1280,1]{1,0:T(8,128)S(1)}) fusion(s32[]{:T(128)S(6)} %select_n.219, s32[]{:T(128)S(6)} %sub.62), kind=kLoop, calls=%fused_computation.53 | loop fusion | flops 126720 | bytes 10248 | tf_op jit(solution)/shard_map/add | solution.py:342
  100.5 36.9 %all-to-all-done = bf16[32,40,1536]{2,1,0:T(8,128)(2,1)} async-done(((bf16[32,40,1536]{2,1,0:T(8,128)(2,1)}), bf16[32,40,1536]{2,1,0:T(8,128)(2,1)}, u32[]{:S(2)}, u32[]{:S(2)}) %all-to-all-start) | async-done | bytes 3932192 | tf_op jit(solution)/shard_map/all_to_all | solution.py:331
  137.4 6.7 %forward_rows.1 = (f32[1280,768]{1,0:T(8,128)}, bf16[1280,384]{1,0:T(8,128)(2,1)S(1)}) custom-call(bf16[1280,1536]{1,0:T(8,128)(2,1)} %bitcast.7.x_ref, bf16[1536,768]{1,0:T(8,128)(2,1)S(1)} %copy.20.w_ref), custom_call_target="tpu_custom_call" | custom-call | tf_op jit(solution)/shard_map/forward_rows/pallas_call | solution.py:63
  144.1 5.9 %outward_rows.1 = (bf16[1280,384]{1,0:T(8,128)(2,1)S(1)}, bf16[1280,1536]{1,0:T(8,128)(2,1)}) custom-call(s32[1280,1]{1,0:T(8,128)S(1)} %get-tuple-element.38.place_ref, bf16[1280,384]{1,0:T(8,128)(2,1)S(1)} %get-tuple-element.18.hidden_ref, bf16[384,1536]{1,0:T(8,128)(2,1)S(1)} %bitcast.50), custom_call_target="tpu_custom_call" | custom-call | tf_op jit(solution)/shard_map/outward_rows/pallas_call | solution.py:135
  151.0 1.8 pad_maximum_fusion.1.w_ref
  152.8 4.8 %convolution_convert_fusion.3.d_ref = bf16[1280,384]{1,0:T(8,128)(2,1)S(1)} fusion(bf16[1280,1536]{1,0:T(8,128)(2,1)} %all-gather.5.cloned.1.call-done, bf16[1,384,1536]{2,1,0:T(8,128)(2,1)} %param.12), kind=kOutput, calls=%fused_computation.8 | convolution fusion | flops 1510440960 | bytes 6094848 | tf_op jit(solution)/shard_map/dot_general | solution.py:15
  157.7 7.3 %backward_rows.1 = (bf16[1280,768]{1,0:T(8,128)(2,1)}, bf16[1280,1536]{1,0:T(8,128)(2,1)}) custom-call(s32[1280,1]{1,0:T(8,128)S(1)} %copy-done.2, bf16[1280,384]{1,0:T(8,128)(2,1)S(1)} %convolution_convert_fusion.3.d_ref, f32[1280,768]{1,0:T(8,128)S(1)} %copy-done, bf16[768,1536]{1,0:T(8,128)(2,1)S(1)} %pad_maximum_fusion.1.w_ref), custom_call_target="tpu_custom_call" | custom-call | tf_op jit(solution)/shard_map/backward_rows/pallas_call | solution.py:101
  165.0 7.0 %all-to-all-start.3 = ((bf16[32,40,1536]{2,1,0:T(8,128)(2,1)}), bf16[32,40,1536]{2,1,0:T(8,128)(2,1)}, u32[]{:S(2)}, u32[]{:S(2)}) async-start(bf16[32,40,1536]{2,1,0:T(8,128)(2,1)} %bitcast.58), calls=%async_computation.4 | async-start | bytes 7864320 | tf_op jit(solution)/shard_map/all_to_all | solution.py:358
  172.3 48.8 %all-to-all-done.3 = bf16[32,40,1536]{2,1,0:T(8,128)(2,1)} async-done(((bf16[32,40,1536]{2,1,0:T(8,128)(2,1)}), bf16[32,40,1536]{2,1,0:T(8,128)(2,1)}, u32[]{:S(2)}, u32[]{:S(2)}) %all-to-all-start.3) | async-done | bytes 3932192 | tf_op jit(solution)/shard_map/all_to_all | solution.py:358
  221.1 8.2 %fusion.3 = bf16[1024,1536]{1,0:T(8,128)(2,1)} fusion(bf16[1280,1536]{1,0:T(8,128)(2,1)} %bitcast.22, s32[1024]{0:T(1024)S(1)} %bitcast.61, s32[1024]{0:T(1024)S(1)} %bitcast.60), kind=kOutput, calls=%fused_computation.4 | convolution fusion | flops 4032036864 | bytes 7086080 | tf_op jit(solution)/shard_map/dot_general | solution.py:11
  229.4 6.8 %reduce-scatter.3.cloned.1.call-done.mine_ref = bf16[320,1536]{1,0:T(8,128)(2,1)} async-done(((bf16[1280,1536]{1,0:T(8,128)(2,1)}), bf16[320,1536]{1,0:T(8,128)(2,1)}) %reduce-scatter.3.cloned.1.call-update) | async-done | bytes 983056 | tf_op jit(solution)/shard_map/reduce_scatter | solution.py:352
  237.4 12.0 %collective-permute-done.other_ref = bf16[160,1536]{1,0:T(8,128)(2,1)S(1)} collective-permute-done((bf16[160,1536]{1,0:T(8,128)(2,1)S(1)}, bf16[160,1536]{1,0:T(8,128)(2,1)S(1)}, u32[]{:S(2)}, u32[]{:S(2)}) %collective-permute-start) | collective-permute-done | bytes 491552 | tf_op jit(solution)/shard_map/ppermute | solution.py:260
  249.4 1.2 copy-done.3
  250.6 2.2 spread_rows.1
  252.8 8.7 %all-to-all-start.1 = ((bf16[32,16,1536]{2,1,0:T(8,128)(2,1)}), bf16[32,16,1536]{2,1,0:T(8,128)(2,1)S(1)}, u32[]{:S(2)}, u32[]{:S(2)}) async-start(bf16[32,16,1536]{2,1,0:T(8,128)(2,1)} %bitcast.11), calls=%async_computation.2 | async-start | bytes 3145728 | tf_op jit(solution)/shard_map/all_to_all | solution.py:373
  261.6 5.0 %fusion.10 = bf16[1,384,1536]{2,1,0:T(8,128)(2,1)} fusion(bf16[1280,384]{1,0:T(8,128)(2,1)S(1)} %copy-done.6, bf16[1280,1536]{1,0:T(8,128)(2,1)} %all-gather.5.cloned.1.call-done), kind=kOutput, calls=%fused_computation.13 | convolution fusion | flops 1510539264 | bytes 6094848 | tf_op jit(solution)/shard_map/dot_general | solution.py:21
  266.7 5.4 %fusion.9 = bf16[1,1536,384]{2,1,0:T(8,128)(2,1)} fusion(bf16[1280,1536]{1,0:T(8,128)(2,1)} %bitcast.7.x_ref, bf16[1280,768]{1,0:T(8,128)(2,1)S(1)} %copy-done.12), kind=kOutput, calls=%fused_computation.12 | convolution fusion | flops 1510539264 | bytes 6094848 | tf_op jit(solution)/shard_map/dot_general | solution.py:21
  272.1 5.4 %fusion.8 = bf16[1,1536,384]{2,1,0:T(8,128)(2,1)} fusion(bf16[1280,1536]{1,0:T(8,128)(2,1)} %bitcast.7.x_ref, bf16[1280,768]{1,0:T(8,128)(2,1)S(1)} %copy-done.12), kind=kOutput, calls=%fused_computation.11 | convolution fusion | flops 1510539264 | bytes 6094848 | tf_op jit(solution)/shard_map/dot_general | solution.py:21
  277.5 6.8 %all-to-all-done.1 = bf16[32,16,1536]{2,1,0:T(8,128)(2,1)S(1)} async-done(((bf16[32,16,1536]{2,1,0:T(8,128)(2,1)}), bf16[32,16,1536]{2,1,0:T(8,128)(2,1)S(1)}, u32[]{:S(2)}, u32[]{:S(2)}) %all-to-all-start.1) | async-done | bytes 1572896 | tf_op jit(solution)/shard_map/all_to_all | solution.py:373
  284.7 1.4 fusion.13
  (54 shorter events, 9.0 us)
Async XLA Ops:
  7.2 62.4 %all-gather.3.cloned.1.call-start = ((), (), s32[]{:S(2)}) async-start(), calls=%async_computation.6 | async-start | bytes 3760128 | tf_op jit(solution)/shard_map/all_gather | solution.py:317
  10.8 31.3 %all-to-all-start.2 = ((bf16[32,16,1536]{2,1,0:T(8,128)(2,1)}), bf16[32,16,1536]{2,1,0:T(8,128)(2,1)S(1)}, u32[]{:S(2)}, u32[]{:S(2)}) async-start(bf16[32,16,1536]{2,1,0:T(8,128)(2,1)} %bitcast.18), calls=%async_computation.3 | async-start | bytes 3145728 | tf_op jit(solution)/shard_map/all_to_all | solution.py:299
  19.4 133.4 %all-gather.5.cloned.1.call-start = ((), (), s32[]{:S(2)}) async-start(), calls=%async_computation.8 | async-start | bytes 4915200 | tf_op jit(solution)/shard_map/all_gather | solution.py:320
  44.4 23.6 %collective-permute-start.1 = (bf16[160,1536]{1,0:T(8,128)(2,1)S(1)}, bf16[160,1536]{1,0:T(8,128)(2,1)S(1)}, u32[]{:S(2)}, u32[]{:S(2)}) collective-permute-start(bf16[160,1536]{1,0:T(8,128)(2,1)S(1)} %select_n.241), channel_id=1, source_target_pairs={{0,2},{1,3},{2,0},{3,1},{4,6},{5,7},{6,4},{7,5},{8,10},{9,11},{10,... | collective-permute-start | bytes 1474568 | tf_op jit(solution)/shard_map/ppermute | solution.py:260
  70.5 1.9 copy-start.1
  79.2 9.1 %copy-start.10 = (bf16[1,1536,384]{2,1,0:T(8,128)(2,1)S(1)}, bf16[1,1536,384]{2,1,0:T(8,128)(2,1)}, u32[]{:S(2)}) copy-start(bf16[1,1536,384]{2,1,0:T(8,128)(2,1)} %param.10) | copy-start | bytes 3538948
  79.2 58.2 %all-to-all-start = ((bf16[32,40,1536]{2,1,0:T(8,128)(2,1)}), bf16[32,40,1536]{2,1,0:T(8,128)(2,1)}, u32[]{:S(2)}, u32[]{:S(2)}) async-start(bf16[32,40,1536]{2,1,0:T(8,128)(2,1)} %bitcast.51), calls=%async_computation | async-start | bytes 7864320 | tf_op jit(solution)/shard_map/all_to_all | solution.py:331
  88.2 148.0 %reduce-scatter.3.cloned.1.call-start = ((), (), s32[]{:S(2)}) async-start(), calls=%async_computation.7 | async-start | bytes 4915200 | tf_op jit(solution)/shard_map/reduce_scatter | solution.py:352
  88.9 2.0 copy-start.7
  91.0 1.0 copy-start.8
  137.4 6.7 %copy-start.4 = (bf16[1,384,1536]{2,1,0:T(8,128)(2,1)S(1)}, bf16[1,384,1536]{2,1,0:T(8,128)(2,1)}, u32[]{:S(2)}) copy-start(bf16[1,384,1536]{2,1,0:T(8,128)(2,1)} %param.12) | copy-start | bytes 3538948
  150.0 1.0 copy-start.5
  152.8 4.9 %copy-start.2 = (s32[1280,1]{1,0:T(8,128)S(1)}, s32[1280,1]{1,0:T(8,128)}, u32[]{:S(2)}) copy-start(s32[1280,1]{1,0:T(8,128)} %get-tuple-element.37.place_ref) | copy-start | bytes 15364
  152.8 4.9 %copy-start = (f32[1280,768]{1,0:T(8,128)S(1)}, f32[1280,768]{1,0:T(8,128)}, u32[]{:S(2)}) copy-start(f32[1280,768]{1,0:T(8,128)} %get-tuple-element.22.pre_ref) | copy-start | bytes 11796484
  165.0 56.1 %all-to-all-start.3 = ((bf16[32,40,1536]{2,1,0:T(8,128)(2,1)}), bf16[32,40,1536]{2,1,0:T(8,128)(2,1)}, u32[]{:S(2)}, u32[]{:S(2)}) async-start(bf16[32,40,1536]{2,1,0:T(8,128)(2,1)} %bitcast.58), calls=%async_computation.4 | async-start | bytes 7864320 | tf_op jit(solution)/shard_map/all_to_all | solution.py:358
  172.0 114.6 %reduce-scatter.5.cloned.1.call-start = ((), (), s32[]{:S(2)}) async-start(), calls=%async_computation.9 | async-start | bytes 3538944 | tf_op jit(solution)/shard_map/reduce_scatter | solution.py:369
  229.4 8.0 %copy-start.11 = (f32[128,2]{0,1:T(2,128)S(1)}, f32[128,2]{0,1:T(2,128)}, u32[]{:S(2)}) copy-start(f32[128,2]{0,1:T(2,128)} %param.9) | copy-start | bytes 3076
  237.3 12.1 %collective-permute-start = (bf16[160,1536]{1,0:T(8,128)(2,1)S(1)}, bf16[160,1536]{1,0:T(8,128)(2,1)S(1)}, u32[]{:S(2)}, u32[]{:S(2)}) collective-permute-start(bf16[160,1536]{1,0:T(8,128)(2,1)S(1)} %slice.70), channel_id=1, source_target_pairs={{0,2},{1,3},{2,0},{3,1},{4,6},{5,7},{6,4},{7,5},{8,10},{9,11},{10,... | collective-permute-start | bytes 1474568 | tf_op jit(solution)/shard_map/ppermute | solution.py:260
  249.4 1.2 copy-start.3
  250.6 10.9 %copy-start.6 = (bf16[1280,384]{1,0:T(8,128)(2,1)S(1)}, bf16[1280,384]{1,0:T(8,128)(2,1)}, u32[]{:S(2)}) copy-start(bf16[1280,384]{1,0:T(8,128)(2,1)} %copy-done.5) | copy-start | bytes 2949124
  252.8 31.4 %all-to-all-start.1 = ((bf16[32,16,1536]{2,1,0:T(8,128)(2,1)}), bf16[32,16,1536]{2,1,0:T(8,128)(2,1)S(1)}, u32[]{:S(2)}, u32[]{:S(2)}) async-start(bf16[32,16,1536]{2,1,0:T(8,128)(2,1)} %bitcast.11), calls=%async_computation.2 | async-start | bytes 3145728 | tf_op jit(solution)/shard_map/all_to_all | solution.py:373
  261.6 5.1 %copy-start.12 = (bf16[1280,768]{1,0:T(8,128)(2,1)S(1)}, bf16[1280,768]{1,0:T(8,128)(2,1)}, u32[]{:S(2)}) copy-start(bf16[1280,768]{1,0:T(8,128)(2,1)} %get-tuple-element.24) | copy-start | bytes 5898244
  277.5 7.2 %copy-start.9 = (bf16[128,1536]{1,0:T(8,128)(2,1)S(1)}, bf16[128,1536]{1,0:T(8,128)(2,1)}, u32[]{:S(2)}) copy-start(bf16[128,1536]{1,0:T(8,128)(2,1)} %cot_ref.1) | copy-start | bytes 1179652
Sparse Core Ops, SparseCore 0:
  10.9 58.5 all-gather.2
  71.9 78.9 all-gather.4
  153.5 82.6 reduce-scatter.2
  239.2 42.8 reduce-scatter.4
